TPU v7x, 32 devices: a whole 2x2x4 slice. The times are simulated.
32 devices in a mesh: groups: 2 (over x), cluster: 16 (over z, y, core).
Axes of the slice: x: 2, y: 2, z: 4, core: 2. Of those that a mesh axis runs over, the one named last changes fastest.
Arguments:
- hidden_states: bfloat16 [128, 128, 1024], P(('groups', 'cluster')), parts along dimension 0, may hold values from -6 to 6
- token_ids: int32 [128, 128], P(('groups', 'cluster')), parts along dimension 0, may hold values from 0 to 30521, as said below
- up_weight: bfloat16 [1024, 2048], replicated, may hold values from -0.1875 to 0.1875
- down_weight: bfloat16 [2048, 1024], replicated, may hold values from -0.125 to 0.125
- centroids: bfloat16 [65536, 1024], P('cluster'), may hold values from -0.1875 to 0.1875
- positives: int32 [128, 16], P('groups'), parts along dimension 0, may hold values from 0 to 65535
- counts: int32 [128], P('groups'), parts along dimension 0, may hold values from 1 to 16
Outputs:
- query_grad: float32 [128, 1024], P(('groups', 'cluster')), parts along dimension 0
- centroid_grad: float32 [131072, 1024], P(('groups', 'cluster')), parts along dimension 0
There are 2 independent parts, one for each index of `groups`. A program takes and returns all parts, laid end to end along the dimension named above; an argument that names none is the same for every part. Nothing has to cross between parts.
Inputs may be any that keep to these rules, and one draw needn't show every extreme that they name: `token_ids`: in each query's row the nonzero ids come first and zeros fill the rest; every query has at least 16 nonzero ids.
All inputs are finite; a program needn't handle non-finite values.
Results may differ from a plain program's by a relative error of at most 0.003.
Values may be sent and summed in bfloat16 or wider, within the bound.
No kernel may reach another device: no remote copies, remote signals or barrier semaphores. Data moves between devices by JAX's collectives and lax.ppermute only.
A program may use at most 128 MiB of HBM per device.

v0:
```python
import jax
import jax.numpy as jnp
from jax import lax
from jax.sharding import PartitionSpec as P

MB = 32


def layer_norm(values):
    centered = values - jnp.mean(values, axis=-1, keepdims=True)
    spread = jnp.mean(centered * centered, axis=-1, keepdims=True)
    return centered * lax.rsqrt(spread + 1e-05)


def encode(states, ids, up_weight, down_weight):
    count, length, width = states.shape
    flat = states.reshape(count * length, width)
    up_part = jnp.dot(flat, up_weight, preferred_element_type=jnp.float32)
    act = jax.nn.gelu(up_part).astype(jnp.bfloat16)
    ffn = jnp.dot(act, down_weight, preferred_element_type=jnp.float32)
    normed = layer_norm(flat.astype(jnp.float32) + ffn).reshape(count, length, width)
    keep = (ids != 0).astype(jnp.float32)
    pooled = jnp.sum(normed * keep[:, :, None], axis=1) / jnp.sum(keep, axis=1)[:, None]
    return layer_norm(pooled).astype(jnp.bfloat16)


def logit_grads(gathered, centroids, cluster_ids, pos_rows, cnt_rows):
    logits = jnp.dot(gathered, centroids.T, preferred_element_type=jnp.float32)
    slots = jnp.arange(pos_rows.shape[1], dtype=jnp.int32)
    valid = slots[None, :] < cnt_rows[:, None]
    hits = (pos_rows[:, :, None] == cluster_ids[None, None, :]) & valid[:, :, None]
    target = jnp.any(hits, axis=1).astype(jnp.float32)
    return ((jax.nn.sigmoid(logits) - target) / MB).astype(jnp.bfloat16)


def centroid_term(dlogit, gathered):
    return lax.dot_general(
        dlogit, gathered, (((0,), (0,)), ((), ())), preferred_element_type=jnp.float32
    )


def shards(hidden_states, token_ids, up_weight, down_weight, centroids, positives, counts):
    c_dev = centroids.shape[0]
    first = lax.axis_index("cluster") * c_dev
    cluster_ids = first + jnp.arange(c_dev, dtype=jnp.int32)
    queries = encode(hidden_states, token_ids, up_weight, down_weight)
    gathered = lax.all_gather(queries, "cluster", axis=0, tiled=True)
    dlogit = logit_grads(gathered, centroids, cluster_ids, positives, counts)
    query_grad = lax.psum_scatter(
        jnp.dot(dlogit, centroids, preferred_element_type=jnp.float32),
        "cluster",
        scatter_dimension=0,
        tiled=True,
    )
    centroid_grad = centroid_term(dlogit, gathered)
    return (query_grad, centroid_grad)


def solution(mesh):
    placed = (
        P(("groups", "cluster"), None, None),
        P(("groups", "cluster"), None),
        P(),
        P(),
        P("cluster", None),
        P("groups", None),
        P("groups"),
    )
    return jax.shard_map(
        shards,
        mesh=mesh,
        in_specs=placed,
        out_specs=(P(("groups", "cluster"), None), P(("groups", "cluster"), None)),
        check_vma=False,
    )
```

profile of v0, /device:TPU:0, one launch (start us, length us, event | category | flops | bytes accessed | tf_op | source)
XLA Modules:
  0.0 157.2 jit_solution(6863686236339006003)
XLA Ops:
  7.2 0.0 all-reduce.3.cloned.1.call-start
  7.2 0.8 fusion.27
  8.0 0.7 compare_convert_fusion
  8.7 0.7 iota_compare_fusion
  9.4 0.8 copy.11
  10.2 8.6 %fusion.29 = (f32[512]{0:T(512)S(1)}, f32[512,1024]{1,0:T(8,128)S(1)}) fusion(bf16[2048,1024]{1,0:T(8,128)(2,1)} %param.10, bf16[512,1024]{1,0:T(8,128)(2,1)} %bitcast.15, bf16[1024,2048]{1,0:T(8,128)(2,1)} %param.9), kind=kOutput, calls=%fused_computation.44 | convolution fusion | flops 4305976832 | bytes 11536384 | tf_op jit(solution)/shard_map/dot_general | solution.py:20
  18.9 0.3 multiply_reduce_fusion.1
  19.2 0.4 multiply_reduce_fusion
  19.6 0.2 fusion.28
  19.8 0.2 multiply_reduce_fusion.2
  20.0 0.1 fusion.22
  20.1 23.6 %all-gather = bf16[16,4,1024]{2,1,0:T(4,128)(2,1)S(1)} all-gather(bf16[1,4,1024]{2,1,0:T(4,128)(2,1)S(1)} %fusion.22), channel_id=1, replica_groups=mesh['groups'=2,'cluster'=16] {'cluster'}, dimensions={0}, use_global_device_ids=true | all-gather | bytes 139264 | tf_op jit(solution)/shard_map/all_gather | solution.py:47
  43.8 7.2 %and_reduce_fusion = pred[64,4096]{1,0:T(8,128)(4,1)S(1)} fusion(s32[4096]{0:T(1024)S(1)} %iota_add_fusion, s32[64,16]{1,0:T(8,128)S(1)} %copy.11, pred[64,16]{1,0:T(8,128)(4,1)S(1)} %iota_compare_fusion), kind=kLoop, calls=%fused_computation | loop fusion | flops 12320768 | bytes 283648 | tf_op jit(solution)/shard_map/reduce_or | solution.py:32
  51.0 6.1 %fusion.5 = bf16[64,4096]{1,0:T(8,128)(2,1)S(1)} fusion(bf16[64,1024]{1,0:T(8,128)(2,1)S(1)} %reshape.65, bf16[4096,1024]{1,0:T(8,128)(2,1)} %param.11, pred[64,4096]{1,0:T(8,128)(4,1)S(1)} %and_reduce_fusion), kind=kOutput, calls=%fused_computation.8 | convolution fusion | flops 538705920 | bytes 9306112 | tf_op jit(solution)/shard_map/dot_general | solution.py:28
  57.1 5.7 %fusion.32 = f32[64,1024]{1,0:T(8,128)} fusion(bf16[64,4096]{1,0:T(8,128)(2,1)S(1)} %fusion.5, bf16[4096,1024]{1,0:T(8,128)(2,1)} %param.11), kind=kOutput, calls=%fused_computation.46 | convolution fusion | flops 536870912 | bytes 9175040 | tf_op jit(solution)/shard_map/dot_general | solution.py:50
  62.7 0.0 all-reduce.3.cloned.1.call-update
  62.8 0.0 copy-start
  62.8 8.5 %fusion.33 = f32[4096,1024]{1,0:T(8,128)} fusion(bf16[64,4096]{1,0:T(8,128)(2,1)S(1)} %fusion.5, bf16[64,1024]{1,0:T(8,128)(2,1)S(1)} %reshape.65), kind=kOutput, calls=%fused_computation.47 | convolution fusion | flops 536870912 | bytes 17432576 | tf_op jit(solution)/shard_map/dot_general | solution.py:37
  71.3 0.0 copy-done
  71.3 0.6 dynamic-slice
  72.5 76.5 %all-reduce.3.cloned.1.call-done = f32[64,1024]{1,0:T(8,128)} async-done(((f32[64,1024]{1,0:T(8,128)}), f32[64,1024]{1,0:T(8,128)}) %all-reduce.3.cloned.1.call-update) | async-done | bytes 262160
  149.0 1.4 constant_dynamic-slice_fusion
  (6 shorter events, 0.1 us)
Async XLA Ops:
  7.2 141.9 %all-reduce.3.cloned.1.call-start = ((), (), s32[]{:S(2)}) async-start(), calls=%async_computation | async-start | bytes 524288
  62.8 8.5 %copy-start = (u32[32]{0:T(128)S(1)}, u32[32]{0:T(128)}, u32[]{:S(2)}) copy-start(u32[32]{0:T(128)} %constant.38) | copy-start | bytes 388
Sparse Core Ops, SparseCore 0:
  62.9 86.0 all-reduce.2
where the time goes:
time: 158 us; the launch traced here: 157 us
  waiting for transfers between devices  76.5 us (48%)
  matrix products  28.9 us (18%)
  blocking collectives  23.6 us (15%)
  between operations  14.7 us (9%)
  other arithmetic  10.7 us (7%)
  local copies, waits for them, and re-layouts  2.77 us (2%)
    unnamed x2, waiting for transfers between devices  76.5 us
    all_gather x1, blocking collectives, shards(): gathered = lax.all_gather(queries, 'cluster', axis=0, tiled=True)  23.6 us
    dot_general x1, matrix products, encode(): ffn = jnp.dot(act, down_weight, preferred_element_type=jnp.float32)  8.63 us
    dot_general x1, matrix products, centroid_term(): lax.dot_general(dlogit, gathered, (((0,), (0,)), ((), ())), preferred_ele...  8.53 us
    reduce_or x1, other arithmetic, logit_grads(): target = jnp.any(hits, axis=1).astype(jnp.float32)  7.2 us
    dot_general x1, matrix products, logit_grads(): logits = jnp.dot(gathered, centroids.T, preferred_element_type=jnp.float32)  6.07 us
    dot_general x1, matrix products, shards(): jnp.dot(dlogit, centroids, preferred_element_type=jnp.float32)  5.67 us
  transfers between devices with their start and end apart: 1, of which 1 were waited for; matrix products, arithmetic and copies ran while one was open for 6% of the time, Pallas kernels for 0%

commit v1 on v0

v1 whole, which is shorter than its diff:
```python
import functools

import jax
import jax.numpy as jnp
from jax import lax
from jax.experimental import pallas as pl
from jax.experimental.pallas import tpu as pltpu
from jax.sharding import PartitionSpec as P

MB = 32
EPS = 1e-05
F32 = jnp.float32
BF16 = jnp.bfloat16
HBM = pltpu.MemorySpace.HBM
NN = (((1,), (0,)), ((), ()))
NT = (((1,), (1,)), ((), ()))
TN = (((0,), (0,)), ((), ()))


def dot(a, b, dims):
    return lax.dot_general(a, b, dims, preferred_element_type=F32)


def whole(shape):
    return pl.BlockSpec(shape, lambda: (0,) * len(shape))


def normed(values):
    centered = values - jnp.mean(values, axis=-1, keepdims=True)
    spread = jnp.mean(centered * centered, axis=-1, keepdims=True)
    return centered, lax.rsqrt(spread + EPS)


def encode_kernel(up_step, down_step, x_hbm, ids_ref, up_hbm, down_hbm, q_ref, x_ref, up_ref, down_ref, act_ref, sum_ref, sems):
    count, length, width = x_ref.shape
    hidden = up_ref.shape[1]
    x_copy = pltpu.make_async_copy(x_hbm, x_ref, sems.at[0, 0])
    x_copy.start()
    ups, downs = [], []
    for k in range(hidden // up_step):
        cut = (slice(None), pl.ds(k * up_step, up_step))
        ups.append(pltpu.make_async_copy(up_hbm.at[cut], up_ref.at[cut], sems.at[1, k]))
    for k in range(width // down_step):
        cut = (slice(None), pl.ds(k * down_step, down_step))
        downs.append(pltpu.make_async_copy(down_hbm.at[cut], down_ref.at[cut], sems.at[2, k]))
    for copy in ups + downs:
        copy.start()
    x_copy.wait()
    x = x_ref[...].reshape(count * length, width)
    for k, copy in enumerate(ups):
        copy.wait()
        cut = slice(k * up_step, (k + 1) * up_step)
        act_ref[:, cut] = jax.nn.gelu(dot(x, up_ref[:, cut], NN)).astype(BF16)
    for k, copy in enumerate(downs):
        copy.wait()
        cut = slice(k * down_step, (k + 1) * down_step)
        sum_ref[:, cut] = x[:, cut].astype(F32) + dot(act_ref[...], down_ref[:, cut], NN)
    kept = jnp.sum((ids_ref[...] != 0).astype(F32), axis=1, keepdims=True)
    place = lax.broadcasted_iota(jnp.int32, (length, 1), 0).astype(F32)
    rows = []
    for k in range(count):
        centered, scale = normed(sum_ref[k * length : (k + 1) * length, :])
        own = kept[k : k + 1, :]
        scale = jnp.where(place < own, scale, 0.0)
        rows.append(jnp.sum(centered * scale, axis=0, keepdims=True) / own)
    centered, scale = normed(jnp.concatenate(rows, axis=0))
    q_ref[0] = (centered * scale).astype(BF16)


def encode(states, ids, up_weight, down_weight):
    count, length, width = states.shape
    hidden = up_weight.shape[1]
    up_step, down_step = min(512, hidden), min(256, width)
    steps = max(hidden // up_step, width // down_step)
    tokens = count * length
    return pl.pallas_call(
        functools.partial(encode_kernel, up_step, down_step),
        out_shape=jax.ShapeDtypeStruct((1, count, width), BF16),
        in_specs=[
            pl.BlockSpec(memory_space=HBM),
            whole(ids.shape),
            pl.BlockSpec(memory_space=HBM),
            pl.BlockSpec(memory_space=HBM),
        ],
        out_specs=whole((1, count, width)),
        scratch_shapes=[
            pltpu.VMEM(states.shape, BF16),
            pltpu.VMEM(up_weight.shape, BF16),
            pltpu.VMEM(down_weight.shape, BF16),
            pltpu.VMEM((tokens, hidden), BF16),
            pltpu.VMEM((tokens, width), F32),
            pltpu.SemaphoreType.DMA((3, steps)),
        ],
        compiler_params=pltpu.CompilerParams(vmem_limit_bytes=60 << 20),
        cost_estimate=pl.CostEstimate(
            flops=4 * tokens * hidden * width,
            transcendentals=tokens * hidden,
            bytes_accessed=4 * hidden * width + 2 * tokens * width,
        ),
        name="encode",
    )(states, ids, up_weight, down_weight)


def target_kernel(order, me_ref, pos_ref, cnt_ref, out_ref, rel_ref):
    slots, queries = pos_ref.shape
    c_dev = out_ref.shape[1]
    per = rel_ref.shape[1]
    me = me_ref[0]
    slot = lax.broadcasted_iota(jnp.int32, (slots, queries), 0)
    rel = jnp.where(slot < cnt_ref[...], pos_ref[...] - me * c_dev, -1).T
    for k in range(queries // per):
        rel_ref[k] = rel[k * per : (k + 1) * per, :]
    rel = jnp.concatenate([rel_ref[lax.bitwise_xor(me, k)] for k in order], axis=0)
    step = min(512, c_dev)
    for k in range(c_dev // step):
        ids = lax.broadcasted_iota(jnp.int32, (queries, step), 1) + k * step
        hit = ids == rel[:, 0:1]
        for s in range(1, slots):
            hit = jnp.logical_or(hit, ids == rel[:, s : s + 1])
        out_ref[:, k * step : (k + 1) * step] = jnp.where(hit, 1.0 / MB, 0.0)


def targets(me, positives, counts, order, c_dev):
    queries, slots = positives.shape
    return pl.pallas_call(
        functools.partial(target_kernel, order),
        out_shape=jax.ShapeDtypeStruct((queries, c_dev), F32),
        in_specs=[
            pl.BlockSpec(memory_space=pltpu.SMEM),
            whole((slots, queries)),
            whole((1, queries)),
        ],
        out_specs=whole((queries, c_dev)),
        scratch_shapes=[pltpu.VMEM((len(order), queries // len(order), slots), jnp.int32)],
        compiler_params=pltpu.CompilerParams(vmem_limit_bytes=8 << 20),
        cost_estimate=pl.CostEstimate(
            flops=2 * queries * slots * c_dev, transcendentals=0, bytes_accessed=4 * queries * c_dev
        ),
        name="targets",
    )(me.reshape(1), positives.T, counts.reshape(1, queries))


def score_kernel(c_ref, q_ref, target_ref, keep_ref, send_ref, dlogit_ref):
    c_dev = c_ref.shape[0]
    half = keep_ref.shape[0]
    step = min(512, c_dev)
    queries = q_ref[...]
    for k in range(c_dev // step):
        cut = slice(k * step, (k + 1) * step)
        logits = dot(c_ref[cut, :], queries, NT).T
        dlogit_ref[:, cut] = (jax.nn.sigmoid(logits) * (1.0 / MB) - target_ref[:, cut]).astype(BF16)
    grad = dot(dlogit_ref[...], c_ref[...], NN)
    keep_ref[...] = grad[:half]
    send_ref[...] = grad[half:]


def score(centroids, queries, target):
    c_dev, width = centroids.shape
    count = queries.shape[0]
    half = count // 2
    return pl.pallas_call(
        score_kernel,
        out_shape=(
            jax.ShapeDtypeStruct((half, width), F32),
            jax.ShapeDtypeStruct((half, width), F32),
            jax.ShapeDtypeStruct((count, c_dev), BF16),
        ),
        in_specs=[whole((c_dev, width)), whole((count, width)), whole((count, c_dev))],
        out_specs=(whole((half, width)), whole((half, width)), whole((count, c_dev))),
        compiler_params=pltpu.CompilerParams(vmem_limit_bytes=32 << 20),
        cost_estimate=pl.CostEstimate(
            flops=4 * count * c_dev * width, transcendentals=count * c_dev, bytes_accessed=2 * c_dev * width
        ),
        name="score",
    )(centroids, queries, target)


def outer_kernel(first, sub, dlogit_ref, q_ref, *rest):
    out_hbm, held_ref, sems = rest[-3:]
    queries = q_ref[...]
    copies = []
    for k in range(held_ref.shape[0] // sub):
        cut = slice(k * sub, (k + 1) * sub)
        held_ref[cut, :] = dot(dlogit_ref[:, cut], queries, TN)
        copies.append(
            pltpu.make_async_copy(held_ref.at[cut], out_hbm.at[pl.ds(first + k * sub, sub)], sems.at[k])
        )
        copies[-1].start()
    for copy in copies:
        copy.wait()


def outer(dlogit, queries, piece, pieces, grown):
    count, c_dev = dlogit.shape
    width = queries.shape[1]
    rows = c_dev // pieces
    sub = min(256, rows)
    return pl.pallas_call(
        functools.partial(outer_kernel, piece * rows, sub),
        out_shape=jax.ShapeDtypeStruct((c_dev, width), F32),
        grid=(1,),
        in_specs=[
            pl.BlockSpec((count, rows), lambda i: (0, piece)),
            pl.BlockSpec((count, width), lambda i: (0, 0)),
        ]
        + [pl.BlockSpec(memory_space=HBM)] * len(grown),
        out_specs=pl.BlockSpec(memory_space=HBM),
        scratch_shapes=[pltpu.VMEM((rows, width), F32), pltpu.SemaphoreType.DMA((rows // sub,))],
        input_output_aliases={2: 0} if grown else {},
        compiler_params=pltpu.CompilerParams(vmem_limit_bytes=16 << 20),
        cost_estimate=pl.CostEstimate(
            flops=2 * count * rows * width, transcendentals=0, bytes_accessed=4 * rows * width
        ),
        name="outer",
    )(dlogit, queries, *grown)


def shards(n, hidden_states, token_ids, up_weight, down_weight, centroids, positives, counts):
    me = lax.axis_index("cluster")
    bits = n.bit_length() - 1
    order = [int(format(k, f"0{bits}b")[::-1], 2) for k in range(n)]

    def swap(values, bit):
        return lax.ppermute(values, "cluster", [(i, i ^ bit) for i in range(n)])

    target = targets(me, positives, counts, order, centroids.shape[0])
    queries = encode(hidden_states, token_ids, up_weight, down_weight)
    for k in reversed(range(bits)):
        queries = jnp.concatenate([queries, swap(queries, 1 << k)], axis=0)
    queries = queries.reshape(-1, queries.shape[-1])
    keep, send, dlogit = score(centroids, queries, target)
    pieces = 4
    grown = []
    for k in range(bits):
        got = swap(send, 1 << k)
        if k < pieces:
            grown = [outer(dlogit, queries, k, pieces, grown)]
        total = keep + got
        half = total.shape[0] // 2
        keep, send = total[:half], total[half:]
    return (total, grown[0])


def solution(mesh):
    placed = (
        P(("groups", "cluster"), None, None),
        P(("groups", "cluster"), None),
        P(),
        P(),
        P("cluster", None),
        P("groups", None),
        P("groups"),
    )
    return jax.shard_map(
        functools.partial(shards, mesh.shape["cluster"]),
        mesh=mesh,
        in_specs=placed,
        out_specs=(P(("groups", "cluster"), None), P(("groups", "cluster"), None)),
        check_vma=False,
    )
```

time: 158 us -> 58.3 us (0.37)
  waiting for transfers between devices: 76.5 us -> 9.69 us
  matrix products: 28.9 us -> 0 us
  Pallas kernels: 0 us -> 27.6 us
  blocking collectives: 23.6 us -> 0 us
  between operations: 14.7 us -> 0.79 us
  starting transfers between devices: 0.04 us -> 11.3 us
  other arithmetic: 10.7 us -> 2.83 us
  local copies, waits for them, and re-layouts: 2.77 us -> 5.6 us
    unnamed x2 -> x0, waiting for transfers between devices: 76.5 us -> none
    dot_general x4 -> x0, matrix products: 28.9 us -> none  [the longest x1 8.63 us: encode(): ffn = jnp.dot(act, down_weight, preferred_element_type=jnp.float32)]
    pallas_call x0 -> x7, Pallas kernels: none -> 27.6 us  [the longest x1 12.1 us: encode(): pl.pallas_call(functools.partial(encode_kernel, up_step, down_step), out_...]
    all_gather x1 -> x0, blocking collectives: 23.6 us -> none  [shards(): gathered = lax.all_gather(queries, 'cluster', axis=0, tiled=True)]
    ppermute x0 -> x8, starting transfers between devices: none -> 11.3 us  [swap(): return lax.ppermute(values, 'cluster', [(i, i ^ bit) for i in range(n)])]
    ppermute x0 -> x8, waiting for transfers between devices: none -> 9.69 us  [swap(): return lax.ppermute(values, 'cluster', [(i, i ^ bit) for i in range(n)])]
    reduce_or x1 -> x0, other arithmetic: 7.2 us -> none  [logit_grads(): target = jnp.any(hits, axis=1).astype(jnp.float32)]
    unnamed x6 -> x10, local copies, waits for them, and re-layouts: 2.77 us -> 5.51 us
  transfers between devices with their start and end apart: 1 -> 8, of which waited for: 1 -> 5; matrix products, arithmetic and copies ran while one was open for 6% -> 1% of each run, Pallas kernels for 0% -> 20%
where the time goes in v1:
time: 58.3 us; the launch traced here: 57.8 us
  Pallas kernels  27.6 us (47%)
  starting transfers between devices  11.3 us (19%)
  waiting for transfers between devices  9.69 us (17%)
  local copies, waits for them, and re-layouts  5.6 us (10%)
  other arithmetic  2.83 us (5%)
  between operations  0.79 us (1%)
    pallas_call x1, Pallas kernels, encode(): pl.pallas_call(functools.partial(encode_kernel, up_step, down_step), out_...  12.1 us
    ppermute x8, starting transfers between devices, swap(): return lax.ppermute(values, 'cluster', [(i, i ^ bit) for i in range(n)])  11.3 us
    ppermute x8, waiting for transfers between devices, swap(): return lax.ppermute(values, 'cluster', [(i, i ^ bit) for i in range(n)])  9.69 us
    pallas_call x4, Pallas kernels, outer(): pl.pallas_call(functools.partial(outer_kernel, piece * rows, sub), out_sh...  9.43 us
    unnamed x10, local copies, waits for them, and re-layouts  5.51 us
    pallas_call x1, Pallas kernels, score(): pl.pallas_call(score_kernel, out_shape=(jax.ShapeDtypeStruct((half, width...  3.73 us
    pallas_call x1, Pallas kernels, targets(): pl.pallas_call(functools.partial(target_kernel, order), out_shape=jax.Sha...  2.4 us
    concatenate x3, other arithmetic, shards(): queries = jnp.concatenate([queries, swap(queries, 1 << k)], axis=0)  2.18 us
  transfers between devices with their start and end apart: 8, of which 5 were waited for; matrix products, arithmetic and copies ran while one was open for 1% of the time, Pallas kernels for 20%

profile of v1, /device:TPU:0, one launch (start us, length us, event | category | flops | bytes accessed | tf_op | source)
XLA Modules:
  0.0 57.8 jit_solution(17341716837199334509)
XLA Ops:
  0.6 12.1 %encode.1 = bf16[1,4,1024]{2,1,0:T(4,128)(2,1)} custom-call(bf16[4,128,1024]{2,1,0:T(8,128)(2,1)} %x_hbm.1, s32[4,128]{1,0:T(4,128)} %ids_ref.1, bf16[1024,2048]{1,0:T(8,128)(2,1)} %up_hbm.1, bf16[2048,1024]{1,0:T(8,128)(2,1)} %down_hbm.1), custom_call_target="tpu_custom_call" | custom-call | flops 4294967296 | bytes 9437184 | tf_op jit(solution)/shard_map/encode/pallas_call | solution.py:76
  12.7 4.1 %collective-permute-start = (bf16[1,4,1024]{2,1,0:T(4,128)(2,1)}, bf16[1,4,1024]{2,1,0:T(4,128)(2,1)S(1)}, u32[]{:S(2)}, u32[]{:S(2)}) collective-permute-start(bf16[1,4,1024]{2,1,0:T(4,128)(2,1)} %encode.1), channel_id=1, source_target_pairs={{0,8},{1,9},{2,10},{3,11},{4,12},{5,13},{6,14},{7,15},{8,0},{9,1},... | collective-permute-start | bytes 24584 | tf_op jit(solution)/shard_map/ppermute | solution.py:224
  16.8 0.7 %constant_dynamic-update-slice_fusion.4 = bf16[16,4,1024]{2,1,0:T(4,128)(2,1)S(1)} fusion(bf16[1,4,1024]{2,1,0:T(4,128)(2,1)} %encode.1), kind=kLoop, calls=%fused_computation.10 | loop fusion | bytes 16384
  17.5 0.7 %copy-done.1 = s32[64,16]{0,1:T(8,128)S(1)} copy-done((s32[64,16]{0,1:T(8,128)S(1)}, s32[64,16]{0,1:T(8,128)}, u32[]{:S(2)}) %copy-start.1) | copy-done | bytes 4120
  18.2 0.7 %copy-done.2 = s32[64]{0:T(128)S(1)} copy-done((s32[64]{0:T(128)S(1)}, s32[64]{0:T(128)}, u32[]{:S(2)}) %copy-start.2) | copy-done | bytes 280
  18.9 2.4 %targets.1.target_ref = f32[64,4096]{1,0:T(8,128)S(1)} custom-call(s32[1]{0:T(128)} %bitcast.me_ref, s32[16,64]{1,0:T(8,128)S(1)} %bitcast.3, s32[1,64]{1,0:T(1,128)S(1)} %bitcast.4), custom_call_target="tpu_custom_call" | custom-call | flops 8388608 | bytes 1048576 | tf_op jit(solution)/shard_map/targets/pallas_call | solution.py:125
  21.3 0.7 %pad_maximum_fusion.2 = bf16[2,4,1024]{2,1,0:T(4,128)(2,1)S(1)} fusion(bf16[1,4,1024]{2,1,0:T(4,128)(2,1)S(1)} %collective-permute-done, bf16[1,4,1024]{2,1,0:T(4,128)(2,1)} %encode.1), kind=kLoop, calls=%fused_computation.5 | loop fusion | flops 8192 | bytes 32768 | tf_op jit(solution)/shard_map/concatenate | solution.py:229
  22.0 1.6 %collective-permute-start.1 = (bf16[2,4,1024]{2,1,0:T(4,128)(2,1)S(1)}, bf16[2,4,1024]{2,1,0:T(4,128)(2,1)S(1)}, u32[]{:S(2)}, u32[]{:S(2)}) collective-permute-start(bf16[2,4,1024]{2,1,0:T(4,128)(2,1)S(1)} %pad_maximum_fusion.2), channel_id=1, source_target_pairs={{0,4},{1,5},{2,6},{3,7},{4,0},{5,1},{6,2},{7,3},{8,12},{9,13},{10,... | collective-permute-start | bytes 49160 | tf_op jit(solution)/shard_map/ppermute | solution.py:224
  23.7 2.1 %collective-permute-done.1 = bf16[2,4,1024]{2,1,0:T(4,128)(2,1)S(1)} collective-permute-done((bf16[2,4,1024]{2,1,0:T(4,128)(2,1)S(1)}, bf16[2,4,1024]{2,1,0:T(4,128)(2,1)S(1)}, u32[]{:S(2)}, u32[]{:S(2)}) %collective-permute-start.1) | collective-permute-done | bytes 16416 | tf_op jit(solution)/shard_map/ppermute | solution.py:224
  25.8 0.7 %pad_maximum_fusion.1 = bf16[4,4,1024]{2,1,0:T(4,128)(2,1)S(1)} fusion(bf16[2,4,1024]{2,1,0:T(4,128)(2,1)S(1)} %collective-permute-done.1, bf16[1,4,1024]{2,1,0:T(4,128)(2,1)S(1)} %collective-permute-done, bf16[1,4,1024]{2,1,0:T(4,128)(2,1)} %encode.1), kind=kLoop, calls=%fused_computation.3 | loop fusion | flops 32768 | bytes 65536 | tf_op jit(solution)/shard_map/concatenate | solution.py:229
  26.6 1.6 %collective-permute-start.2 = (bf16[4,4,1024]{2,1,0:T(4,128)(2,1)S(1)}, bf16[4,4,1024]{2,1,0:T(4,128)(2,1)S(1)}, u32[]{:S(2)}, u32[]{:S(2)}) collective-permute-start(bf16[4,4,1024]{2,1,0:T(4,128)(2,1)S(1)} %pad_maximum_fusion.1), channel_id=1, source_target_pairs={{0,2},{1,3},{2,0},{3,1},{4,6},{5,7},{6,4},{7,5},{8,10},{9,11},{10,... | collective-permute-start | bytes 98312 | tf_op jit(solution)/shard_map/ppermute | solution.py:224
  28.2 2.4 %collective-permute-done.2 = bf16[4,4,1024]{2,1,0:T(4,128)(2,1)S(1)} collective-permute-done((bf16[4,4,1024]{2,1,0:T(4,128)(2,1)S(1)}, bf16[4,4,1024]{2,1,0:T(4,128)(2,1)S(1)}, u32[]{:S(2)}, u32[]{:S(2)}) %collective-permute-start.2) | collective-permute-done | bytes 32800 | tf_op jit(solution)/shard_map/ppermute | solution.py:224
  30.5 0.7 %pad_maximum_fusion = bf16[8,4,1024]{2,1,0:T(4,128)(2,1)S(1)} fusion(bf16[4,4,1024]{2,1,0:T(4,128)(2,1)S(1)} %collective-permute-done.2, bf16[2,4,1024]{2,1,0:T(4,128)(2,1)S(1)} %collective-permute-done.1, bf16[1,4,1024]{2,1,0:T(4,128)(2,1)S(1)} %collective-permute-done, bf16[1,4,1024]{2,1,0:T(4,128)(2,1)} %encode.1), kind=kLoop, calls=%fused_computation.1 | loop fusion | flops 98304 | bytes 131072 | tf_op jit(solution)/shard_map/concatenate | solution.py:229
  31.4 1.2 %collective-permute-done.3 = bf16[8,4,1024]{2,1,0:T(4,128)(2,1)S(1)} collective-permute-done((bf16[8,4,1024]{2,1,0:T(4,128)(2,1)S(1)}, bf16[8,4,1024]{2,1,0:T(4,128)(2,1)S(1)}, u32[]{:S(2)}, u32[]{:S(2)}) %collective-permute-start.3) | collective-permute-done | bytes 65568 | tf_op jit(solution)/shard_map/ppermute | solution.py:224
  32.7 3.4 %copy-done = bf16[4096,1024]{1,0:T(8,128)(2,1)S(1)} copy-done((bf16[4096,1024]{1,0:T(8,128)(2,1)S(1)}, bf16[4096,1024]{1,0:T(8,128)(2,1)}, u32[]{:S(2)}) %copy-start) | copy-done | bytes 8388632
  36.1 3.7 %score.1 = (f32[32,1024]{1,0:T(8,128)S(1)}, f32[32,1024]{1,0:T(8,128)S(1)}, bf16[64,4096]{1,0:T(8,128)(2,1)S(1)}) custom-call(bf16[4096,1024]{1,0:T(8,128)(2,1)S(1)} %copy-done, bf16[64,1024]{1,0:T(8,128)(2,1)S(1)} %reshape.13.q_ref, f32[64,4096]{1,0:T(8,128)S(1)} %targets.1.target_ref), custom_call_target="tpu_custom_call" | custom-call | flops 1073741824 | bytes 8388608 | tf_op jit(solution)/shard_map/score/pallas_call | solution.py:161
  40.0 1.2 %collective-permute-done.4 = f32[32,1024]{1,0:T(8,128)S(1)} collective-permute-done((f32[32,1024]{1,0:T(8,128)S(1)}, f32[32,1024]{1,0:T(8,128)S(1)}, u32[]{:S(2)}, u32[]{:S(2)}) %collective-permute-start.4) | collective-permute-done | bytes 131104 | tf_op jit(solution)/shard_map/ppermute | solution.py:224
  41.3 1.6 %collective-permute-start.5 = (f32[16,1024]{1,0:T(8,128)S(1)}, f32[16,1024]{1,0:T(8,128)S(1)}, u32[]{:S(2)}, u32[]{:S(2)}) collective-permute-start(f32[16,1024]{1,0:T(8,128)S(1)} %slice.25), channel_id=1, source_target_pairs={{0,2},{1,3},{2,0},{3,1},{4,6},{5,7},{6,4},{7,5},{8,10},{9,11},{10,... | collective-permute-start | bytes 196616 | tf_op jit(solution)/shard_map/ppermute | solution.py:224
  42.8 2.7 %collective-permute-done.5 = f32[16,1024]{1,0:T(8,128)S(1)} collective-permute-done((f32[16,1024]{1,0:T(8,128)S(1)}, f32[16,1024]{1,0:T(8,128)S(1)}, u32[]{:S(2)}, u32[]{:S(2)}) %collective-permute-start.5) | collective-permute-done | bytes 65568 | tf_op jit(solution)/shard_map/ppermute | solution.py:224
  45.6 1.6 %collective-permute-start.6 = (f32[8,1024]{1,0:T(8,128)S(1)}, f32[8,1024]{1,0:T(8,128)S(1)}, u32[]{:S(2)}, u32[]{:S(2)}) collective-permute-start(f32[8,1024]{1,0:T(8,128)S(1)} %slice.27), channel_id=1, source_target_pairs={{0,4},{1,5},{2,6},{3,7},{4,0},{5,1},{6,2},{7,3},{8,12},{9,13},{10,... | collective-permute-start | bytes 98312 | tf_op jit(solution)/shard_map/ppermute | solution.py:224
  47.3 2.4 %outer.4.rest_0_ = f32[4096,1024]{1,0:T(8,128)} custom-call(bf16[64,4096]{1,0:T(8,128)(2,1)S(1)} %get-tuple-element.7.dlogit_ref, bf16[64,1024]{1,0:T(8,128)(2,1)S(1)} %reshape.13.q_ref), custom_call_target="tpu_custom_call" | custom-call | flops 134217728 | bytes 4194304 | tf_op jit(solution)/shard_map/outer/pallas_call | solution.py:198
  49.6 2.4 %outer.5.rest_0_ = f32[4096,1024]{1,0:T(8,128)} custom-call(bf16[64,4096]{1,0:T(8,128)(2,1)S(1)} %get-tuple-element.7.dlogit_ref, bf16[64,1024]{1,0:T(8,128)(2,1)S(1)} %reshape.13.q_ref, f32[4096,1024]{1,0:T(8,128)} %outer.4.rest_0_), custom_call_target="tpu_custom_call", output_to_operand_aliasing={{}: (2, {})} | custom-call | flops 134217728 | bytes 4194304 | tf_op jit(solution)/shard_map/outer/pallas_call | solution.py:198
  52.4 2.4 %outer.6.rest_0_ = f32[4096,1024]{1,0:T(8,128)} custom-call(bf16[64,4096]{1,0:T(8,128)(2,1)S(1)} %get-tuple-element.7.dlogit_ref, bf16[64,1024]{1,0:T(8,128)(2,1)S(1)} %reshape.13.q_ref, f32[4096,1024]{1,0:T(8,128)} %outer.5.rest_0_), custom_call_target="tpu_custom_call", output_to_operand_aliasing={{}: (2, {})} | custom-call | flops 134217728 | bytes 4194304 | tf_op jit(solution)/shard_map/outer/pallas_call | solution.py:198
  54.8 2.4 %outer.7 = f32[4096,1024]{1,0:T(8,128)} custom-call(bf16[64,4096]{1,0:T(8,128)(2,1)S(1)} %get-tuple-element.7.dlogit_ref, bf16[64,1024]{1,0:T(8,128)(2,1)S(1)} %reshape.13.q_ref, f32[4096,1024]{1,0:T(8,128)} %outer.6.rest_0_), custom_call_target="tpu_custom_call", output_to_operand_aliasing={{}: (2, {})} | custom-call | flops 134217728 | bytes 4194304 | tf_op jit(solution)/shard_map/outer/pallas_call | solution.py:198
  (21 shorter events, 1.5 us)
Async XLA Ops:
  12.7 8.6 %collective-permute-start = (bf16[1,4,1024]{2,1,0:T(4,128)(2,1)}, bf16[1,4,1024]{2,1,0:T(4,128)(2,1)S(1)}, u32[]{:S(2)}, u32[]{:S(2)}) collective-permute-start(bf16[1,4,1024]{2,1,0:T(4,128)(2,1)} %encode.1), channel_id=1, source_target_pairs={{0,8},{1,9},{2,10},{3,11},{4,12},{5,13},{6,14},{7,15},{8,0},{9,1},... | collective-permute-start | bytes 24584 | tf_op jit(solution)/shard_map/ppermute | solution.py:224
  17.5 0.7 %copy-start.1 = (s32[64,16]{0,1:T(8,128)S(1)}, s32[64,16]{0,1:T(8,128)}, u32[]{:S(2)}) copy-start(s32[64,16]{0,1:T(8,128)} %param.12) | copy-start | bytes 12292
  18.2 0.7 %copy-start.2 = (s32[64]{0:T(128)S(1)}, s32[64]{0:T(128)}, u32[]{:S(2)}) copy-start(s32[64]{0:T(128)} %param.13) | copy-start | bytes 772
  22.0 3.8 %collective-permute-start.1 = (bf16[2,4,1024]{2,1,0:T(4,128)(2,1)S(1)}, bf16[2,4,1024]{2,1,0:T(4,128)(2,1)S(1)}, u32[]{:S(2)}, u32[]{:S(2)}) collective-permute-start(bf16[2,4,1024]{2,1,0:T(4,128)(2,1)S(1)} %pad_maximum_fusion.2), channel_id=1, source_target_pairs={{0,4},{1,5},{2,6},{3,7},{4,0},{5,1},{6,2},{7,3},{8,12},{9,13},{10,... | collective-permute-start | bytes 49160 | tf_op jit(solution)/shard_map/ppermute | solution.py:224
  26.6 4.0 %collective-permute-start.2 = (bf16[4,4,1024]{2,1,0:T(4,128)(2,1)S(1)}, bf16[4,4,1024]{2,1,0:T(4,128)(2,1)S(1)}, u32[]{:S(2)}, u32[]{:S(2)}) collective-permute-start(bf16[4,4,1024]{2,1,0:T(4,128)(2,1)S(1)} %pad_maximum_fusion.1), channel_id=1, source_target_pairs={{0,2},{1,3},{2,0},{3,1},{4,6},{5,7},{6,4},{7,5},{8,10},{9,11},{10,... | collective-permute-start | bytes 98312 | tf_op jit(solution)/shard_map/ppermute | solution.py:224
  31.3 1.3 %collective-permute-start.3 = (bf16[8,4,1024]{2,1,0:T(4,128)(2,1)S(1)}, bf16[8,4,1024]{2,1,0:T(4,128)(2,1)S(1)}, u32[]{:S(2)}, u32[]{:S(2)}) collective-permute-start(bf16[8,4,1024]{2,1,0:T(4,128)(2,1)S(1)} %pad_maximum_fusion), channel_id=1, source_target_pairs={{0,1},{1,0},{2,3},{3,2},{4,5},{5,4},{6,7},{7,6},{8,9},{9,8},{10,11... | collective-permute-start | bytes 196616 | tf_op jit(solution)/shard_map/ppermute | solution.py:224
  32.7 3.4 %copy-start = (bf16[4096,1024]{1,0:T(8,128)(2,1)S(1)}, bf16[4096,1024]{1,0:T(8,128)(2,1)}, u32[]{:S(2)}) copy-start(bf16[4096,1024]{1,0:T(8,128)(2,1)} %c_ref.1) | copy-start | bytes 25165828
  39.8 1.4 %collective-permute-start.4 = (f32[32,1024]{1,0:T(8,128)S(1)}, f32[32,1024]{1,0:T(8,128)S(1)}, u32[]{:S(2)}, u32[]{:S(2)}) collective-permute-start(f32[32,1024]{1,0:T(8,128)S(1)} %get-tuple-element.6), channel_id=1, source_target_pairs={{0,1},{1,0},{2,3},{3,2},{4,5},{5,4},{6,7},{7,6},{8,9},{9,8},{10,11... | collective-permute-start | bytes 393224 | tf_op jit(solution)/shard_map/ppermute | solution.py:224
  41.3 4.3 %collective-permute-start.5 = (f32[16,1024]{1,0:T(8,128)S(1)}, f32[16,1024]{1,0:T(8,128)S(1)}, u32[]{:S(2)}, u32[]{:S(2)}) collective-permute-start(f32[16,1024]{1,0:T(8,128)S(1)} %slice.25), channel_id=1, source_target_pairs={{0,2},{1,3},{2,0},{3,1},{4,6},{5,7},{6,4},{7,5},{8,10},{9,11},{10,... | collective-permute-start | bytes 196616 | tf_op jit(solution)/shard_map/ppermute | solution.py:224
  45.6 6.4 %collective-permute-start.6 = (f32[8,1024]{1,0:T(8,128)S(1)}, f32[8,1024]{1,0:T(8,128)S(1)}, u32[]{:S(2)}, u32[]{:S(2)}) collective-permute-start(f32[8,1024]{1,0:T(8,128)S(1)} %slice.27), channel_id=1, source_target_pairs={{0,4},{1,5},{2,6},{3,7},{4,0},{5,1},{6,2},{7,3},{8,12},{9,13},{10,... | collective-permute-start | bytes 98312 | tf_op jit(solution)/shard_map/ppermute | solution.py:224
  52.0 5.1 %collective-permute-start.7 = (f32[4,1024]{1,0:T(4,128)S(1)}, f32[4,1024]{1,0:T(4,128)S(1)}, u32[]{:S(2)}, u32[]{:S(2)}) collective-permute-start(f32[4,1024]{1,0:T(4,128)S(1)} %slice.29), channel_id=1, source_target_pairs={{0,8},{1,9},{2,10},{3,11},{4,12},{5,13},{6,14},{7,15},{8,0},{9,1},... | collective-permute-start | bytes 49160 | tf_op jit(solution)/shard_map/ppermute | solution.py:224

commit v2 on v1

v2 whole, which is shorter than its diff:
```python
import functools

import jax
import jax.numpy as jnp
from jax import lax
from jax.experimental import pallas as pl
from jax.experimental.pallas import tpu as pltpu
from jax.sharding import PartitionSpec as P

MB = 32
EPS = 1e-05
F32 = jnp.float32
BF16 = jnp.bfloat16
HBM = pltpu.MemorySpace.HBM
NN = (((1,), (0,)), ((), ()))
NT = (((1,), (1,)), ((), ()))
TN = (((0,), (0,)), ((), ()))


def dot(a, b, dims):
    return lax.dot_general(a, b, dims, preferred_element_type=F32)


def held(count):
    return (pl.BlockSpec(memory_space=pltpu.VMEM),) * count


def far(values):
    return pltpu.with_memory_space_constraint(values, HBM)


def normed(values):
    centered = values - jnp.mean(values, axis=-1, keepdims=True)
    spread = jnp.mean(centered * centered, axis=-1, keepdims=True)
    return centered, lax.rsqrt(spread + EPS)


def mark_targets(rel, target_ref):
    asked, slots = rel.shape
    tiles = target_ref.shape[1] // 128
    entries, rows = 8 * slots, 8 * tiles
    sub = lax.broadcasted_iota(jnp.int32, (8, 1), 0)
    low_at = lax.broadcasted_iota(jnp.int32, (entries, 128), 1)
    row_at = lax.broadcasted_iota(jnp.int32, (entries, rows), 1)
    for q in range(0, asked, 8):
        own = [rel[q : q + 8, s : s + 1] for s in range(slots)]
        low = jnp.concatenate([lax.bitwise_and(r, 127) for r in own], axis=0)
        row = jnp.concatenate([lax.shift_right_arithmetic(r, 7) * 8 + sub for r in own], axis=0)
        lows = jnp.where(low_at == low, 1.0, 0.0).astype(BF16)
        rows_hit = jnp.where(row_at == row, 1.0, 0.0).astype(BF16)
        hits = dot(rows_hit, lows, TN)
        for t in range(tiles):
            target_ref[q : q + 8, t * 128 : (t + 1) * 128] = jnp.where(
                hits[t * 8 : (t + 1) * 8, :] > 0.5, 1.0 / MB, 0.0
            )


def encode_kernel(
    order, c_dev, up_step, x_hbm, ids_hbm, up_hbm, down_hbm, pos_hbm, cnt_hbm, q_ref, target_ref,
    x_ref, ids_ref, up_ref, down_ref, pos_ref, cnt_ref, own_ref, act_ref, sems,
):
    count, length, width = x_ref.shape
    hidden = up_ref.shape[1]
    slots, asked = pos_ref.shape
    me = lax.axis_index("cluster")
    small = [
        pltpu.make_async_copy(src, dst, sems.at[0, k])
        for k, (src, dst) in enumerate([(pos_hbm, pos_ref), (cnt_hbm, cnt_ref), (ids_hbm, ids_ref)])
    ]
    x_copy = pltpu.make_async_copy(x_hbm, x_ref, sems.at[0, 3])
    down_copy = pltpu.make_async_copy(down_hbm, down_ref, sems.at[0, 4])
    ups = []
    for k in range(hidden // up_step):
        cut = (slice(None), pl.ds(k * up_step, up_step))
        ups.append(pltpu.make_async_copy(up_hbm.at[cut], up_ref.at[cut], sems.at[1, k]))
    for copy in small + [x_copy] + ups + [down_copy]:
        copy.start()
    for copy in small:
        copy.wait()
    slot = lax.broadcasted_iota(jnp.int32, (slots, asked), 0)
    rel = jnp.where(slot < cnt_ref[...], pos_ref[...] - me * c_dev, -1).T
    per = own_ref.shape[1]
    for k in range(asked // per):
        own_ref[k] = rel[k * per : (k + 1) * per, :]
    rel = jnp.concatenate([own_ref[lax.bitwise_xor(me, k)] for k in order], axis=0)
    mark_targets(rel, target_ref)
    x_copy.wait()
    x = x_ref[...].reshape(count * length, width)
    for k, copy in enumerate(ups):
        copy.wait()
        cut = slice(k * up_step, (k + 1) * up_step)
        act_ref[:, cut] = jax.nn.gelu(dot(x, up_ref[:, cut], NN)).astype(BF16)
    kept = jnp.sum((ids_ref[...] != 0).astype(F32), axis=1, keepdims=True)
    place = lax.broadcasted_iota(jnp.int32, (length, 1), 0).astype(F32)
    down_copy.wait()
    rows = []
    for k in range(count):
        ffn = dot(act_ref[k * length : (k + 1) * length, :], down_ref[...], NN)
        centered, scale = normed(x_ref[k].astype(F32) + ffn)
        own = kept[k : k + 1, :]
        scale = jnp.where(place < own, scale, 0.0)
        rows.append(jnp.sum(centered * scale, axis=0, keepdims=True) / own)
    centered, scale = normed(jnp.concatenate(rows, axis=0))
    q_ref[...] = (centered * scale).astype(BF16)


def encode(states, ids, up_weight, down_weight, positives, counts, order, c_dev):
    count, length, width = states.shape
    hidden = up_weight.shape[1]
    asked, slots = positives.shape
    up_step = min(512, hidden)
    tokens = count * length
    return pl.pallas_call(
        functools.partial(encode_kernel, order, c_dev, up_step),
        out_shape=(pltpu.VMEM((count, width), BF16), pltpu.VMEM((asked, c_dev), F32)),
        in_specs=[pl.BlockSpec(memory_space=HBM)] * 6,
        out_specs=held(2),
        scratch_shapes=[
            pltpu.VMEM(states.shape, BF16),
            pltpu.VMEM(ids.shape, jnp.int32),
            pltpu.VMEM(up_weight.shape, BF16),
            pltpu.VMEM(down_weight.shape, BF16),
            pltpu.VMEM((slots, asked), jnp.int32),
            pltpu.VMEM((1, asked), jnp.int32),
            pltpu.VMEM((len(order), asked // len(order), slots), jnp.int32),
            pltpu.VMEM((tokens, hidden), BF16),
            pltpu.SemaphoreType.DMA((2, max(5, hidden // up_step))),
        ],
        compiler_params=pltpu.CompilerParams(vmem_limit_bytes=32 << 20),
        cost_estimate=pl.CostEstimate(
            flops=4 * tokens * hidden * width,
            transcendentals=tokens * hidden,
            bytes_accessed=4 * hidden * width + 2 * tokens * width,
        ),
        name="encode",
    )(*map(far, (states, ids, up_weight, down_weight, positives.T, counts.reshape(1, asked))))


def fetch_kernel(first, src_hbm, _, out_ref, mark_ref, sems):
    rows = out_ref.shape[0]
    copy = pltpu.make_async_copy(src_hbm.at[pl.ds(first, rows)], out_ref, sems.at[0])
    copy.start()
    mark_ref[...] = jnp.zeros_like(mark_ref)
    copy.wait()


def fetch(values, first, rows, behind):
    width = values.shape[1]
    return pl.pallas_call(
        functools.partial(fetch_kernel, first),
        out_shape=(pltpu.VMEM((rows, width), values.dtype), pltpu.VMEM((8, 128), F32)),
        in_specs=[pl.BlockSpec(memory_space=HBM), *held(1)],
        out_specs=held(2),
        scratch_shapes=[pltpu.SemaphoreType.DMA((1,))],
        compiler_params=pltpu.CompilerParams(vmem_limit_bytes=4 << 20),
        cost_estimate=pl.CostEstimate(flops=0, transcendentals=0, bytes_accessed=2 * rows * width),
        name="fetch",
    )(far(values), behind)


def join_kernel(a_ref, b_ref, *rest):
    out_ref = rest[-1]
    rows = a_ref.shape[0]
    out_ref[:rows, :] = a_ref[...]
    out_ref[rows:, :] = b_ref[...]


def join(a, b, *behind):
    rows, width = a.shape
    return pl.pallas_call(
        join_kernel,
        out_shape=pltpu.VMEM((2 * rows, width), a.dtype),
        in_specs=held(2 + len(behind)),
        out_specs=pl.BlockSpec(memory_space=pltpu.VMEM),
        compiler_params=pltpu.CompilerParams(vmem_limit_bytes=4 << 20),
        cost_estimate=pl.CostEstimate(flops=0, transcendentals=0, bytes_accessed=1024),
        name="join",
    )(a, b, *behind)


def score_kernel(parts, qa_ref, qb_ref, target_ref, *refs):
    c_refs, (q_ref, keep_ref, send_ref, dlogit_ref) = refs[:parts], refs[parts:]
    half = qa_ref.shape[0]
    q_ref[:half, :] = qa_ref[...]
    q_ref[half:, :] = qb_ref[...]
    queries = q_ref[...]
    first = 0
    for c_ref in c_refs:
        step = min(512, c_ref.shape[0])
        for k in range(c_ref.shape[0] // step):
            logits = dot(c_ref[k * step : (k + 1) * step, :], queries, NT).T
            cut = slice(first, first + step)
            dlogit_ref[:, cut] = (jax.nn.sigmoid(logits) * (1.0 / MB) - target_ref[:, cut]).astype(BF16)
            first += step
    first, grad = 0, 0.0
    for c_ref in c_refs:
        rows = c_ref.shape[0]
        grad += dot(dlogit_ref[:, first : first + rows], c_ref[...], NN)
        first += rows
    keep_ref[...] = grad[:half]
    send_ref[...] = grad[half:]


def score(centroids, qa, qb, target):
    half, width = qa.shape
    count, c_dev = target.shape
    return pl.pallas_call(
        functools.partial(score_kernel, len(centroids)),
        out_shape=(
            pltpu.VMEM((count, width), BF16),
            pltpu.VMEM((half, width), F32),
            pltpu.VMEM((half, width), F32),
            pltpu.VMEM((count, c_dev), BF16),
        ),
        in_specs=held(3 + len(centroids)),
        out_specs=held(4),
        compiler_params=pltpu.CompilerParams(vmem_limit_bytes=32 << 20),
        cost_estimate=pl.CostEstimate(
            flops=4 * count * c_dev * width, transcendentals=count * c_dev, bytes_accessed=2 * c_dev * width
        ),
        name="score",
    )(qa, qb, target, *centroids)


def outer_kernel(first, rows, sub, dlogit_ref, q_ref, *rest):
    out_hbm, held_ref, sems = rest[-3:]
    queries = q_ref[...]
    copies = []
    for k in range(rows // sub):
        cut = slice(k * sub, (k + 1) * sub)
        held_ref[cut, :] = dot(dlogit_ref[:, first + k * sub : first + (k + 1) * sub], queries, TN)
        copies.append(
            pltpu.make_async_copy(held_ref.at[cut], out_hbm.at[pl.ds(first + k * sub, sub)], sems.at[k])
        )
        copies[-1].start()
    for copy in copies:
        copy.wait()


def outer(dlogit, queries, first, rows, grown):
    count, c_dev = dlogit.shape
    width = queries.shape[1]
    sub = min(128, rows)
    return pl.pallas_call(
        functools.partial(outer_kernel, first, rows, sub),
        out_shape=jax.ShapeDtypeStruct((c_dev, width), F32),
        in_specs=[*held(2)] + [pl.BlockSpec(memory_space=HBM)] * len(grown),
        out_specs=pl.BlockSpec(memory_space=HBM),
        scratch_shapes=[pltpu.VMEM((rows, width), F32), pltpu.SemaphoreType.DMA((rows // sub,))],
        input_output_aliases={2: 0} if grown else {},
        compiler_params=pltpu.CompilerParams(vmem_limit_bytes=16 << 20),
        cost_estimate=pl.CostEstimate(
            flops=2 * count * rows * width, transcendentals=0, bytes_accessed=4 * rows * width
        ),
        name="outer",
    )(dlogit, queries, *grown)


def shards(n, hidden_states, token_ids, up_weight, down_weight, centroids, positives, counts):
    bits = n.bit_length() - 1
    order = [int(format(k, f"0{bits}b")[::-1], 2) for k in range(n)]
    c_dev = centroids.shape[0]

    def swap(values, bit):
        return lax.ppermute(values, "cluster", [(i, i ^ bit) for i in range(n)])

    queries, target = encode(
        hidden_states, token_ids, up_weight, down_weight, positives, counts, order, c_dev
    )
    part = c_dev // 2
    fetched = []
    for k in range(bits):
        got = swap(queries, 1 << (bits - 1 - k))
        marks = []
        if k in (1, 2):
            centroid_part, mark = fetch(centroids, (k - 1) * part, part, queries)
            fetched.append(centroid_part)
            marks.append(mark)
        if k < bits - 1:
            queries = join(queries, got, *marks)
    queries, keep, send, dlogit = score(fetched, queries, got, target)
    ends = [round(c_dev // 128 * share) * 128 for share in (0.125, 0.5, 0.78125, 1.0)]
    first, grown = 0, []
    for k in range(bits):
        got = swap(send, 1 << k)
        if k < len(ends) and ends[k] > first:
            grown = [outer(dlogit, queries, first, ends[k] - first, grown)]
            first = ends[k]
            got, grown[0] = lax.optimization_barrier((got, grown[0]))
        total = keep + got
        half = total.shape[0] // 2
        keep, send = total[:half], total[half:]
    return (total, grown[0])


def solution(mesh):
    placed = (
        P(("groups", "cluster"), None, None),
        P(("groups", "cluster"), None),
        P(),
        P(),
        P("cluster", None),
        P("groups", None),
        P("groups"),
    )
    return jax.shard_map(
        functools.partial(shards, mesh.shape["cluster"]),
        mesh=mesh,
        in_specs=placed,
        out_specs=(P(("groups", "cluster"), None), P(("groups", "cluster"), None)),
        check_vma=False,
    )
```

time: 58.3 us -> 44.5 us (0.76)
  waiting for transfers between devices: 9.69 us -> 3.07 us
  local copies, waits for them, and re-layouts: 5.6 us -> 0.02 us
  starting transfers between devices: 11.3 us -> 13.6 us
  other arithmetic: 2.83 us -> 0.65 us
  Pallas kernels: 27.6 us -> 26.2 us
    ppermute x8, waiting for transfers between devices: 9.69 us -> 3.07 us  [swap(): return lax.ppermute(values, 'cluster', [(i, i ^ bit) for i in range(n)])]
    unnamed x10 -> x0, local copies, waits for them, and re-layouts: 5.51 us -> none
    ppermute x8, starting transfers between devices: 11.3 us -> 13.6 us  [swap(): return lax.ppermute(values, 'cluster', [(i, i ^ bit) for i in range(n)])]
    concatenate x3 -> x0, other arithmetic: 2.18 us -> none  [shards(): queries = jnp.concatenate([queries, swap(queries, 1 << k)], axis=0)]
    pallas_call x7 -> x11, Pallas kernels: 27.6 us -> 26.2 us  [the longest x4 9.25 us: outer(): pl.pallas_call(functools.partial(outer_kernel, first, rows, sub), out_sha...]
  transfers between devices with their start and end apart: 8 -> 8, of which waited for: 5 -> 3; matrix products, arithmetic and copies ran while one was open for 1% -> 0% of each run, Pallas kernels for 20% -> 31%
where the time goes in v2:
time: 44.5 us; the launch traced here: 44.3 us
  Pallas kernels  26.2 us (59%)
  starting transfers between devices  13.6 us (31%)
  waiting for transfers between devices  3.07 us (7%)
  between operations  0.8 us (2%)
  other arithmetic  0.65 us (1%)
    ppermute x8, starting transfers between devices, swap(): return lax.ppermute(values, 'cluster', [(i, i ^ bit) for i in range(n)])  13.6 us
    pallas_call x4, Pallas kernels, outer(): pl.pallas_call(functools.partial(outer_kernel, first, rows, sub), out_sha...  9.25 us
    pallas_call x1, Pallas kernels, encode(): pl.pallas_call(functools.partial(encode_kernel, order, c_dev, up_step), o...  8.8 us
    pallas_call x2, Pallas kernels, fetch(): pl.pallas_call(functools.partial(fetch_kernel, first), out_shape=(pltpu.V...  4.39 us
    pallas_call x1, Pallas kernels, score(): pl.pallas_call(functools.partial(score_kernel, len(centroids)), out_shape...  3.74 us
    ppermute x8, waiting for transfers between devices, swap(): return lax.ppermute(values, 'cluster', [(i, i ^ bit) for i in range(n)])  3.07 us
  transfers between devices with their start and end apart: 8, of which 3 were waited for; matrix products, arithmetic and copies ran while one was open for 0% of the time, Pallas kernels for 31%

profile of v2, /device:TPU:0, one launch (start us, length us, event | category | flops | bytes accessed | tf_op | source)
XLA Modules:
  0.0 44.3 jit_solution(40087160365128963)
XLA Ops:
  0.6 8.8 %encode.1 = (bf16[4,1024]{1,0:T(4,128)(2,1)S(1)}, f32[64,4096]{1,0:T(8,128)S(1)}) custom-call(bf16[4,128,1024]{2,1,0:T(8,128)(2,1)} %x_hbm.1, s32[4,128]{1,0:T(4,128)} %ids_hbm.1, bf16[1024,2048]{1,0:T(8,128)(2,1)} %up_hbm.1, bf16[2048,1024]{1,0:T(8,128)(2,1)} %down_hbm.1, s32[16,64]{1,0:T(8,128)} %bitcast.2, s32[1,64]{1,0:T(1,128)} %bitcast.3), custom_call_target="tpu_custom_call" | custom-call | flops 4294967296 | bytes 9437184 | tf_op jit(solution)/shard_map/encode/pallas_call | solution.py:113
  9.4 4.1 %collective-permute-start = (bf16[4,1024]{1,0:T(4,128)(2,1)S(1)}, bf16[4,1024]{1,0:T(4,128)(2,1)S(1)}, u32[]{:S(2)}, u32[]{:S(2)}) collective-permute-start(bf16[4,1024]{1,0:T(4,128)(2,1)S(1)} %get-tuple-element.20.a_ref), channel_id=1, source_target_pairs={{0,8},{1,9},{2,10},{3,11},{4,12},{5,13},{6,14},{7,15},{8,0},{9,1},... | collective-permute-start | bytes 24584 | tf_op jit(solution)/shard_map/ppermute | solution.py:265
  13.5 1.6 %collective-permute-done.b_ref = bf16[4,1024]{1,0:T(4,128)(2,1)S(1)} collective-permute-done((bf16[4,1024]{1,0:T(4,128)(2,1)S(1)}, bf16[4,1024]{1,0:T(4,128)(2,1)S(1)}, u32[]{:S(2)}, u32[]{:S(2)}) %collective-permute-start) | collective-permute-done | bytes 8224 | tf_op jit(solution)/shard_map/ppermute | solution.py:265
  15.2 1.9 %collective-permute-start.1 = (bf16[8,1024]{1,0:T(8,128)(2,1)S(1)}, bf16[8,1024]{1,0:T(8,128)(2,1)S(1)}, u32[]{:S(2)}, u32[]{:S(2)}) collective-permute-start(bf16[8,1024]{1,0:T(8,128)(2,1)S(1)} %join.3._.a_ref), channel_id=1, source_target_pairs={{0,4},{1,5},{2,6},{3,7},{4,0},{5,1},{6,2},{7,3},{8,12},{9,13},{10,... | collective-permute-start | bytes 49160 | tf_op jit(solution)/shard_map/ppermute | solution.py:265
  17.1 2.2 %fetch.2 = (bf16[2048,1024]{1,0:T(8,128)(2,1)S(1)}, f32[8,128]{1,0:T(8,128)S(1)}) custom-call(bf16[4096,1024]{1,0:T(8,128)(2,1)} %src_hbm.3, bf16[8,1024]{1,0:T(8,128)(2,1)S(1)} %join.3._.a_ref), custom_call_target="tpu_custom_call" | custom-call | bytes 4194304 | tf_op jit(solution)/shard_map/fetch/pallas_call | solution.py:149
  19.3 0.0 collective-permute-done.1.b_ref
  19.3 1.6 %collective-permute-start.2 = (bf16[16,1024]{1,0:T(8,128)(2,1)S(1)}, bf16[16,1024]{1,0:T(8,128)(2,1)S(1)}, u32[]{:S(2)}, u32[]{:S(2)}) collective-permute-start(bf16[16,1024]{1,0:T(8,128)(2,1)S(1)} %join.4._.a_ref), channel_id=1, source_target_pairs={{0,2},{1,3},{2,0},{3,1},{4,6},{5,7},{6,4},{7,5},{8,10},{9,11},{10,... | collective-permute-start | bytes 98312 | tf_op jit(solution)/shard_map/ppermute | solution.py:265
  20.9 2.2 %fetch.3 = (bf16[2048,1024]{1,0:T(8,128)(2,1)S(1)}, f32[8,128]{1,0:T(8,128)S(1)}) custom-call(bf16[4096,1024]{1,0:T(8,128)(2,1)} %src_hbm.3, bf16[16,1024]{1,0:T(8,128)(2,1)S(1)} %join.4._.a_ref), custom_call_target="tpu_custom_call" | custom-call | bytes 4194304 | tf_op jit(solution)/shard_map/fetch/pallas_call | solution.py:149
  23.1 0.2 collective-permute-done.2.b_ref
  23.3 0.0 collective-permute-start.3
  23.3 1.2 %collective-permute-done.3.qb_ref = bf16[32,1024]{1,0:T(8,128)(2,1)S(1)} collective-permute-done((bf16[32,1024]{1,0:T(8,128)(2,1)S(1)}, bf16[32,1024]{1,0:T(8,128)(2,1)S(1)}, u32[]{:S(2)}, u32[]{:S(2)}) %collective-permute-start.3) | collective-permute-done | bytes 65568 | tf_op jit(solution)/shard_map/ppermute | solution.py:265
  24.6 3.7 %score.1 = (bf16[64,1024]{1,0:T(8,128)(2,1)S(1)}, f32[32,1024]{1,0:T(8,128)S(1)}, f32[32,1024]{1,0:T(8,128)S(1)}, bf16[64,4096]{1,0:T(8,128)(2,1)S(1)}) custom-call(bf16[32,1024]{1,0:T(8,128)(2,1)S(1)} %join.5.qa_ref, bf16[32,1024]{1,0:T(8,128)(2,1)S(1)} %collective-permute-done.3.qb_ref, f32[64,4096]{1,0:T(8,128)S(1)} %get-tuple-element.23.target_ref, ...), custom_call_target="tpu_custom_call" | custom-call | flops 1073741824 | bytes 8388608 | tf_op jit(solution)/shard_map/score/pallas_call | solution.py:207
  28.3 0.2 collective-permute-start.4
  28.5 1.6 %outer.4.rest_0_ = f32[4096,1024]{1,0:T(8,128)} custom-call(bf16[64,4096]{1,0:T(8,128)(2,1)S(1)} %get-tuple-element.28.dlogit_ref, bf16[64,1024]{1,0:T(8,128)(2,1)S(1)} %get-tuple-element.29.q_ref), custom_call_target="tpu_custom_call" | custom-call | flops 67108864 | bytes 2097152 | tf_op jit(solution)/shard_map/outer/pallas_call | solution.py:244
  30.1 0.0 collective-permute-done.4
  30.2 1.6 %collective-permute-start.5 = (f32[16,1024]{1,0:T(8,128)S(1)}, f32[16,1024]{1,0:T(8,128)S(1)}, u32[]{:S(2)}, u32[]{:S(2)}) collective-permute-start(f32[16,1024]{1,0:T(8,128)S(1)} %slice.25), channel_id=1, source_target_pairs={{0,2},{1,3},{2,0},{3,1},{4,6},{5,7},{6,4},{7,5},{8,10},{9,11},{10,... | collective-permute-start | bytes 196616 | tf_op jit(solution)/shard_map/ppermute | solution.py:265
  31.8 3.0 %outer.5.rest_0_ = f32[4096,1024]{1,0:T(8,128)} custom-call(bf16[64,4096]{1,0:T(8,128)(2,1)S(1)} %get-tuple-element.28.dlogit_ref, bf16[64,1024]{1,0:T(8,128)(2,1)S(1)} %get-tuple-element.29.q_ref, f32[4096,1024]{1,0:T(8,128)} %outer.4.rest_0_), custom_call_target="tpu_custom_call", output_to_operand_aliasing={{}: (2, {})} | custom-call | flops 201326592 | bytes 6291456 | tf_op jit(solution)/shard_map/outer/pallas_call | solution.py:244
  34.8 0.0 collective-permute-done.5
  34.8 1.5 %collective-permute-start.6 = (f32[8,1024]{1,0:T(8,128)S(1)}, f32[8,1024]{1,0:T(8,128)S(1)}, u32[]{:S(2)}, u32[]{:S(2)}) collective-permute-start(f32[8,1024]{1,0:T(8,128)S(1)} %slice.27), channel_id=1, source_target_pairs={{0,4},{1,5},{2,6},{3,7},{4,0},{5,1},{6,2},{7,3},{8,12},{9,13},{10,... | collective-permute-start | bytes 98312 | tf_op jit(solution)/shard_map/ppermute | solution.py:265
  36.4 2.5 %outer.6.rest_0_ = f32[4096,1024]{1,0:T(8,128)} custom-call(bf16[64,4096]{1,0:T(8,128)(2,1)S(1)} %get-tuple-element.28.dlogit_ref, bf16[64,1024]{1,0:T(8,128)(2,1)S(1)} %get-tuple-element.29.q_ref, f32[4096,1024]{1,0:T(8,128)} %outer.5.rest_0_), custom_call_target="tpu_custom_call", output_to_operand_aliasing={{}: (2, {})} | custom-call | flops 150994944 | bytes 4718592 | tf_op jit(solution)/shard_map/outer/pallas_call | solution.py:244
  38.9 0.0 collective-permute-done.6
  38.9 2.6 %collective-permute-start.7 = (f32[4,1024]{1,0:T(4,128)S(1)}, f32[4,1024]{1,0:T(4,128)S(1)}, u32[]{:S(2)}, u32[]{:S(2)}) collective-permute-start(f32[4,1024]{1,0:T(4,128)S(1)} %slice.29), channel_id=1, source_target_pairs={{0,8},{1,9},{2,10},{3,11},{4,12},{5,13},{6,14},{7,15},{8,0},{9,1},... | collective-permute-start | bytes 49160 | tf_op jit(solution)/shard_map/ppermute | solution.py:265
  41.5 2.1 %outer.7 = f32[4096,1024]{1,0:T(8,128)} custom-call(bf16[64,4096]{1,0:T(8,128)(2,1)S(1)} %get-tuple-element.28.dlogit_ref, bf16[64,1024]{1,0:T(8,128)(2,1)S(1)} %get-tuple-element.29.q_ref, f32[4096,1024]{1,0:T(8,128)} %outer.6.rest_0_), custom_call_target="tpu_custom_call", output_to_operand_aliasing={{}: (2, {})} | custom-call | flops 117440512 | bytes 3670016 | tf_op jit(solution)/shard_map/outer/pallas_call | solution.py:244
  43.7 0.6 %slice_add_fusion.2 = f32[4,1024]{1,0:T(4,128)} fusion(f32[4,1024]{1,0:T(4,128)S(1)} %collective-permute-done.7, f32[8,1024]{1,0:T(8,128)S(1)} %slice_add_fusion.1), kind=kLoop, calls=%fused_computation.2 | loop fusion | flops 4096 | bytes 49152 | tf_op jit(solution)/shard_map/add | solution.py:290
  (10 shorter events, 0.1 us)
Async XLA Ops:
  9.4 5.7 %collective-permute-start = (bf16[4,1024]{1,0:T(4,128)(2,1)S(1)}, bf16[4,1024]{1,0:T(4,128)(2,1)S(1)}, u32[]{:S(2)}, u32[]{:S(2)}) collective-permute-start(bf16[4,1024]{1,0:T(4,128)(2,1)S(1)} %get-tuple-element.20.a_ref), channel_id=1, source_target_pairs={{0,8},{1,9},{2,10},{3,11},{4,12},{5,13},{6,14},{7,15},{8,0},{9,1},... | collective-permute-start | bytes 24584 | tf_op jit(solution)/shard_map/ppermute | solution.py:265
  15.2 4.1 %collective-permute-start.1 = (bf16[8,1024]{1,0:T(8,128)(2,1)S(1)}, bf16[8,1024]{1,0:T(8,128)(2,1)S(1)}, u32[]{:S(2)}, u32[]{:S(2)}) collective-permute-start(bf16[8,1024]{1,0:T(8,128)(2,1)S(1)} %join.3._.a_ref), channel_id=1, source_target_pairs={{0,4},{1,5},{2,6},{3,7},{4,0},{5,1},{6,2},{7,3},{8,12},{9,13},{10,... | collective-permute-start | bytes 49160 | tf_op jit(solution)/shard_map/ppermute | solution.py:265
  19.3 4.0 %collective-permute-start.2 = (bf16[16,1024]{1,0:T(8,128)(2,1)S(1)}, bf16[16,1024]{1,0:T(8,128)(2,1)S(1)}, u32[]{:S(2)}, u32[]{:S(2)}) collective-permute-start(bf16[16,1024]{1,0:T(8,128)(2,1)S(1)} %join.4._.a_ref), channel_id=1, source_target_pairs={{0,2},{1,3},{2,0},{3,1},{4,6},{5,7},{6,4},{7,5},{8,10},{9,11},{10,... | collective-permute-start | bytes 98312 | tf_op jit(solution)/shard_map/ppermute | solution.py:265
  23.3 1.3 %collective-permute-start.3 = (bf16[32,1024]{1,0:T(8,128)(2,1)S(1)}, bf16[32,1024]{1,0:T(8,128)(2,1)S(1)}, u32[]{:S(2)}, u32[]{:S(2)}) collective-permute-start(bf16[32,1024]{1,0:T(8,128)(2,1)S(1)} %join.5.qa_ref), channel_id=1, source_target_pairs={{0,1},{1,0},{2,3},{3,2},{4,5},{5,4},{6,7},{7,6},{8,9},{9,8},{10,11... | collective-permute-start | bytes 196616 | tf_op jit(solution)/shard_map/ppermute | solution.py:265
  28.3 1.8 %collective-permute-start.4 = (f32[32,1024]{1,0:T(8,128)S(1)}, f32[32,1024]{1,0:T(8,128)S(1)}, u32[]{:S(2)}, u32[]{:S(2)}) collective-permute-start(f32[32,1024]{1,0:T(8,128)S(1)} %get-tuple-element.27), channel_id=1, source_target_pairs={{0,1},{1,0},{2,3},{3,2},{4,5},{5,4},{6,7},{7,6},{8,9},{9,8},{10,11... | collective-permute-start | bytes 393224 | tf_op jit(solution)/shard_map/ppermute | solution.py:265
  30.2 4.6 %collective-permute-start.5 = (f32[16,1024]{1,0:T(8,128)S(1)}, f32[16,1024]{1,0:T(8,128)S(1)}, u32[]{:S(2)}, u32[]{:S(2)}) collective-permute-start(f32[16,1024]{1,0:T(8,128)S(1)} %slice.25), channel_id=1, source_target_pairs={{0,2},{1,3},{2,0},{3,1},{4,6},{5,7},{6,4},{7,5},{8,10},{9,11},{10,... | collective-permute-start | bytes 196616 | tf_op jit(solution)/shard_map/ppermute | solution.py:265
  34.8 4.0 %collective-permute-start.6 = (f32[8,1024]{1,0:T(8,128)S(1)}, f32[8,1024]{1,0:T(8,128)S(1)}, u32[]{:S(2)}, u32[]{:S(2)}) collective-permute-start(f32[8,1024]{1,0:T(8,128)S(1)} %slice.27), channel_id=1, source_target_pairs={{0,4},{1,5},{2,6},{3,7},{4,0},{5,1},{6,2},{7,3},{8,12},{9,13},{10,... | collective-permute-start | bytes 98312 | tf_op jit(solution)/shard_map/ppermute | solution.py:265
  38.9 4.8 %collective-permute-start.7 = (f32[4,1024]{1,0:T(4,128)S(1)}, f32[4,1024]{1,0:T(4,128)S(1)}, u32[]{:S(2)}, u32[]{:S(2)}) collective-permute-start(f32[4,1024]{1,0:T(4,128)S(1)} %slice.29), channel_id=1, source_target_pairs={{0,8},{1,9},{2,10},{3,11},{4,12},{5,13},{6,14},{7,15},{8,0},{9,1},... | collective-permute-start | bytes 49160 | tf_op jit(solution)/shard_map/ppermute | solution.py:265

commit v3 on v2

--- a/solution.py
+++ b/solution.py
@@ -11,6 +11,7 @@
 EPS = 1e-05
 F32 = jnp.float32
 BF16 = jnp.bfloat16
+SHARES = (0.0, 0.46875, 0.75, 1.0)
 HBM = pltpu.MemorySpace.HBM
 NN = (((1,), (0,)), ((), ()))
 NT = (((1,), (1,)), ((), ()))
@@ -35,28 +36,8 @@
     return centered, lax.rsqrt(spread + EPS)
 
 
-def mark_targets(rel, target_ref):
-    asked, slots = rel.shape
-    tiles = target_ref.shape[1] // 128
-    entries, rows = 8 * slots, 8 * tiles
-    sub = lax.broadcasted_iota(jnp.int32, (8, 1), 0)
-    low_at = lax.broadcasted_iota(jnp.int32, (entries, 128), 1)
-    row_at = lax.broadcasted_iota(jnp.int32, (entries, rows), 1)
-    for q in range(0, asked, 8):
-        own = [rel[q : q + 8, s : s + 1] for s in range(slots)]
-        low = jnp.concatenate([lax.bitwise_and(r, 127) for r in own], axis=0)
-        row = jnp.concatenate([lax.shift_right_arithmetic(r, 7) * 8 + sub for r in own], axis=0)
-        lows = jnp.where(low_at == low, 1.0, 0.0).astype(BF16)
-        rows_hit = jnp.where(row_at == row, 1.0, 0.0).astype(BF16)
-        hits = dot(rows_hit, lows, TN)
-        for t in range(tiles):
-            target_ref[q : q + 8, t * 128 : (t + 1) * 128] = jnp.where(
-                hits[t * 8 : (t + 1) * 8, :] > 0.5, 1.0 / MB, 0.0
-            )
-
-
 def encode_kernel(
-    order, c_dev, up_step, x_hbm, ids_hbm, up_hbm, down_hbm, pos_hbm, cnt_hbm, q_ref, target_ref,
+    order, c_dev, up_step, x_hbm, ids_hbm, up_hbm, down_hbm, pos_hbm, cnt_hbm, q_ref, rel_ref,
     x_ref, ids_ref, up_ref, down_ref, pos_ref, cnt_ref, own_ref, act_ref, sems,
 ):
     count, length, width = x_ref.shape
@@ -82,8 +63,7 @@
     per = own_ref.shape[1]
     for k in range(asked // per):
         own_ref[k] = rel[k * per : (k + 1) * per, :]
-    rel = jnp.concatenate([own_ref[lax.bitwise_xor(me, k)] for k in order], axis=0)
-    mark_targets(rel, target_ref)
+    rel_ref[...] = jnp.concatenate([own_ref[lax.bitwise_xor(me, k)] for k in order], axis=0)
     x_copy.wait()
     x = x_ref[...].reshape(count * length, width)
     for k, copy in enumerate(ups):
@@ -112,7 +92,7 @@
     tokens = count * length
     return pl.pallas_call(
         functools.partial(encode_kernel, order, c_dev, up_step),
-        out_shape=(pltpu.VMEM((count, width), BF16), pltpu.VMEM((asked, c_dev), F32)),
+        out_shape=(pltpu.VMEM((count, width), BF16), pltpu.VMEM((asked, slots), jnp.int32)),
         in_specs=[pl.BlockSpec(memory_space=HBM)] * 6,
         out_specs=held(2),
         scratch_shapes=[
@@ -134,6 +114,43 @@
         ),
         name="encode",
     )(*map(far, (states, ids, up_weight, down_weight, positives.T, counts.reshape(1, asked))))
+
+
+def target_kernel(rel_ref, _, target_ref, mark_ref):
+    rel = rel_ref[...]
+    asked, slots = rel.shape
+    mark_ref[...] = jnp.zeros_like(mark_ref)
+    tiles = target_ref.shape[1] // 128
+    entries, rows = 8 * slots, 8 * tiles
+    sub = lax.broadcasted_iota(jnp.int32, (8, 1), 0)
+    low_at = lax.broadcasted_iota(jnp.int32, (entries, 128), 1)
+    row_at = lax.broadcasted_iota(jnp.int32, (entries, rows), 1)
+    for q in range(0, asked, 8):
+        own = [rel[q : q + 8, s : s + 1] for s in range(slots)]
+        low = jnp.concatenate([lax.bitwise_and(r, 127) for r in own], axis=0)
+        row = jnp.concatenate([lax.shift_right_arithmetic(r, 7) * 8 + sub for r in own], axis=0)
+        lows = jnp.where(low_at == low, 1.0, 0.0).astype(BF16)
+        rows_hit = jnp.where(row_at == row, 1.0, 0.0).astype(BF16)
+        hits = dot(rows_hit, lows, TN)
+        for t in range(tiles):
+            target_ref[q : q + 8, t * 128 : (t + 1) * 128] = jnp.where(
+                hits[t * 8 : (t + 1) * 8, :] > 0.5, 1.0 / MB, 0.0
+            )
+
+
+def targets(rel, c_dev, behind):
+    asked, slots = rel.shape
+    return pl.pallas_call(
+        target_kernel,
+        out_shape=(pltpu.VMEM((asked, c_dev), F32), pltpu.VMEM((8, 128), F32)),
+        in_specs=held(2),
+        out_specs=held(2),
+        compiler_params=pltpu.CompilerParams(vmem_limit_bytes=8 << 20),
+        cost_estimate=pl.CostEstimate(
+            flops=16 * asked * slots * c_dev, transcendentals=0, bytes_accessed=4 * asked * c_dev
+        ),
+        name="targets",
+    )(rel, behind)
 
 
 def fetch_kernel(first, src_hbm, _, out_ref, mark_ref, sems):
@@ -258,31 +275,37 @@
 
 def shards(n, hidden_states, token_ids, up_weight, down_weight, centroids, positives, counts):
     bits = n.bit_length() - 1
-    order = [int(format(k, f"0{bits}b")[::-1], 2) for k in range(n)]
+    pairs = [1] + [1 << k | 1 for k in range(1, bits)]
+    order = [0]
+    for pair in reversed(pairs):
+        order += [k ^ pair for k in order]
     c_dev = centroids.shape[0]
 
-    def swap(values, bit):
-        return lax.ppermute(values, "cluster", [(i, i ^ bit) for i in range(n)])
-
-    queries, target = encode(
+    def swap(values, pair):
+        return lax.ppermute(values, "cluster", [(i, i ^ pair) for i in range(n)])
+
+    queries, rel = encode(
         hidden_states, token_ids, up_weight, down_weight, positives, counts, order, c_dev
     )
     part = c_dev // 2
     fetched = []
-    for k in range(bits):
-        got = swap(queries, 1 << (bits - 1 - k))
+    for k, pair in enumerate(reversed(pairs)):
+        got = swap(queries, pair)
         marks = []
-        if k in (1, 2):
-            centroid_part, mark = fetch(centroids, (k - 1) * part, part, queries)
+        if k == min(2, bits - 2):
+            target, mark = targets(rel, c_dev, queries)
+            marks.append(mark)
+        if k < 2:
+            centroid_part, mark = fetch(centroids, k * part, part, queries)
             fetched.append(centroid_part)
             marks.append(mark)
         if k < bits - 1:
             queries = join(queries, got, *marks)
     queries, keep, send, dlogit = score(fetched, queries, got, target)
-    ends = [round(c_dev // 128 * share) * 128 for share in (0.125, 0.5, 0.78125, 1.0)]
+    ends = [round(c_dev // 128 * share) * 128 for share in SHARES]
     first, grown = 0, []
-    for k in range(bits):
-        got = swap(send, 1 << k)
+    for k, pair in enumerate(pairs):
+        got = swap(send, pair)
         if k < len(ends) and ends[k] > first:
             grown = [outer(dlogit, queries, first, ends[k] - first, grown)]
             first = ends[k]

time: 44.5 us -> 42.2 us (0.948)
  starting transfers between devices: 13.6 us -> 10.6 us
  waiting for transfers between devices: 3.07 us -> 3.91 us
    ppermute x8, starting transfers between devices: 13.6 us -> 10.6 us  [swap(): return lax.ppermute(values, 'cluster', [(i, i ^ pair) for i in range(n)])]
    pallas_call x0 -> x1, Pallas kernels: none -> 1.47 us  [targets(): pl.pallas_call(target_kernel, out_shape=(pltpu.VMEM((asked, c_dev), F32),...]
    pallas_call x4 -> x3, Pallas kernels: 9.25 us -> 8.32 us  [outer(): pl.pallas_call(functools.partial(outer_kernel, first, rows, sub), out_sha...]
    ppermute x8, waiting for transfers between devices: 3.07 us -> 3.91 us  [swap(): return lax.ppermute(values, 'cluster', [(i, i ^ pair) for i in range(n)])]
    pallas_call x1, Pallas kernels: 8.8 us -> 8.13 us  [encode(): pl.pallas_call(functools.partial(encode_kernel, order, c_dev, up_step), o...]
  transfers between devices with their start and end apart: 8 -> 8, of which waited for: 3 -> 5; matrix products, arithmetic and copies ran while one was open for 0% -> 0% of each run, Pallas kernels for 31% -> 34%
where the time goes in v3:
time: 42.2 us; the launch traced here: 42 us
  Pallas kernels  26.1 us (62%)
  starting transfers between devices  10.6 us (25%)
  waiting for transfers between devices  3.91 us (9%)
  between operations  0.77 us (2%)
  other arithmetic  0.65 us (2%)
    ppermute x8, starting transfers between devices, swap(): return lax.ppermute(values, 'cluster', [(i, i ^ pair) for i in range(n)])  10.6 us
    pallas_call x3, Pallas kernels, outer(): pl.pallas_call(functools.partial(outer_kernel, first, rows, sub), out_sha...  8.32 us
    pallas_call x1, Pallas kernels, encode(): pl.pallas_call(functools.partial(encode_kernel, order, c_dev, up_step), o...  8.13 us
    pallas_call x2, Pallas kernels, fetch(): pl.pallas_call(functools.partial(fetch_kernel, first), out_shape=(pltpu.V...  4.39 us
    ppermute x8, waiting for transfers between devices, swap(): return lax.ppermute(values, 'cluster', [(i, i ^ pair) for i in range(n)])  3.91 us
    pallas_call x1, Pallas kernels, score(): pl.pallas_call(functools.partial(score_kernel, len(centroids)), out_shape...  3.73 us
    pallas_call x1, Pallas kernels, targets(): pl.pallas_call(target_kernel, out_shape=(pltpu.VMEM((asked, c_dev), F32),...  1.47 us
  transfers between devices with their start and end apart: 8, of which 5 were waited for; matrix products, arithmetic and copies ran while one was open for 0% of the time, Pallas kernels for 34%

profile of v3, /device:TPU:0, one launch (start us, length us, event | category | flops | bytes accessed | tf_op | source)
XLA Modules:
  0.0 42.0 jit_solution(7292348702983061458)
XLA Ops:
  0.6 8.1 %encode.1 = (bf16[4,1024]{1,0:T(4,128)(2,1)S(1)}, s32[64,16]{1,0:T(8,128)S(1)}) custom-call(bf16[4,128,1024]{2,1,0:T(8,128)(2,1)} %x_hbm.1, s32[4,128]{1,0:T(4,128)} %ids_hbm.1, bf16[1024,2048]{1,0:T(8,128)(2,1)} %up_hbm.1, bf16[2048,1024]{1,0:T(8,128)(2,1)} %down_hbm.1, s32[16,64]{1,0:T(8,128)} %bitcast.2, s32[1,64]{1,0:T(1,128)} %bitcast.3), custom_call_target="tpu_custom_call" | custom-call | flops 4294967296 | bytes 9437184 | tf_op jit(solution)/shard_map/encode/pallas_call | solution.py:93
  8.8 3.5 %collective-permute-start = (bf16[4,1024]{1,0:T(4,128)(2,1)S(1)}, bf16[4,1024]{1,0:T(4,128)(2,1)S(1)}, u32[]{:S(2)}, u32[]{:S(2)}) collective-permute-start(bf16[4,1024]{1,0:T(4,128)(2,1)S(1)} %get-tuple-element.20._.a_ref), channel_id=1, source_target_pairs={{0,9},{1,8},{2,11},{3,10},{4,13},{5,12},{6,15},{7,14},{8,1},{9,0},... | collective-permute-start | bytes 24584 | tf_op jit(solution)/shard_map/ppermute | solution.py:285
  12.3 2.2 %fetch.2 = (bf16[2048,1024]{1,0:T(8,128)(2,1)S(1)}, f32[8,128]{1,0:T(8,128)S(1)}) custom-call(bf16[4096,1024]{1,0:T(8,128)(2,1)} %src_hbm.3, bf16[4,1024]{1,0:T(4,128)(2,1)S(1)} %get-tuple-element.20._.a_ref), custom_call_target="tpu_custom_call" | custom-call | bytes 4194304 | tf_op jit(solution)/shard_map/fetch/pallas_call | solution.py:166
  14.5 0.0 collective-permute-done.b_ref
  14.5 1.9 %collective-permute-start.1 = (bf16[8,1024]{1,0:T(8,128)(2,1)S(1)}, bf16[8,1024]{1,0:T(8,128)(2,1)S(1)}, u32[]{:S(2)}, u32[]{:S(2)}) collective-permute-start(bf16[8,1024]{1,0:T(8,128)(2,1)S(1)} %join.3._.a_ref), channel_id=1, source_target_pairs={{0,5},{1,4},{2,7},{3,6},{4,1},{5,0},{6,3},{7,2},{8,13},{9,12},{10,... | collective-permute-start | bytes 49160 | tf_op jit(solution)/shard_map/ppermute | solution.py:285
  16.5 2.2 %fetch.3 = (bf16[2048,1024]{1,0:T(8,128)(2,1)S(1)}, f32[8,128]{1,0:T(8,128)S(1)}) custom-call(bf16[4096,1024]{1,0:T(8,128)(2,1)} %src_hbm.3, bf16[8,1024]{1,0:T(8,128)(2,1)S(1)} %join.3._.a_ref), custom_call_target="tpu_custom_call" | custom-call | bytes 4194304 | tf_op jit(solution)/shard_map/fetch/pallas_call | solution.py:166
  18.7 1.0 %collective-permute-start.2 = (bf16[16,1024]{1,0:T(8,128)(2,1)S(1)}, bf16[16,1024]{1,0:T(8,128)(2,1)S(1)}, u32[]{:S(2)}, u32[]{:S(2)}) collective-permute-start(bf16[16,1024]{1,0:T(8,128)(2,1)S(1)} %join.4._.a_ref), channel_id=1, source_target_pairs={{0,3},{1,2},{2,1},{3,0},{4,7},{5,6},{6,5},{7,4},{8,11},{9,10},{10,... | collective-permute-start | bytes 98312 | tf_op jit(solution)/shard_map/ppermute | solution.py:285
  19.7 1.5 %targets.1 = (f32[64,4096]{1,0:T(8,128)S(1)}, f32[8,128]{1,0:T(8,128)S(1)}) custom-call(s32[64,16]{1,0:T(8,128)S(1)} %get-tuple-element.23.rel_ref, bf16[16,1024]{1,0:T(8,128)(2,1)S(1)} %join.4._.a_ref), custom_call_target="tpu_custom_call" | custom-call | flops 67108864 | bytes 1048576 | tf_op jit(solution)/shard_map/targets/pallas_call | solution.py:143
  21.2 1.2 %collective-permute-done.2.b_ref = bf16[16,1024]{1,0:T(8,128)(2,1)S(1)} collective-permute-done((bf16[16,1024]{1,0:T(8,128)(2,1)S(1)}, bf16[16,1024]{1,0:T(8,128)(2,1)S(1)}, u32[]{:S(2)}, u32[]{:S(2)}) %collective-permute-start.2) | collective-permute-done | bytes 32800 | tf_op jit(solution)/shard_map/ppermute | solution.py:285
  22.4 0.1 collective-permute-start.3
  22.5 1.1 %collective-permute-done.3.qb_ref = bf16[32,1024]{1,0:T(8,128)(2,1)S(1)} collective-permute-done((bf16[32,1024]{1,0:T(8,128)(2,1)S(1)}, bf16[32,1024]{1,0:T(8,128)(2,1)S(1)}, u32[]{:S(2)}, u32[]{:S(2)}) %collective-permute-start.3) | collective-permute-done | bytes 65568 | tf_op jit(solution)/shard_map/ppermute | solution.py:285
  23.6 3.7 %score.1 = (bf16[64,1024]{1,0:T(8,128)(2,1)S(1)}, f32[32,1024]{1,0:T(8,128)S(1)}, f32[32,1024]{1,0:T(8,128)S(1)}, bf16[64,4096]{1,0:T(8,128)(2,1)S(1)}) custom-call(bf16[32,1024]{1,0:T(8,128)(2,1)S(1)} %join.5.qa_ref, bf16[32,1024]{1,0:T(8,128)(2,1)S(1)} %collective-permute-done.3.qb_ref, f32[64,4096]{1,0:T(8,128)S(1)} %get-tuple-element.25.target_ref, ...), custom_call_target="tpu_custom_call" | custom-call | flops 1073741824 | bytes 8388608 | tf_op jit(solution)/shard_map/score/pallas_call | solution.py:224
  27.4 0.2 collective-permute-start.4
  27.6 1.2 %collective-permute-done.4 = f32[32,1024]{1,0:T(8,128)S(1)} collective-permute-done((f32[32,1024]{1,0:T(8,128)S(1)}, f32[32,1024]{1,0:T(8,128)S(1)}, u32[]{:S(2)}, u32[]{:S(2)}) %collective-permute-start.4) | collective-permute-done | bytes 131104 | tf_op jit(solution)/shard_map/ppermute | solution.py:285
  28.8 1.4 %collective-permute-start.5 = (f32[16,1024]{1,0:T(8,128)S(1)}, f32[16,1024]{1,0:T(8,128)S(1)}, u32[]{:S(2)}, u32[]{:S(2)}) collective-permute-start(f32[16,1024]{1,0:T(8,128)S(1)} %slice.25), channel_id=1, source_target_pairs={{0,3},{1,2},{2,1},{3,0},{4,7},{5,6},{6,5},{7,4},{8,11},{9,10},{10,... | collective-permute-start | bytes 196616 | tf_op jit(solution)/shard_map/ppermute | solution.py:285
  30.2 3.5 %outer.3.rest_0_ = f32[4096,1024]{1,0:T(8,128)} custom-call(bf16[64,4096]{1,0:T(8,128)(2,1)S(1)} %get-tuple-element.30.dlogit_ref, bf16[64,1024]{1,0:T(8,128)(2,1)S(1)} %get-tuple-element.31.q_ref), custom_call_target="tpu_custom_call" | custom-call | flops 251658240 | bytes 7864320 | tf_op jit(solution)/shard_map/outer/pallas_call | solution.py:261
  33.7 0.0 collective-permute-done.5
  33.8 0.6 %collective-permute-start.6 = (f32[8,1024]{1,0:T(8,128)S(1)}, f32[8,1024]{1,0:T(8,128)S(1)}, u32[]{:S(2)}, u32[]{:S(2)}) collective-permute-start(f32[8,1024]{1,0:T(8,128)S(1)} %slice.27), channel_id=1, source_target_pairs={{0,5},{1,4},{2,7},{3,6},{4,1},{5,0},{6,3},{7,2},{8,13},{9,12},{10,... | collective-permute-start | bytes 98312 | tf_op jit(solution)/shard_map/ppermute | solution.py:285
  34.4 2.5 %outer.4.rest_0_ = f32[4096,1024]{1,0:T(8,128)} custom-call(bf16[64,4096]{1,0:T(8,128)(2,1)S(1)} %get-tuple-element.30.dlogit_ref, bf16[64,1024]{1,0:T(8,128)(2,1)S(1)} %get-tuple-element.31.q_ref, f32[4096,1024]{1,0:T(8,128)} %outer.3.rest_0_), custom_call_target="tpu_custom_call", output_to_operand_aliasing={{}: (2, {})} | custom-call | flops 150994944 | bytes 4718592 | tf_op jit(solution)/shard_map/outer/pallas_call | solution.py:261
  36.9 0.3 collective-permute-done.6
  37.2 1.7 %collective-permute-start.7 = (f32[4,1024]{1,0:T(4,128)S(1)}, f32[4,1024]{1,0:T(4,128)S(1)}, u32[]{:S(2)}, u32[]{:S(2)}) collective-permute-start(f32[4,1024]{1,0:T(4,128)S(1)} %slice.29), channel_id=1, source_target_pairs={{0,9},{1,8},{2,11},{3,10},{4,13},{5,12},{6,15},{7,14},{8,1},{9,0},... | collective-permute-start | bytes 49160 | tf_op jit(solution)/shard_map/ppermute | solution.py:285
  38.9 2.3 %outer.5 = f32[4096,1024]{1,0:T(8,128)} custom-call(bf16[64,4096]{1,0:T(8,128)(2,1)S(1)} %get-tuple-element.30.dlogit_ref, bf16[64,1024]{1,0:T(8,128)(2,1)S(1)} %get-tuple-element.31.q_ref, f32[4096,1024]{1,0:T(8,128)} %outer.4.rest_0_), custom_call_target="tpu_custom_call", output_to_operand_aliasing={{}: (2, {})} | custom-call | flops 134217728 | bytes 4194304 | tf_op jit(solution)/shard_map/outer/pallas_call | solution.py:261
  41.2 0.1 collective-permute-done.7
  41.3 0.6 %slice_add_fusion.2 = f32[4,1024]{1,0:T(4,128)} fusion(f32[4,1024]{1,0:T(4,128)S(1)} %collective-permute-done.7, f32[8,1024]{1,0:T(8,128)S(1)} %slice_add_fusion.1), kind=kLoop, calls=%fused_computation.2 | loop fusion | flops 4096 | bytes 49152 | tf_op jit(solution)/shard_map/add | solution.py:313
  (10 shorter events, 0.1 us)
Async XLA Ops:
  8.8 5.8 %collective-permute-start = (bf16[4,1024]{1,0:T(4,128)(2,1)S(1)}, bf16[4,1024]{1,0:T(4,128)(2,1)S(1)}, u32[]{:S(2)}, u32[]{:S(2)}) collective-permute-start(bf16[4,1024]{1,0:T(4,128)(2,1)S(1)} %get-tuple-element.20._.a_ref), channel_id=1, source_target_pairs={{0,9},{1,8},{2,11},{3,10},{4,13},{5,12},{6,15},{7,14},{8,1},{9,0},... | collective-permute-start | bytes 24584 | tf_op jit(solution)/shard_map/ppermute | solution.py:285
  14.5 4.1 %collective-permute-start.1 = (bf16[8,1024]{1,0:T(8,128)(2,1)S(1)}, bf16[8,1024]{1,0:T(8,128)(2,1)S(1)}, u32[]{:S(2)}, u32[]{:S(2)}) collective-permute-start(bf16[8,1024]{1,0:T(8,128)(2,1)S(1)} %join.3._.a_ref), channel_id=1, source_target_pairs={{0,5},{1,4},{2,7},{3,6},{4,1},{5,0},{6,3},{7,2},{8,13},{9,12},{10,... | collective-permute-start | bytes 49160 | tf_op jit(solution)/shard_map/ppermute | solution.py:285
  18.7 3.7 %collective-permute-start.2 = (bf16[16,1024]{1,0:T(8,128)(2,1)S(1)}, bf16[16,1024]{1,0:T(8,128)(2,1)S(1)}, u32[]{:S(2)}, u32[]{:S(2)}) collective-permute-start(bf16[16,1024]{1,0:T(8,128)(2,1)S(1)} %join.4._.a_ref), channel_id=1, source_target_pairs={{0,3},{1,2},{2,1},{3,0},{4,7},{5,6},{6,5},{7,4},{8,11},{9,10},{10,... | collective-permute-start | bytes 98312 | tf_op jit(solution)/shard_map/ppermute | solution.py:285
  22.4 1.3 %collective-permute-start.3 = (bf16[32,1024]{1,0:T(8,128)(2,1)S(1)}, bf16[32,1024]{1,0:T(8,128)(2,1)S(1)}, u32[]{:S(2)}, u32[]{:S(2)}) collective-permute-start(bf16[32,1024]{1,0:T(8,128)(2,1)S(1)} %join.5.qa_ref), channel_id=1, source_target_pairs={{0,1},{1,0},{2,3},{3,2},{4,5},{5,4},{6,7},{7,6},{8,9},{9,8},{10,11... | collective-permute-start | bytes 196616 | tf_op jit(solution)/shard_map/ppermute | solution.py:285
  27.4 1.4 %collective-permute-start.4 = (f32[32,1024]{1,0:T(8,128)S(1)}, f32[32,1024]{1,0:T(8,128)S(1)}, u32[]{:S(2)}, u32[]{:S(2)}) collective-permute-start(f32[32,1024]{1,0:T(8,128)S(1)} %get-tuple-element.29), channel_id=1, source_target_pairs={{0,1},{1,0},{2,3},{3,2},{4,5},{5,4},{6,7},{7,6},{8,9},{9,8},{10,11... | collective-permute-start | bytes 393224 | tf_op jit(solution)/shard_map/ppermute | solution.py:285
  28.8 4.9 %collective-permute-start.5 = (f32[16,1024]{1,0:T(8,128)S(1)}, f32[16,1024]{1,0:T(8,128)S(1)}, u32[]{:S(2)}, u32[]{:S(2)}) collective-permute-start(f32[16,1024]{1,0:T(8,128)S(1)} %slice.25), channel_id=1, source_target_pairs={{0,3},{1,2},{2,1},{3,0},{4,7},{5,6},{6,5},{7,4},{8,11},{9,10},{10,... | collective-permute-start | bytes 196616 | tf_op jit(solution)/shard_map/ppermute | solution.py:285
  33.8 3.4 %collective-permute-start.6 = (f32[8,1024]{1,0:T(8,128)S(1)}, f32[8,1024]{1,0:T(8,128)S(1)}, u32[]{:S(2)}, u32[]{:S(2)}) collective-permute-start(f32[8,1024]{1,0:T(8,128)S(1)} %slice.27), channel_id=1, source_target_pairs={{0,5},{1,4},{2,7},{3,6},{4,1},{5,0},{6,3},{7,2},{8,13},{9,12},{10,... | collective-permute-start | bytes 98312 | tf_op jit(solution)/shard_map/ppermute | solution.py:285
  37.2 4.1 %collective-permute-start.7 = (f32[4,1024]{1,0:T(4,128)S(1)}, f32[4,1024]{1,0:T(4,128)S(1)}, u32[]{:S(2)}, u32[]{:S(2)}) collective-permute-start(f32[4,1024]{1,0:T(4,128)S(1)} %slice.29), channel_id=1, source_target_pairs={{0,9},{1,8},{2,11},{3,10},{4,13},{5,12},{6,15},{7,14},{8,1},{9,0},... | collective-permute-start | bytes 49160 | tf_op jit(solution)/shard_map/ppermute | solution.py:285

commit v4 on v2

--- a/solution.py
+++ b/solution.py
@@ -11,6 +11,8 @@
 EPS = 1e-05
 F32 = jnp.float32
 BF16 = jnp.bfloat16
+FETCH = (0.0, 0.3125, 0.6875, 1.0)
+SHARES = (0.0, 0.46875, 0.75, 1.0)
 HBM = pltpu.MemorySpace.HBM
 NN = (((1,), (0,)), ((), ()))
 NT = (((1,), (1,)), ((), ()))
@@ -35,14 +37,14 @@
     return centered, lax.rsqrt(spread + EPS)
 
 
-def mark_targets(rel, target_ref):
-    asked, slots = rel.shape
+def mark_targets(rel, first, asked, target_ref):
+    slots = rel.shape[1]
     tiles = target_ref.shape[1] // 128
     entries, rows = 8 * slots, 8 * tiles
     sub = lax.broadcasted_iota(jnp.int32, (8, 1), 0)
     low_at = lax.broadcasted_iota(jnp.int32, (entries, 128), 1)
     row_at = lax.broadcasted_iota(jnp.int32, (entries, rows), 1)
-    for q in range(0, asked, 8):
+    for q in range(first, first + asked, 8):
         own = [rel[q : q + 8, s : s + 1] for s in range(slots)]
         low = jnp.concatenate([lax.bitwise_and(r, 127) for r in own], axis=0)
         row = jnp.concatenate([lax.shift_right_arithmetic(r, 7) * 8 + sub for r in own], axis=0)
@@ -83,13 +85,14 @@
     for k in range(asked // per):
         own_ref[k] = rel[k * per : (k + 1) * per, :]
     rel = jnp.concatenate([own_ref[lax.bitwise_xor(me, k)] for k in order], axis=0)
-    mark_targets(rel, target_ref)
     x_copy.wait()
     x = x_ref[...].reshape(count * length, width)
     for k, copy in enumerate(ups):
         copy.wait()
         cut = slice(k * up_step, (k + 1) * up_step)
         act_ref[:, cut] = jax.nn.gelu(dot(x, up_ref[:, cut], NN)).astype(BF16)
+        share = asked // len(ups)
+        mark_targets(rel, k * share, share, target_ref)
     kept = jnp.sum((ids_ref[...] != 0).astype(F32), axis=1, keepdims=True)
     place = lax.broadcasted_iota(jnp.int32, (length, 1), 0).astype(F32)
     down_copy.wait()
@@ -136,22 +139,35 @@
     )(*map(far, (states, ids, up_weight, down_weight, positives.T, counts.reshape(1, asked))))
 
 
-def fetch_kernel(first, src_hbm, _, out_ref, mark_ref, sems):
-    rows = out_ref.shape[0]
-    copy = pltpu.make_async_copy(src_hbm.at[pl.ds(first, rows)], out_ref, sems.at[0])
-    copy.start()
+def fetch_kernel(first, sub, src_hbm, _, out_ref, flip_ref, mark_ref, sems):
+    copies = []
+    for k in range(out_ref.shape[0] // sub):
+        copies.append(
+            pltpu.make_async_copy(
+                src_hbm.at[pl.ds(first + k * sub, sub)], out_ref.at[pl.ds(k * sub, sub)], sems.at[k]
+            )
+        )
+        copies[-1].start()
     mark_ref[...] = jnp.zeros_like(mark_ref)
-    copy.wait()
+    for k, copy in enumerate(copies):
+        copy.wait()
+        cut = slice(k * sub, (k + 1) * sub)
+        flip_ref[:, cut] = out_ref[cut, :].T
 
 
 def fetch(values, first, rows, behind):
     width = values.shape[1]
-    return pl.pallas_call(
-        functools.partial(fetch_kernel, first),
-        out_shape=(pltpu.VMEM((rows, width), values.dtype), pltpu.VMEM((8, 128), F32)),
+    sub = min(256, rows)
+    return pl.pallas_call(
+        functools.partial(fetch_kernel, first, sub),
+        out_shape=(
+            pltpu.VMEM((rows, width), values.dtype),
+            pltpu.VMEM((width, rows), values.dtype),
+            pltpu.VMEM((8, 128), F32),
+        ),
         in_specs=[pl.BlockSpec(memory_space=HBM), *held(1)],
-        out_specs=held(2),
-        scratch_shapes=[pltpu.SemaphoreType.DMA((1,))],
+        out_specs=held(3),
+        scratch_shapes=[pltpu.SemaphoreType.DMA((rows // sub,))],
         compiler_params=pltpu.CompilerParams(vmem_limit_bytes=4 << 20),
         cost_estimate=pl.CostEstimate(flops=0, transcendentals=0, bytes_accessed=2 * rows * width),
         name="fetch",
@@ -179,16 +195,18 @@
 
 
 def score_kernel(parts, qa_ref, qb_ref, target_ref, *refs):
-    c_refs, (q_ref, keep_ref, send_ref, dlogit_ref) = refs[:parts], refs[parts:]
+    c_refs, flip_refs = refs[:parts], refs[parts : 2 * parts]
+    q_ref, keep_ref, send_ref, dlogit_ref = refs[2 * parts :]
     half = qa_ref.shape[0]
     q_ref[:half, :] = qa_ref[...]
     q_ref[half:, :] = qb_ref[...]
     queries = q_ref[...]
     first = 0
-    for c_ref in c_refs:
-        step = min(512, c_ref.shape[0])
-        for k in range(c_ref.shape[0] // step):
-            logits = dot(c_ref[k * step : (k + 1) * step, :], queries, NT).T
+    for flip_ref in flip_refs:
+        columns = flip_ref.shape[1]
+        for k in range(0, columns, 512):
+            step = min(512, columns - k)
+            logits = dot(queries, flip_ref[:, k : k + step], NN)
             cut = slice(first, first + step)
             dlogit_ref[:, cut] = (jax.nn.sigmoid(logits) * (1.0 / MB) - target_ref[:, cut]).astype(BF16)
             first += step
@@ -201,7 +219,7 @@
     send_ref[...] = grad[half:]
 
 
-def score(centroids, qa, qb, target):
+def score(centroids, flipped, qa, qb, target):
     half, width = qa.shape
     count, c_dev = target.shape
     return pl.pallas_call(
@@ -212,14 +230,14 @@
             pltpu.VMEM((half, width), F32),
             pltpu.VMEM((count, c_dev), BF16),
         ),
-        in_specs=held(3 + len(centroids)),
+        in_specs=held(3 + 2 * len(centroids)),
         out_specs=held(4),
         compiler_params=pltpu.CompilerParams(vmem_limit_bytes=32 << 20),
         cost_estimate=pl.CostEstimate(
             flops=4 * count * c_dev * width, transcendentals=count * c_dev, bytes_accessed=2 * c_dev * width
         ),
         name="score",
-    )(qa, qb, target, *centroids)
+    )(qa, qb, target, *centroids, *flipped)
 
 
 def outer_kernel(first, rows, sub, dlogit_ref, q_ref, *rest):
@@ -258,31 +276,35 @@
 
 def shards(n, hidden_states, token_ids, up_weight, down_weight, centroids, positives, counts):
     bits = n.bit_length() - 1
-    order = [int(format(k, f"0{bits}b")[::-1], 2) for k in range(n)]
+    pairs = [1] + [1 << k | 1 for k in range(1, bits)]
+    order = [0]
+    for pair in reversed(pairs):
+        order += [k ^ pair for k in order]
     c_dev = centroids.shape[0]
 
-    def swap(values, bit):
-        return lax.ppermute(values, "cluster", [(i, i ^ bit) for i in range(n)])
+    def swap(values, pair):
+        return lax.ppermute(values, "cluster", [(i, i ^ pair) for i in range(n)])
 
     queries, target = encode(
         hidden_states, token_ids, up_weight, down_weight, positives, counts, order, c_dev
     )
-    part = c_dev // 2
-    fetched = []
-    for k in range(bits):
-        got = swap(queries, 1 << (bits - 1 - k))
+    cuts = [round(c_dev // 256 * share) * 256 for share in FETCH]
+    fetched, flipped = [], []
+    for k, pair in enumerate(reversed(pairs)):
+        got = swap(queries, pair)
         marks = []
-        if k in (1, 2):
-            centroid_part, mark = fetch(centroids, (k - 1) * part, part, queries)
-            fetched.append(centroid_part)
+        if k < len(cuts) - 1 and cuts[k + 1] > cuts[k]:
+            part, flip, mark = fetch(centroids, cuts[k], cuts[k + 1] - cuts[k], queries)
+            fetched.append(part)
+            flipped.append(flip)
             marks.append(mark)
         if k < bits - 1:
             queries = join(queries, got, *marks)
-    queries, keep, send, dlogit = score(fetched, queries, got, target)
-    ends = [round(c_dev // 128 * share) * 128 for share in (0.125, 0.5, 0.78125, 1.0)]
+    queries, keep, send, dlogit = score(fetched, flipped, queries, got, target)
+    ends = [round(c_dev // 128 * share) * 128 for share in SHARES]
     first, grown = 0, []
-    for k in range(bits):
-        got = swap(send, 1 << k)
+    for k, pair in enumerate(pairs):
+        got = swap(send, pair)
         if k < len(ends) and ends[k] > first:
             grown = [outer(dlogit, queries, first, ends[k] - first, grown)]
             first = ends[k]

time: 44.5 us -> 41.4 us (0.930)
  starting transfers between devices: 13.6 us -> 10.6 us
    ppermute x8, starting transfers between devices: 13.6 us -> 10.6 us  [swap(): return lax.ppermute(values, 'cluster', [(i, i ^ pair) for i in range(n)])]
    pallas_call x2 -> x3, Pallas kernels: 4.39 us -> 6.34 us  [fetch(): pl.pallas_call(functools.partial(fetch_kernel, first, sub), out_shape=(pl...]
    pallas_call x4 -> x3, Pallas kernels: 9.25 us -> 8.32 us  [outer(): pl.pallas_call(functools.partial(outer_kernel, first, rows, sub), out_sha...]
    pallas_call x1, Pallas kernels: 3.74 us -> 3.03 us  [score(): pl.pallas_call(functools.partial(score_kernel, len(centroids)), out_shape...]
    pallas_call x1, Pallas kernels: 8.8 us -> 8.21 us  [encode(): pl.pallas_call(functools.partial(encode_kernel, order, c_dev, up_step), o...]
  transfers between devices with their start and end apart: 8 -> 8, of which waited for: 3 -> 4; matrix products, arithmetic and copies ran while one was open for 0% -> 0% of each run, Pallas kernels for 31% -> 36%
where the time goes in v4:
time: 41.4 us; the launch traced here: 41.2 us
  Pallas kernels  25.9 us (63%)
  starting transfers between devices  10.6 us (26%)
  waiting for transfers between devices  3.23 us (8%)
  between operations  0.77 us (2%)
  other arithmetic  0.65 us (2%)
    ppermute x8, starting transfers between devices, swap(): return lax.ppermute(values, 'cluster', [(i, i ^ pair) for i in range(n)])  10.6 us
    pallas_call x3, Pallas kernels, outer(): pl.pallas_call(functools.partial(outer_kernel, first, rows, sub), out_sha...  8.32 us
    pallas_call x1, Pallas kernels, encode(): pl.pallas_call(functools.partial(encode_kernel, order, c_dev, up_step), o...  8.21 us
    pallas_call x3, Pallas kernels, fetch(): pl.pallas_call(functools.partial(fetch_kernel, first, sub), out_shape=(pl...  6.34 us
    ppermute x8, waiting for transfers between devices, swap(): return lax.ppermute(values, 'cluster', [(i, i ^ pair) for i in range(n)])  3.23 us
    pallas_call x1, Pallas kernels, score(): pl.pallas_call(functools.partial(score_kernel, len(centroids)), out_shape...  3.03 us
  transfers between devices with their start and end apart: 8, of which 4 were waited for; matrix products, arithmetic and copies ran while one was open for 0% of the time, Pallas kernels for 36%

profile of v4, /device:TPU:0, one launch (start us, length us, event | category | flops | bytes accessed | tf_op | source)
XLA Modules:
  0.0 41.2 jit_solution(11479713457131618194)
XLA Ops:
  0.6 8.2 %encode.1 = (bf16[4,1024]{1,0:T(4,128)(2,1)S(1)}, f32[64,4096]{1,0:T(8,128)S(1)}) custom-call(bf16[4,128,1024]{2,1,0:T(8,128)(2,1)} %x_hbm.1, s32[4,128]{1,0:T(4,128)} %ids_hbm.1, bf16[1024,2048]{1,0:T(8,128)(2,1)} %up_hbm.1, bf16[2048,1024]{1,0:T(8,128)(2,1)} %down_hbm.1, s32[16,64]{1,0:T(8,128)} %bitcast.2, s32[1,64]{1,0:T(1,128)} %bitcast.3), custom_call_target="tpu_custom_call" | custom-call | flops 4294967296 | bytes 9437184 | tf_op jit(solution)/shard_map/encode/pallas_call | solution.py:116
  8.8 3.5 %collective-permute-start = (bf16[4,1024]{1,0:T(4,128)(2,1)S(1)}, bf16[4,1024]{1,0:T(4,128)(2,1)S(1)}, u32[]{:S(2)}, u32[]{:S(2)}) collective-permute-start(bf16[4,1024]{1,0:T(4,128)(2,1)S(1)} %get-tuple-element.23._.a_ref), channel_id=1, source_target_pairs={{0,9},{1,8},{2,11},{3,10},{4,13},{5,12},{6,15},{7,14},{8,1},{9,0},... | collective-permute-start | bytes 24584 | tf_op jit(solution)/shard_map/ppermute | solution.py:286
  12.4 2.0 %fetch.3 = (bf16[1280,1024]{1,0:T(8,128)(2,1)S(1)}, bf16[1024,1280]{1,0:T(8,128)(2,1)S(1)}, f32[8,128]{1,0:T(8,128)S(1)}) custom-call(bf16[4096,1024]{1,0:T(8,128)(2,1)} %src_hbm.5, bf16[4,1024]{1,0:T(4,128)(2,1)S(1)} %get-tuple-element.23._.a_ref), custom_call_target="tpu_custom_call" | custom-call | bytes 2621440 | tf_op jit(solution)/shard_map/fetch/pallas_call | solution.py:161
  14.4 0.0 collective-permute-done.b_ref
  14.5 1.9 %collective-permute-start.1 = (bf16[8,1024]{1,0:T(8,128)(2,1)S(1)}, bf16[8,1024]{1,0:T(8,128)(2,1)S(1)}, u32[]{:S(2)}, u32[]{:S(2)}) collective-permute-start(bf16[8,1024]{1,0:T(8,128)(2,1)S(1)} %join.3._.a_ref), channel_id=1, source_target_pairs={{0,5},{1,4},{2,7},{3,6},{4,1},{5,0},{6,3},{7,2},{8,13},{9,12},{10,... | collective-permute-start | bytes 49160 | tf_op jit(solution)/shard_map/ppermute | solution.py:286
  16.4 2.2 %fetch.4 = (bf16[1536,1024]{1,0:T(8,128)(2,1)S(1)}, bf16[1024,1536]{1,0:T(8,128)(2,1)S(1)}, f32[8,128]{1,0:T(8,128)S(1)}) custom-call(bf16[4096,1024]{1,0:T(8,128)(2,1)} %src_hbm.5, bf16[8,1024]{1,0:T(8,128)(2,1)S(1)} %join.3._.a_ref), custom_call_target="tpu_custom_call" | custom-call | bytes 3145728 | tf_op jit(solution)/shard_map/fetch/pallas_call | solution.py:161
  18.6 0.0 collective-permute-done.1.b_ref
  18.7 1.0 %collective-permute-start.2 = (bf16[16,1024]{1,0:T(8,128)(2,1)S(1)}, bf16[16,1024]{1,0:T(8,128)(2,1)S(1)}, u32[]{:S(2)}, u32[]{:S(2)}) collective-permute-start(bf16[16,1024]{1,0:T(8,128)(2,1)S(1)} %join.4._.a_ref), channel_id=1, source_target_pairs={{0,3},{1,2},{2,1},{3,0},{4,7},{5,6},{6,5},{7,4},{8,11},{9,10},{10,... | collective-permute-start | bytes 98312 | tf_op jit(solution)/shard_map/ppermute | solution.py:286
  19.7 2.0 %fetch.5 = (bf16[1280,1024]{1,0:T(8,128)(2,1)S(1)}, bf16[1024,1280]{1,0:T(8,128)(2,1)S(1)}, f32[8,128]{1,0:T(8,128)S(1)}) custom-call(bf16[4096,1024]{1,0:T(8,128)(2,1)} %src_hbm.5, bf16[16,1024]{1,0:T(8,128)(2,1)S(1)} %join.4._.a_ref), custom_call_target="tpu_custom_call" | custom-call | bytes 2621440 | tf_op jit(solution)/shard_map/fetch/pallas_call | solution.py:161
  21.7 0.6 %collective-permute-done.2.b_ref = bf16[16,1024]{1,0:T(8,128)(2,1)S(1)} collective-permute-done((bf16[16,1024]{1,0:T(8,128)(2,1)S(1)}, bf16[16,1024]{1,0:T(8,128)(2,1)S(1)}, u32[]{:S(2)}, u32[]{:S(2)}) %collective-permute-start.2) | collective-permute-done | bytes 32800 | tf_op jit(solution)/shard_map/ppermute | solution.py:286
  22.3 0.2 collective-permute-start.3
  22.5 1.1 %collective-permute-done.3.qb_ref = bf16[32,1024]{1,0:T(8,128)(2,1)S(1)} collective-permute-done((bf16[32,1024]{1,0:T(8,128)(2,1)S(1)}, bf16[32,1024]{1,0:T(8,128)(2,1)S(1)}, u32[]{:S(2)}, u32[]{:S(2)}) %collective-permute-start.3) | collective-permute-done | bytes 65568 | tf_op jit(solution)/shard_map/ppermute | solution.py:286
  23.6 3.0 %score.1 = (bf16[64,1024]{1,0:T(8,128)(2,1)S(1)}, f32[32,1024]{1,0:T(8,128)S(1)}, f32[32,1024]{1,0:T(8,128)S(1)}, bf16[64,4096]{1,0:T(8,128)(2,1)S(1)}) custom-call(bf16[32,1024]{1,0:T(8,128)(2,1)S(1)} %join.5.qa_ref, bf16[32,1024]{1,0:T(8,128)(2,1)S(1)} %collective-permute-done.3.qb_ref, f32[64,4096]{1,0:T(8,128)S(1)} %get-tuple-element.27.target_ref, ...), custom_call_target="tpu_custom_call" | custom-call | flops 1073741824 | bytes 8388608 | tf_op jit(solution)/shard_map/score/pallas_call | solution.py:225
  26.6 0.2 collective-permute-start.4
  26.9 1.2 %collective-permute-done.4 = f32[32,1024]{1,0:T(8,128)S(1)} collective-permute-done((f32[32,1024]{1,0:T(8,128)S(1)}, f32[32,1024]{1,0:T(8,128)S(1)}, u32[]{:S(2)}, u32[]{:S(2)}) %collective-permute-start.4) | collective-permute-done | bytes 131104 | tf_op jit(solution)/shard_map/ppermute | solution.py:286
  28.1 1.4 %collective-permute-start.5 = (f32[16,1024]{1,0:T(8,128)S(1)}, f32[16,1024]{1,0:T(8,128)S(1)}, u32[]{:S(2)}, u32[]{:S(2)}) collective-permute-start(f32[16,1024]{1,0:T(8,128)S(1)} %slice.25), channel_id=1, source_target_pairs={{0,3},{1,2},{2,1},{3,0},{4,7},{5,6},{6,5},{7,4},{8,11},{9,10},{10,... | collective-permute-start | bytes 196616 | tf_op jit(solution)/shard_map/ppermute | solution.py:286
  29.5 3.5 %outer.3.rest_0_ = f32[4096,1024]{1,0:T(8,128)} custom-call(bf16[64,4096]{1,0:T(8,128)(2,1)S(1)} %get-tuple-element.36.dlogit_ref, bf16[64,1024]{1,0:T(8,128)(2,1)S(1)} %get-tuple-element.37.q_ref), custom_call_target="tpu_custom_call" | custom-call | flops 251658240 | bytes 7864320 | tf_op jit(solution)/shard_map/outer/pallas_call | solution.py:262
  33.0 0.0 collective-permute-done.5
  33.0 0.6 %collective-permute-start.6 = (f32[8,1024]{1,0:T(8,128)S(1)}, f32[8,1024]{1,0:T(8,128)S(1)}, u32[]{:S(2)}, u32[]{:S(2)}) collective-permute-start(f32[8,1024]{1,0:T(8,128)S(1)} %slice.27), channel_id=1, source_target_pairs={{0,5},{1,4},{2,7},{3,6},{4,1},{5,0},{6,3},{7,2},{8,13},{9,12},{10,... | collective-permute-start | bytes 98312 | tf_op jit(solution)/shard_map/ppermute | solution.py:286
  33.6 2.5 %outer.4.rest_0_ = f32[4096,1024]{1,0:T(8,128)} custom-call(bf16[64,4096]{1,0:T(8,128)(2,1)S(1)} %get-tuple-element.36.dlogit_ref, bf16[64,1024]{1,0:T(8,128)(2,1)S(1)} %get-tuple-element.37.q_ref, f32[4096,1024]{1,0:T(8,128)} %outer.3.rest_0_), custom_call_target="tpu_custom_call", output_to_operand_aliasing={{}: (2, {})} | custom-call | flops 150994944 | bytes 4718592 | tf_op jit(solution)/shard_map/outer/pallas_call | solution.py:262
  36.1 0.3 collective-permute-done.6
  36.5 1.8 %collective-permute-start.7 = (f32[4,1024]{1,0:T(4,128)S(1)}, f32[4,1024]{1,0:T(4,128)S(1)}, u32[]{:S(2)}, u32[]{:S(2)}) collective-permute-start(f32[4,1024]{1,0:T(4,128)S(1)} %slice.29), channel_id=1, source_target_pairs={{0,9},{1,8},{2,11},{3,10},{4,13},{5,12},{6,15},{7,14},{8,1},{9,0},... | collective-permute-start | bytes 49160 | tf_op jit(solution)/shard_map/ppermute | solution.py:286
  38.3 2.3 %outer.5 = f32[4096,1024]{1,0:T(8,128)} custom-call(bf16[64,4096]{1,0:T(8,128)(2,1)S(1)} %get-tuple-element.36.dlogit_ref, bf16[64,1024]{1,0:T(8,128)(2,1)S(1)} %get-tuple-element.37.q_ref, f32[4096,1024]{1,0:T(8,128)} %outer.4.rest_0_), custom_call_target="tpu_custom_call", output_to_operand_aliasing={{}: (2, {})} | custom-call | flops 134217728 | bytes 4194304 | tf_op jit(solution)/shard_map/outer/pallas_call | solution.py:262
  40.6 0.6 %slice_add_fusion.2 = f32[4,1024]{1,0:T(4,128)} fusion(f32[4,1024]{1,0:T(4,128)S(1)} %collective-permute-done.7, f32[8,1024]{1,0:T(8,128)S(1)} %slice_add_fusion.1), kind=kLoop, calls=%fused_computation.2 | loop fusion | flops 4096 | bytes 49152 | tf_op jit(solution)/shard_map/add | solution.py:312
  (10 shorter events, 0.1 us)
Async XLA Ops:
  8.8 5.6 %collective-permute-start = (bf16[4,1024]{1,0:T(4,128)(2,1)S(1)}, bf16[4,1024]{1,0:T(4,128)(2,1)S(1)}, u32[]{:S(2)}, u32[]{:S(2)}) collective-permute-start(bf16[4,1024]{1,0:T(4,128)(2,1)S(1)} %get-tuple-element.23._.a_ref), channel_id=1, source_target_pairs={{0,9},{1,8},{2,11},{3,10},{4,13},{5,12},{6,15},{7,14},{8,1},{9,0},... | collective-permute-start | bytes 24584 | tf_op jit(solution)/shard_map/ppermute | solution.py:286
  14.5 4.2 %collective-permute-start.1 = (bf16[8,1024]{1,0:T(8,128)(2,1)S(1)}, bf16[8,1024]{1,0:T(8,128)(2,1)S(1)}, u32[]{:S(2)}, u32[]{:S(2)}) collective-permute-start(bf16[8,1024]{1,0:T(8,128)(2,1)S(1)} %join.3._.a_ref), channel_id=1, source_target_pairs={{0,5},{1,4},{2,7},{3,6},{4,1},{5,0},{6,3},{7,2},{8,13},{9,12},{10,... | collective-permute-start | bytes 49160 | tf_op jit(solution)/shard_map/ppermute | solution.py:286
  18.7 3.7 %collective-permute-start.2 = (bf16[16,1024]{1,0:T(8,128)(2,1)S(1)}, bf16[16,1024]{1,0:T(8,128)(2,1)S(1)}, u32[]{:S(2)}, u32[]{:S(2)}) collective-permute-start(bf16[16,1024]{1,0:T(8,128)(2,1)S(1)} %join.4._.a_ref), channel_id=1, source_target_pairs={{0,3},{1,2},{2,1},{3,0},{4,7},{5,6},{6,5},{7,4},{8,11},{9,10},{10,... | collective-permute-start | bytes 98312 | tf_op jit(solution)/shard_map/ppermute | solution.py:286
  22.3 1.3 %collective-permute-start.3 = (bf16[32,1024]{1,0:T(8,128)(2,1)S(1)}, bf16[32,1024]{1,0:T(8,128)(2,1)S(1)}, u32[]{:S(2)}, u32[]{:S(2)}) collective-permute-start(bf16[32,1024]{1,0:T(8,128)(2,1)S(1)} %join.5.qa_ref), channel_id=1, source_target_pairs={{0,1},{1,0},{2,3},{3,2},{4,5},{5,4},{6,7},{7,6},{8,9},{9,8},{10,11... | collective-permute-start | bytes 196616 | tf_op jit(solution)/shard_map/ppermute | solution.py:286
  26.6 1.4 %collective-permute-start.4 = (f32[32,1024]{1,0:T(8,128)S(1)}, f32[32,1024]{1,0:T(8,128)S(1)}, u32[]{:S(2)}, u32[]{:S(2)}) collective-permute-start(f32[32,1024]{1,0:T(8,128)S(1)} %get-tuple-element.35), channel_id=1, source_target_pairs={{0,1},{1,0},{2,3},{3,2},{4,5},{5,4},{6,7},{7,6},{8,9},{9,8},{10,11... | collective-permute-start | bytes 393224 | tf_op jit(solution)/shard_map/ppermute | solution.py:286
  28.1 4.9 %collective-permute-start.5 = (f32[16,1024]{1,0:T(8,128)S(1)}, f32[16,1024]{1,0:T(8,128)S(1)}, u32[]{:S(2)}, u32[]{:S(2)}) collective-permute-start(f32[16,1024]{1,0:T(8,128)S(1)} %slice.25), channel_id=1, source_target_pairs={{0,3},{1,2},{2,1},{3,0},{4,7},{5,6},{6,5},{7,4},{8,11},{9,10},{10,... | collective-permute-start | bytes 196616 | tf_op jit(solution)/shard_map/ppermute | solution.py:286
  33.0 3.4 %collective-permute-start.6 = (f32[8,1024]{1,0:T(8,128)S(1)}, f32[8,1024]{1,0:T(8,128)S(1)}, u32[]{:S(2)}, u32[]{:S(2)}) collective-permute-start(f32[8,1024]{1,0:T(8,128)S(1)} %slice.27), channel_id=1, source_target_pairs={{0,5},{1,4},{2,7},{3,6},{4,1},{5,0},{6,3},{7,2},{8,13},{9,12},{10,... | collective-permute-start | bytes 98312 | tf_op jit(solution)/shard_map/ppermute | solution.py:286
  36.5 4.1 %collective-permute-start.7 = (f32[4,1024]{1,0:T(4,128)S(1)}, f32[4,1024]{1,0:T(4,128)S(1)}, u32[]{:S(2)}, u32[]{:S(2)}) collective-permute-start(f32[4,1024]{1,0:T(4,128)S(1)} %slice.29), channel_id=1, source_target_pairs={{0,9},{1,8},{2,11},{3,10},{4,13},{5,12},{6,15},{7,14},{8,1},{9,0},... | collective-permute-start | bytes 49160 | tf_op jit(solution)/shard_map/ppermute | solution.py:286

commit v5 on v4

--- a/solution.py
+++ b/solution.py
@@ -12,7 +12,8 @@
 F32 = jnp.float32
 BF16 = jnp.bfloat16
 FETCH = (0.0, 0.3125, 0.6875, 1.0)
-SHARES = (0.0, 0.46875, 0.75, 1.0)
+FIRST = 0.25
+SHARES = (0.0, 0.5625, 0.78125, 1.0)
 HBM = pltpu.MemorySpace.HBM
 NN = (((1,), (0,)), ((), ()))
 NT = (((1,), (1,)), ((), ()))
@@ -139,39 +140,25 @@
     )(*map(far, (states, ids, up_weight, down_weight, positives.T, counts.reshape(1, asked))))
 
 
-def fetch_kernel(first, sub, src_hbm, _, out_ref, flip_ref, mark_ref, sems):
-    copies = []
-    for k in range(out_ref.shape[0] // sub):
-        copies.append(
-            pltpu.make_async_copy(
-                src_hbm.at[pl.ds(first + k * sub, sub)], out_ref.at[pl.ds(k * sub, sub)], sems.at[k]
-            )
-        )
-        copies[-1].start()
+def flip_kernel(first, src_ref, _, flip_ref, mark_ref):
     mark_ref[...] = jnp.zeros_like(mark_ref)
-    for k, copy in enumerate(copies):
-        copy.wait()
-        cut = slice(k * sub, (k + 1) * sub)
-        flip_ref[:, cut] = out_ref[cut, :].T
-
-
-def fetch(values, first, rows, behind):
+    rows = flip_ref.shape[1]
+    sub = min(256, rows)
+    for k in range(0, rows, sub):
+        flip_ref[:, k : k + sub] = src_ref[first + k : first + k + sub, :].T
+
+
+def flip(values, first, rows, behind):
     width = values.shape[1]
-    sub = min(256, rows)
-    return pl.pallas_call(
-        functools.partial(fetch_kernel, first, sub),
-        out_shape=(
-            pltpu.VMEM((rows, width), values.dtype),
-            pltpu.VMEM((width, rows), values.dtype),
-            pltpu.VMEM((8, 128), F32),
-        ),
-        in_specs=[pl.BlockSpec(memory_space=HBM), *held(1)],
-        out_specs=held(3),
-        scratch_shapes=[pltpu.SemaphoreType.DMA((rows // sub,))],
+    return pl.pallas_call(
+        functools.partial(flip_kernel, first),
+        out_shape=(pltpu.VMEM((width, rows), values.dtype), pltpu.VMEM((8, 128), F32)),
+        in_specs=held(2),
+        out_specs=held(2),
         compiler_params=pltpu.CompilerParams(vmem_limit_bytes=4 << 20),
         cost_estimate=pl.CostEstimate(flops=0, transcendentals=0, bytes_accessed=2 * rows * width),
-        name="fetch",
-    )(far(values), behind)
+        name="flip",
+    )(values, behind)
 
 
 def join_kernel(a_ref, b_ref, *rest):
@@ -194,9 +181,20 @@
     )(a, b, *behind)
 
 
-def score_kernel(parts, qa_ref, qb_ref, target_ref, *refs):
-    c_refs, flip_refs = refs[:parts], refs[parts : 2 * parts]
-    q_ref, keep_ref, send_ref, dlogit_ref = refs[2 * parts :]
+def outer_copies(first, rows, dlogit_ref, queries, out_hbm, held_ref, sems):
+    copies = []
+    for k in range(rows // 128):
+        cut = slice(k * 128, (k + 1) * 128)
+        held_ref[cut, :] = dot(dlogit_ref[:, first + k * 128 : first + (k + 1) * 128], queries, TN)
+        copies.append(
+            pltpu.make_async_copy(held_ref.at[cut], out_hbm.at[pl.ds(first + k * 128, 128)], sems.at[k])
+        )
+        copies[-1].start()
+    return copies
+
+
+def score_kernel(parts, qa_ref, qb_ref, target_ref, c_ref, *refs):
+    flip_refs, (q_ref, keep_ref, send_ref, dlogit_ref, out_hbm, held_ref, sems) = refs[:parts], refs[parts:]
     half = qa_ref.shape[0]
     q_ref[:half, :] = qa_ref[...]
     q_ref[half:, :] = qb_ref[...]
@@ -210,68 +208,58 @@
             cut = slice(first, first + step)
             dlogit_ref[:, cut] = (jax.nn.sigmoid(logits) * (1.0 / MB) - target_ref[:, cut]).astype(BF16)
             first += step
-    first, grad = 0, 0.0
-    for c_ref in c_refs:
-        rows = c_ref.shape[0]
-        grad += dot(dlogit_ref[:, first : first + rows], c_ref[...], NN)
-        first += rows
+    copies = outer_copies(0, held_ref.shape[0], dlogit_ref, queries, out_hbm, held_ref, sems)
+    grad = dot(dlogit_ref[...], c_ref[...], NN)
     keep_ref[...] = grad[:half]
     send_ref[...] = grad[half:]
-
-
-def score(centroids, flipped, qa, qb, target):
+    for copy in copies:
+        copy.wait()
+
+
+def score(centroids, flipped, qa, qb, target, rows):
     half, width = qa.shape
     count, c_dev = target.shape
     return pl.pallas_call(
-        functools.partial(score_kernel, len(centroids)),
+        functools.partial(score_kernel, len(flipped)),
         out_shape=(
             pltpu.VMEM((count, width), BF16),
             pltpu.VMEM((half, width), F32),
             pltpu.VMEM((half, width), F32),
             pltpu.VMEM((count, c_dev), BF16),
+            jax.ShapeDtypeStruct((c_dev, width), F32),
         ),
-        in_specs=held(3 + 2 * len(centroids)),
-        out_specs=held(4),
+        in_specs=held(4 + len(flipped)),
+        out_specs=(*held(4), pl.BlockSpec(memory_space=HBM)),
+        scratch_shapes=[pltpu.VMEM((rows, width), F32), pltpu.SemaphoreType.DMA((rows // 128,))],
         compiler_params=pltpu.CompilerParams(vmem_limit_bytes=32 << 20),
         cost_estimate=pl.CostEstimate(
             flops=4 * count * c_dev * width, transcendentals=count * c_dev, bytes_accessed=2 * c_dev * width
         ),
         name="score",
-    )(qa, qb, target, *centroids, *flipped)
-
-
-def outer_kernel(first, rows, sub, dlogit_ref, q_ref, *rest):
-    out_hbm, held_ref, sems = rest[-3:]
-    queries = q_ref[...]
-    copies = []
-    for k in range(rows // sub):
-        cut = slice(k * sub, (k + 1) * sub)
-        held_ref[cut, :] = dot(dlogit_ref[:, first + k * sub : first + (k + 1) * sub], queries, TN)
-        copies.append(
-            pltpu.make_async_copy(held_ref.at[cut], out_hbm.at[pl.ds(first + k * sub, sub)], sems.at[k])
-        )
-        copies[-1].start()
-    for copy in copies:
+    )(qa, qb, target, centroids, *flipped)
+
+
+def outer_kernel(first, rows, dlogit_ref, q_ref, _, out_hbm, held_ref, sems):
+    for copy in outer_copies(first, rows, dlogit_ref, q_ref[...], out_hbm, held_ref, sems):
         copy.wait()
 
 
 def outer(dlogit, queries, first, rows, grown):
     count, c_dev = dlogit.shape
     width = queries.shape[1]
-    sub = min(128, rows)
-    return pl.pallas_call(
-        functools.partial(outer_kernel, first, rows, sub),
+    return pl.pallas_call(
+        functools.partial(outer_kernel, first, rows),
         out_shape=jax.ShapeDtypeStruct((c_dev, width), F32),
-        in_specs=[*held(2)] + [pl.BlockSpec(memory_space=HBM)] * len(grown),
+        in_specs=[*held(2), pl.BlockSpec(memory_space=HBM)],
         out_specs=pl.BlockSpec(memory_space=HBM),
-        scratch_shapes=[pltpu.VMEM((rows, width), F32), pltpu.SemaphoreType.DMA((rows // sub,))],
-        input_output_aliases={2: 0} if grown else {},
+        scratch_shapes=[pltpu.VMEM((rows, width), F32), pltpu.SemaphoreType.DMA((rows // 128,))],
+        input_output_aliases={2: 0},
         compiler_params=pltpu.CompilerParams(vmem_limit_bytes=16 << 20),
         cost_estimate=pl.CostEstimate(
             flops=2 * count * rows * width, transcendentals=0, bytes_accessed=4 * rows * width
         ),
         name="outer",
-    )(dlogit, queries, *grown)
+    )(dlogit, queries, grown)
 
 
 def shards(n, hidden_states, token_ids, up_weight, down_weight, centroids, positives, counts):
@@ -289,30 +277,29 @@
         hidden_states, token_ids, up_weight, down_weight, positives, counts, order, c_dev
     )
     cuts = [round(c_dev // 256 * share) * 256 for share in FETCH]
-    fetched, flipped = [], []
+    flipped = []
     for k, pair in enumerate(reversed(pairs)):
         got = swap(queries, pair)
         marks = []
         if k < len(cuts) - 1 and cuts[k + 1] > cuts[k]:
-            part, flip, mark = fetch(centroids, cuts[k], cuts[k + 1] - cuts[k], queries)
-            fetched.append(part)
-            flipped.append(flip)
+            part, mark = flip(centroids, cuts[k], cuts[k + 1] - cuts[k], queries)
+            flipped.append(part)
             marks.append(mark)
         if k < bits - 1:
             queries = join(queries, got, *marks)
-    queries, keep, send, dlogit = score(fetched, flipped, queries, got, target)
     ends = [round(c_dev // 128 * share) * 128 for share in SHARES]
-    first, grown = 0, []
+    first = max(128, round(c_dev // 128 * FIRST) * 128)
+    queries, keep, send, dlogit, grown = score(centroids, flipped, queries, got, target, first)
     for k, pair in enumerate(pairs):
         got = swap(send, pair)
         if k < len(ends) and ends[k] > first:
-            grown = [outer(dlogit, queries, first, ends[k] - first, grown)]
+            grown = outer(dlogit, queries, first, ends[k] - first, grown)
             first = ends[k]
-            got, grown[0] = lax.optimization_barrier((got, grown[0]))
+            got, grown = lax.optimization_barrier((got, grown))
         total = keep + got
         half = total.shape[0] // 2
         keep, send = total[:half], total[half:]
-    return (total, grown[0])
+    return (total, grown)
 
 
 def solution(mesh):

time: 41.4 us -> 40.9 us (0.988)
  Pallas kernels: 25.9 us -> 21.4 us
  starting transfers between devices: 10.6 us -> 13.9 us
  waiting for transfers between devices: 3.23 us -> 4.04 us
    pallas_call x7, Pallas kernels: 17.7 us -> 13 us  [the longest x3 6.95 us: outer(): pl.pallas_call(functools.partial(outer_kernel, first, rows), out_shape=ja...]
    ppermute x8, starting transfers between devices: 10.6 us -> 13.9 us  [swap(): return lax.ppermute(values, 'cluster', [(i, i ^ pair) for i in range(n)])]
    ppermute x8, waiting for transfers between devices: 3.23 us -> 4.04 us  [swap(): return lax.ppermute(values, 'cluster', [(i, i ^ pair) for i in range(n)])]
  transfers between devices with their start and end apart: 8 -> 8, of which waited for: 4 -> 5; matrix products, arithmetic and copies ran while one was open for 0% -> 0% of each run, Pallas kernels for 36% -> 23%
where the time goes in v5:
time: 40.9 us; the launch traced here: 40.8 us
  Pallas kernels  21.4 us (52%)
  starting transfers between devices  13.9 us (34%)
  waiting for transfers between devices  4.04 us (10%)
  between operations  0.77 us (2%)
  other arithmetic  0.65 us (2%)
    ppermute x8, starting transfers between devices, swap(): return lax.ppermute(values, 'cluster', [(i, i ^ pair) for i in range(n)])  13.9 us
    pallas_call x1, Pallas kernels, encode(): pl.pallas_call(functools.partial(encode_kernel, order, c_dev, up_step), o...  8.37 us
    pallas_call x3, Pallas kernels, outer(): pl.pallas_call(functools.partial(outer_kernel, first, rows), out_shape=ja...  6.95 us
    ppermute x8, waiting for transfers between devices, swap(): return lax.ppermute(values, 'cluster', [(i, i ^ pair) for i in range(n)])  4.04 us
    pallas_call x1, Pallas kernels, score(): pl.pallas_call(functools.partial(score_kernel, len(flipped)), out_shape=(...  3.73 us
    pallas_call x3, Pallas kernels, flip(): pl.pallas_call(functools.partial(flip_kernel, first), out_shape=(pltpu.VM...  2.31 us
  transfers between devices with their start and end apart: 8, of which 5 were waited for; matrix products, arithmetic and copies ran while one was open for 0% of the time, Pallas kernels for 23%

profile of v5, /device:TPU:0, one launch (start us, length us, event | category | flops | bytes accessed | tf_op | source)
XLA Modules:
  0.0 40.8 jit_solution(9352077486765188931)
XLA Ops:
  0.6 0.0 slice-start.1
  0.7 8.4 %encode.1 = (bf16[4,1024]{1,0:T(4,128)(2,1)S(1)}, f32[64,4096]{1,0:T(8,128)S(1)}) custom-call(bf16[4,128,1024]{2,1,0:T(8,128)(2,1)} %x_hbm.1, s32[4,128]{1,0:T(4,128)} %ids_hbm.1, bf16[1024,2048]{1,0:T(8,128)(2,1)} %up_hbm.1, bf16[2048,1024]{1,0:T(8,128)(2,1)} %down_hbm.1, s32[16,64]{1,0:T(8,128)} %bitcast.4, s32[1,64]{1,0:T(1,128)} %bitcast.5), custom_call_target="tpu_custom_call" | custom-call | flops 4294967296 | bytes 9437184 | tf_op jit(solution)/shard_map/encode/pallas_call | solution.py:117
  9.0 3.5 %collective-permute-start = (bf16[4,1024]{1,0:T(4,128)(2,1)S(1)}, bf16[4,1024]{1,0:T(4,128)(2,1)S(1)}, u32[]{:S(2)}, u32[]{:S(2)}) collective-permute-start(bf16[4,1024]{1,0:T(4,128)(2,1)S(1)} %get-tuple-element.21._.a_ref), channel_id=1, source_target_pairs={{0,9},{1,8},{2,11},{3,10},{4,13},{5,12},{6,15},{7,14},{8,1},{9,0},... | collective-permute-start | bytes 24584 | tf_op jit(solution)/shard_map/ppermute | solution.py:274
  12.6 0.7 %flip.3 = (bf16[1024,1280]{1,0:T(8,128)(2,1)S(1)}, f32[8,128]{1,0:T(8,128)S(1)}) custom-call(bf16[4096,1024]{1,0:T(8,128)(2,1)S(1)} %bitcast.3, bf16[4,1024]{1,0:T(4,128)(2,1)S(1)} %get-tuple-element.21._.a_ref), custom_call_target="tpu_custom_call" | custom-call | bytes 2621440 | tf_op jit(solution)/shard_map/flip/pallas_call | solution.py:153
  13.3 0.6 %collective-permute-done.b_ref = bf16[4,1024]{1,0:T(4,128)(2,1)S(1)} collective-permute-done((bf16[4,1024]{1,0:T(4,128)(2,1)S(1)}, bf16[4,1024]{1,0:T(4,128)(2,1)S(1)}, u32[]{:S(2)}, u32[]{:S(2)}) %collective-permute-start) | collective-permute-done | bytes 8224 | tf_op jit(solution)/shard_map/ppermute | solution.py:274
  13.9 1.9 %collective-permute-start.1 = (bf16[8,1024]{1,0:T(8,128)(2,1)S(1)}, bf16[8,1024]{1,0:T(8,128)(2,1)S(1)}, u32[]{:S(2)}, u32[]{:S(2)}) collective-permute-start(bf16[8,1024]{1,0:T(8,128)(2,1)S(1)} %join.3._.a_ref), channel_id=1, source_target_pairs={{0,5},{1,4},{2,7},{3,6},{4,1},{5,0},{6,3},{7,2},{8,13},{9,12},{10,... | collective-permute-start | bytes 49160 | tf_op jit(solution)/shard_map/ppermute | solution.py:274
  15.8 0.9 %flip.4 = (bf16[1024,1536]{1,0:T(8,128)(2,1)S(1)}, f32[8,128]{1,0:T(8,128)S(1)}) custom-call(bf16[4096,1024]{1,0:T(8,128)(2,1)S(1)} %bitcast.3, bf16[8,1024]{1,0:T(8,128)(2,1)S(1)} %join.3._.a_ref), custom_call_target="tpu_custom_call" | custom-call | bytes 3145728 | tf_op jit(solution)/shard_map/flip/pallas_call | solution.py:153
  16.7 0.6 %collective-permute-done.1.b_ref = bf16[8,1024]{1,0:T(8,128)(2,1)S(1)} collective-permute-done((bf16[8,1024]{1,0:T(8,128)(2,1)S(1)}, bf16[8,1024]{1,0:T(8,128)(2,1)S(1)}, u32[]{:S(2)}, u32[]{:S(2)}) %collective-permute-start.1) | collective-permute-done | bytes 16416 | tf_op jit(solution)/shard_map/ppermute | solution.py:274
  17.3 1.7 %collective-permute-start.2 = (bf16[16,1024]{1,0:T(8,128)(2,1)S(1)}, bf16[16,1024]{1,0:T(8,128)(2,1)S(1)}, u32[]{:S(2)}, u32[]{:S(2)}) collective-permute-start(bf16[16,1024]{1,0:T(8,128)(2,1)S(1)} %join.4._.a_ref), channel_id=1, source_target_pairs={{0,3},{1,2},{2,1},{3,0},{4,7},{5,6},{6,5},{7,4},{8,11},{9,10},{10,... | collective-permute-start | bytes 98312 | tf_op jit(solution)/shard_map/ppermute | solution.py:274
  18.9 0.7 %flip.5 = (bf16[1024,1280]{1,0:T(8,128)(2,1)S(1)}, f32[8,128]{1,0:T(8,128)S(1)}) custom-call(bf16[4096,1024]{1,0:T(8,128)(2,1)S(1)} %bitcast.3, bf16[16,1024]{1,0:T(8,128)(2,1)S(1)} %join.4._.a_ref), custom_call_target="tpu_custom_call" | custom-call | bytes 2621440 | tf_op jit(solution)/shard_map/flip/pallas_call | solution.py:153
  19.7 0.9 %collective-permute-done.2.b_ref = bf16[16,1024]{1,0:T(8,128)(2,1)S(1)} collective-permute-done((bf16[16,1024]{1,0:T(8,128)(2,1)S(1)}, bf16[16,1024]{1,0:T(8,128)(2,1)S(1)}, u32[]{:S(2)}, u32[]{:S(2)}) %collective-permute-start.2) | collective-permute-done | bytes 32800 | tf_op jit(solution)/shard_map/ppermute | solution.py:274
  20.6 0.5 %collective-permute-start.3 = (bf16[32,1024]{1,0:T(8,128)(2,1)S(1)}, bf16[32,1024]{1,0:T(8,128)(2,1)S(1)}, u32[]{:S(2)}, u32[]{:S(2)}) collective-permute-start(bf16[32,1024]{1,0:T(8,128)(2,1)S(1)} %join.5.qa_ref), channel_id=1, source_target_pairs={{0,1},{1,0},{2,3},{3,2},{4,5},{5,4},{6,7},{7,6},{8,9},{9,8},{10,11... | collective-permute-start | bytes 196616 | tf_op jit(solution)/shard_map/ppermute | solution.py:274
  21.1 0.9 %collective-permute-done.3.qb_ref = bf16[32,1024]{1,0:T(8,128)(2,1)S(1)} collective-permute-done((bf16[32,1024]{1,0:T(8,128)(2,1)S(1)}, bf16[32,1024]{1,0:T(8,128)(2,1)S(1)}, u32[]{:S(2)}, u32[]{:S(2)}) %collective-permute-start.3) | collective-permute-done | bytes 65568 | tf_op jit(solution)/shard_map/ppermute | solution.py:274
  22.0 3.7 %score.1 = (bf16[64,1024]{1,0:T(8,128)(2,1)S(1)}, f32[32,1024]{1,0:T(8,128)S(1)}, f32[32,1024]{1,0:T(8,128)S(1)}, bf16[64,4096]{1,0:T(8,128)(2,1)S(1)}, f32[4096,1024]{1,0:T(8,128)}) custom-call(bf16[32,1024]{1,0:T(8,128)(2,1)S(1)} %join.5.qa_ref, bf16[32,1024]{1,0:T(8,128)(2,1)S(1)} %collective-permute-done.3.qb_ref, ...), custom_call_target="tpu_custom_call" | custom-call | flops 1073741824 | bytes 8388608 | tf_op jit(solution)/shard_map/score/pallas_call | solution.py:222
  25.7 0.4 %collective-permute-start.4 = (f32[32,1024]{1,0:T(8,128)S(1)}, f32[32,1024]{1,0:T(8,128)S(1)}, u32[]{:S(2)}, u32[]{:S(2)}) collective-permute-start(f32[32,1024]{1,0:T(8,128)S(1)} %get-tuple-element.30), channel_id=1, source_target_pairs={{0,1},{1,0},{2,3},{3,2},{4,5},{5,4},{6,7},{7,6},{8,9},{9,8},{10,11... | collective-permute-start | bytes 393224 | tf_op jit(solution)/shard_map/ppermute | solution.py:274
  26.1 1.0 %collective-permute-done.4 = f32[32,1024]{1,0:T(8,128)S(1)} collective-permute-done((f32[32,1024]{1,0:T(8,128)S(1)}, f32[32,1024]{1,0:T(8,128)S(1)}, u32[]{:S(2)}, u32[]{:S(2)}) %collective-permute-start.4) | collective-permute-done | bytes 131104 | tf_op jit(solution)/shard_map/ppermute | solution.py:274
  27.2 1.7 %collective-permute-start.5 = (f32[16,1024]{1,0:T(8,128)S(1)}, f32[16,1024]{1,0:T(8,128)S(1)}, u32[]{:S(2)}, u32[]{:S(2)}) collective-permute-start(f32[16,1024]{1,0:T(8,128)S(1)} %slice.25), channel_id=1, source_target_pairs={{0,3},{1,2},{2,1},{3,0},{4,7},{5,6},{6,5},{7,4},{8,11},{9,10},{10,... | collective-permute-start | bytes 196616 | tf_op jit(solution)/shard_map/ppermute | solution.py:274
  28.9 2.7 %outer.3._ = f32[4096,1024]{1,0:T(8,128)} custom-call(bf16[64,4096]{1,0:T(8,128)(2,1)S(1)} %get-tuple-element.31.dlogit_ref, bf16[64,1024]{1,0:T(8,128)(2,1)S(1)} %get-tuple-element.32.q_ref, f32[4096,1024]{1,0:T(8,128)} %get-tuple-element.33._), custom_call_target="tpu_custom_call", output_to_operand_aliasing={{}: (2, {})} | custom-call | flops 167772160 | bytes 5242880 | tf_op jit(solution)/shard_map/outer/pallas_call | solution.py:250
  31.6 1.6 %collective-permute-start.6 = (f32[8,1024]{1,0:T(8,128)S(1)}, f32[8,1024]{1,0:T(8,128)S(1)}, u32[]{:S(2)}, u32[]{:S(2)}) collective-permute-start(f32[8,1024]{1,0:T(8,128)S(1)} %slice.27), channel_id=1, source_target_pairs={{0,5},{1,4},{2,7},{3,6},{4,1},{5,0},{6,3},{7,2},{8,13},{9,12},{10,... | collective-permute-start | bytes 98312 | tf_op jit(solution)/shard_map/ppermute | solution.py:274
  33.2 2.1 %outer.4._ = f32[4096,1024]{1,0:T(8,128)} custom-call(bf16[64,4096]{1,0:T(8,128)(2,1)S(1)} %get-tuple-element.31.dlogit_ref, bf16[64,1024]{1,0:T(8,128)(2,1)S(1)} %get-tuple-element.32.q_ref, f32[4096,1024]{1,0:T(8,128)} %outer.3._), custom_call_target="tpu_custom_call", output_to_operand_aliasing={{}: (2, {})} | custom-call | flops 117440512 | bytes 3670016 | tf_op jit(solution)/shard_map/outer/pallas_call | solution.py:250
  35.4 2.6 %collective-permute-start.7 = (f32[4,1024]{1,0:T(4,128)S(1)}, f32[4,1024]{1,0:T(4,128)S(1)}, u32[]{:S(2)}, u32[]{:S(2)}) collective-permute-start(f32[4,1024]{1,0:T(4,128)S(1)} %slice.29), channel_id=1, source_target_pairs={{0,9},{1,8},{2,11},{3,10},{4,13},{5,12},{6,15},{7,14},{8,1},{9,0},... | collective-permute-start | bytes 49160 | tf_op jit(solution)/shard_map/ppermute | solution.py:274
  38.0 2.1 %outer.5 = f32[4096,1024]{1,0:T(8,128)} custom-call(bf16[64,4096]{1,0:T(8,128)(2,1)S(1)} %get-tuple-element.31.dlogit_ref, bf16[64,1024]{1,0:T(8,128)(2,1)S(1)} %get-tuple-element.32.q_ref, f32[4096,1024]{1,0:T(8,128)} %outer.4._), custom_call_target="tpu_custom_call", output_to_operand_aliasing={{}: (2, {})} | custom-call | flops 117440512 | bytes 3670016 | tf_op jit(solution)/shard_map/outer/pallas_call | solution.py:250
  40.2 0.0 collective-permute-done.7
  40.2 0.6 %slice_add_fusion.2 = f32[4,1024]{1,0:T(4,128)} fusion(f32[4,1024]{1,0:T(4,128)S(1)} %collective-permute-done.7, f32[8,1024]{1,0:T(8,128)S(1)} %slice_add_fusion.1), kind=kLoop, calls=%fused_computation.2 | loop fusion | flops 4096 | bytes 49152 | tf_op jit(solution)/shard_map/add | solution.py:299
  (15 shorter events, 0.1 us)
Async XLA Ops:
  0.6 11.9 %slice-start = ((s8[8388608]{0:T(1024)(128)(4,1)}), s8[4194304]{0:T(1024)(128)(4,1)S(1)}, s32[]{:S(2)}) async-start(s8[8388608]{0:T(1024)(128)(4,1)} %bitcast.2), calls=%async_computation | async-start | bytes 8388608
  0.6 11.9 %slice-start.1 = ((s8[8388608]{0:T(1024)(128)(4,1)}), s8[4194304]{0:T(1024)(128)(4,1)S(1)}, s32[]{:S(2)}) async-start(s8[8388608]{0:T(1024)(128)(4,1)} %bitcast.2), calls=%async_computation.1 | async-start | bytes 8388608
  9.0 4.9 %collective-permute-start = (bf16[4,1024]{1,0:T(4,128)(2,1)S(1)}, bf16[4,1024]{1,0:T(4,128)(2,1)S(1)}, u32[]{:S(2)}, u32[]{:S(2)}) collective-permute-start(bf16[4,1024]{1,0:T(4,128)(2,1)S(1)} %get-tuple-element.21._.a_ref), channel_id=1, source_target_pairs={{0,9},{1,8},{2,11},{3,10},{4,13},{5,12},{6,15},{7,14},{8,1},{9,0},... | collective-permute-start | bytes 24584 | tf_op jit(solution)/shard_map/ppermute | solution.py:274
  13.9 3.3 %collective-permute-start.1 = (bf16[8,1024]{1,0:T(8,128)(2,1)S(1)}, bf16[8,1024]{1,0:T(8,128)(2,1)S(1)}, u32[]{:S(2)}, u32[]{:S(2)}) collective-permute-start(bf16[8,1024]{1,0:T(8,128)(2,1)S(1)} %join.3._.a_ref), channel_id=1, source_target_pairs={{0,5},{1,4},{2,7},{3,6},{4,1},{5,0},{6,3},{7,2},{8,13},{9,12},{10,... | collective-permute-start | bytes 49160 | tf_op jit(solution)/shard_map/ppermute | solution.py:274
  17.3 3.3 %collective-permute-start.2 = (bf16[16,1024]{1,0:T(8,128)(2,1)S(1)}, bf16[16,1024]{1,0:T(8,128)(2,1)S(1)}, u32[]{:S(2)}, u32[]{:S(2)}) collective-permute-start(bf16[16,1024]{1,0:T(8,128)(2,1)S(1)} %join.4._.a_ref), channel_id=1, source_target_pairs={{0,3},{1,2},{2,1},{3,0},{4,7},{5,6},{6,5},{7,4},{8,11},{9,10},{10,... | collective-permute-start | bytes 98312 | tf_op jit(solution)/shard_map/ppermute | solution.py:274
  20.6 1.4 %collective-permute-start.3 = (bf16[32,1024]{1,0:T(8,128)(2,1)S(1)}, bf16[32,1024]{1,0:T(8,128)(2,1)S(1)}, u32[]{:S(2)}, u32[]{:S(2)}) collective-permute-start(bf16[32,1024]{1,0:T(8,128)(2,1)S(1)} %join.5.qa_ref), channel_id=1, source_target_pairs={{0,1},{1,0},{2,3},{3,2},{4,5},{5,4},{6,7},{7,6},{8,9},{9,8},{10,11... | collective-permute-start | bytes 196616 | tf_op jit(solution)/shard_map/ppermute | solution.py:274
  25.7 1.4 %collective-permute-start.4 = (f32[32,1024]{1,0:T(8,128)S(1)}, f32[32,1024]{1,0:T(8,128)S(1)}, u32[]{:S(2)}, u32[]{:S(2)}) collective-permute-start(f32[32,1024]{1,0:T(8,128)S(1)} %get-tuple-element.30), channel_id=1, source_target_pairs={{0,1},{1,0},{2,3},{3,2},{4,5},{5,4},{6,7},{7,6},{8,9},{9,8},{10,11... | collective-permute-start | bytes 393224 | tf_op jit(solution)/shard_map/ppermute | solution.py:274
  27.2 4.4 %collective-permute-start.5 = (f32[16,1024]{1,0:T(8,128)S(1)}, f32[16,1024]{1,0:T(8,128)S(1)}, u32[]{:S(2)}, u32[]{:S(2)}) collective-permute-start(f32[16,1024]{1,0:T(8,128)S(1)} %slice.25), channel_id=1, source_target_pairs={{0,3},{1,2},{2,1},{3,0},{4,7},{5,6},{6,5},{7,4},{8,11},{9,10},{10,... | collective-permute-start | bytes 196616 | tf_op jit(solution)/shard_map/ppermute | solution.py:274
  31.6 3.8 %collective-permute-start.6 = (f32[8,1024]{1,0:T(8,128)S(1)}, f32[8,1024]{1,0:T(8,128)S(1)}, u32[]{:S(2)}, u32[]{:S(2)}) collective-permute-start(f32[8,1024]{1,0:T(8,128)S(1)} %slice.27), channel_id=1, source_target_pairs={{0,5},{1,4},{2,7},{3,6},{4,1},{5,0},{6,3},{7,2},{8,13},{9,12},{10,... | collective-permute-start | bytes 98312 | tf_op jit(solution)/shard_map/ppermute | solution.py:274
  35.4 4.8 %collective-permute-start.7 = (f32[4,1024]{1,0:T(4,128)S(1)}, f32[4,1024]{1,0:T(4,128)S(1)}, u32[]{:S(2)}, u32[]{:S(2)}) collective-permute-start(f32[4,1024]{1,0:T(4,128)S(1)} %slice.29), channel_id=1, source_target_pairs={{0,9},{1,8},{2,11},{3,10},{4,13},{5,12},{6,15},{7,14},{8,1},{9,0},... | collective-permute-start | bytes 49160 | tf_op jit(solution)/shard_map/ppermute | solution.py:274

commit v6 on v5

--- a/solution.py
+++ b/solution.py
@@ -13,7 +13,7 @@
 BF16 = jnp.bfloat16
 FETCH = (0.0, 0.3125, 0.6875, 1.0)
 FIRST = 0.25
-SHARES = (0.0, 0.5625, 0.78125, 1.0)
+SHARES = (0.0, 0.59375, 0.84375, 1.0)
 HBM = pltpu.MemorySpace.HBM
 NN = (((1,), (0,)), ((), ()))
 NT = (((1,), (1,)), ((), ()))

time: 40.9 us -> 40.9 us (level)
  no operation moved by 1% of the time
where the time goes in v6:
time: 40.9 us; the launch traced here: 40.7 us
  Pallas kernels  21.4 us (52%)
  starting transfers between devices  13.9 us (34%)
  waiting for transfers between devices  4.04 us (10%)
  between operations  0.77 us (2%)
  other arithmetic  0.65 us (2%)
    ppermute x8, starting transfers between devices, swap(): return lax.ppermute(values, 'cluster', [(i, i ^ pair) for i in range(n)])  13.9 us
    pallas_call x1, Pallas kernels, encode(): pl.pallas_call(functools.partial(encode_kernel, order, c_dev, up_step), o...  8.37 us
    pallas_call x3, Pallas kernels, outer(): pl.pallas_call(functools.partial(outer_kernel, first, rows), out_shape=ja...  6.93 us
    ppermute x8, waiting for transfers between devices, swap(): return lax.ppermute(values, 'cluster', [(i, i ^ pair) for i in range(n)])  4.04 us
    pallas_call x1, Pallas kernels, score(): pl.pallas_call(functools.partial(score_kernel, len(flipped)), out_shape=(...  3.73 us
    pallas_call x3, Pallas kernels, flip(): pl.pallas_call(functools.partial(flip_kernel, first), out_shape=(pltpu.VM...  2.31 us
  transfers between devices with their start and end apart: 8, of which 5 were waited for; matrix products, arithmetic and copies ran while one was open for 0% of the time, Pallas kernels for 23%

profile of v6, /device:TPU:0, one launch (start us, length us, event | category | flops | bytes accessed | tf_op | source)
XLA Modules:
  0.0 40.7 jit_solution(8814754386334625311)
XLA Ops:
  0.6 0.0 slice-start
  0.6 0.0 slice-start.1
  0.7 8.4 %encode.1 = (bf16[4,1024]{1,0:T(4,128)(2,1)S(1)}, f32[64,4096]{1,0:T(8,128)S(1)}) custom-call(bf16[4,128,1024]{2,1,0:T(8,128)(2,1)} %x_hbm.1, s32[4,128]{1,0:T(4,128)} %ids_hbm.1, bf16[1024,2048]{1,0:T(8,128)(2,1)} %up_hbm.1, bf16[2048,1024]{1,0:T(8,128)(2,1)} %down_hbm.1, s32[16,64]{1,0:T(8,128)} %bitcast.4, s32[1,64]{1,0:T(1,128)} %bitcast.5), custom_call_target="tpu_custom_call" | custom-call | flops 4294967296 | bytes 9437184 | tf_op jit(solution)/shard_map/encode/pallas_call | solution.py:117
  9.0 3.5 %collective-permute-start = (bf16[4,1024]{1,0:T(4,128)(2,1)S(1)}, bf16[4,1024]{1,0:T(4,128)(2,1)S(1)}, u32[]{:S(2)}, u32[]{:S(2)}) collective-permute-start(bf16[4,1024]{1,0:T(4,128)(2,1)S(1)} %get-tuple-element.21._.a_ref), channel_id=1, source_target_pairs={{0,9},{1,8},{2,11},{3,10},{4,13},{5,12},{6,15},{7,14},{8,1},{9,0},... | collective-permute-start | bytes 24584 | tf_op jit(solution)/shard_map/ppermute | solution.py:274
  12.6 0.7 %flip.3 = (bf16[1024,1280]{1,0:T(8,128)(2,1)S(1)}, f32[8,128]{1,0:T(8,128)S(1)}) custom-call(bf16[4096,1024]{1,0:T(8,128)(2,1)S(1)} %bitcast.3, bf16[4,1024]{1,0:T(4,128)(2,1)S(1)} %get-tuple-element.21._.a_ref), custom_call_target="tpu_custom_call" | custom-call | bytes 2621440 | tf_op jit(solution)/shard_map/flip/pallas_call | solution.py:153
  13.3 0.6 %collective-permute-done.b_ref = bf16[4,1024]{1,0:T(4,128)(2,1)S(1)} collective-permute-done((bf16[4,1024]{1,0:T(4,128)(2,1)S(1)}, bf16[4,1024]{1,0:T(4,128)(2,1)S(1)}, u32[]{:S(2)}, u32[]{:S(2)}) %collective-permute-start) | collective-permute-done | bytes 8224 | tf_op jit(solution)/shard_map/ppermute | solution.py:274
  13.9 1.9 %collective-permute-start.1 = (bf16[8,1024]{1,0:T(8,128)(2,1)S(1)}, bf16[8,1024]{1,0:T(8,128)(2,1)S(1)}, u32[]{:S(2)}, u32[]{:S(2)}) collective-permute-start(bf16[8,1024]{1,0:T(8,128)(2,1)S(1)} %join.3._.a_ref), channel_id=1, source_target_pairs={{0,5},{1,4},{2,7},{3,6},{4,1},{5,0},{6,3},{7,2},{8,13},{9,12},{10,... | collective-permute-start | bytes 49160 | tf_op jit(solution)/shard_map/ppermute | solution.py:274
  15.8 0.9 %flip.4 = (bf16[1024,1536]{1,0:T(8,128)(2,1)S(1)}, f32[8,128]{1,0:T(8,128)S(1)}) custom-call(bf16[4096,1024]{1,0:T(8,128)(2,1)S(1)} %bitcast.3, bf16[8,1024]{1,0:T(8,128)(2,1)S(1)} %join.3._.a_ref), custom_call_target="tpu_custom_call" | custom-call | bytes 3145728 | tf_op jit(solution)/shard_map/flip/pallas_call | solution.py:153
  16.7 0.6 %collective-permute-done.1.b_ref = bf16[8,1024]{1,0:T(8,128)(2,1)S(1)} collective-permute-done((bf16[8,1024]{1,0:T(8,128)(2,1)S(1)}, bf16[8,1024]{1,0:T(8,128)(2,1)S(1)}, u32[]{:S(2)}, u32[]{:S(2)}) %collective-permute-start.1) | collective-permute-done | bytes 16416 | tf_op jit(solution)/shard_map/ppermute | solution.py:274
  17.3 1.7 %collective-permute-start.2 = (bf16[16,1024]{1,0:T(8,128)(2,1)S(1)}, bf16[16,1024]{1,0:T(8,128)(2,1)S(1)}, u32[]{:S(2)}, u32[]{:S(2)}) collective-permute-start(bf16[16,1024]{1,0:T(8,128)(2,1)S(1)} %join.4._.a_ref), channel_id=1, source_target_pairs={{0,3},{1,2},{2,1},{3,0},{4,7},{5,6},{6,5},{7,4},{8,11},{9,10},{10,... | collective-permute-start | bytes 98312 | tf_op jit(solution)/shard_map/ppermute | solution.py:274
  18.9 0.7 %flip.5 = (bf16[1024,1280]{1,0:T(8,128)(2,1)S(1)}, f32[8,128]{1,0:T(8,128)S(1)}) custom-call(bf16[4096,1024]{1,0:T(8,128)(2,1)S(1)} %bitcast.3, bf16[16,1024]{1,0:T(8,128)(2,1)S(1)} %join.4._.a_ref), custom_call_target="tpu_custom_call" | custom-call | bytes 2621440 | tf_op jit(solution)/shard_map/flip/pallas_call | solution.py:153
  19.7 0.9 %collective-permute-done.2.b_ref = bf16[16,1024]{1,0:T(8,128)(2,1)S(1)} collective-permute-done((bf16[16,1024]{1,0:T(8,128)(2,1)S(1)}, bf16[16,1024]{1,0:T(8,128)(2,1)S(1)}, u32[]{:S(2)}, u32[]{:S(2)}) %collective-permute-start.2) | collective-permute-done | bytes 32800 | tf_op jit(solution)/shard_map/ppermute | solution.py:274
  20.6 0.5 %collective-permute-start.3 = (bf16[32,1024]{1,0:T(8,128)(2,1)S(1)}, bf16[32,1024]{1,0:T(8,128)(2,1)S(1)}, u32[]{:S(2)}, u32[]{:S(2)}) collective-permute-start(bf16[32,1024]{1,0:T(8,128)(2,1)S(1)} %join.5.qa_ref), channel_id=1, source_target_pairs={{0,1},{1,0},{2,3},{3,2},{4,5},{5,4},{6,7},{7,6},{8,9},{9,8},{10,11... | collective-permute-start | bytes 196616 | tf_op jit(solution)/shard_map/ppermute | solution.py:274
  21.1 0.9 %collective-permute-done.3.qb_ref = bf16[32,1024]{1,0:T(8,128)(2,1)S(1)} collective-permute-done((bf16[32,1024]{1,0:T(8,128)(2,1)S(1)}, bf16[32,1024]{1,0:T(8,128)(2,1)S(1)}, u32[]{:S(2)}, u32[]{:S(2)}) %collective-permute-start.3) | collective-permute-done | bytes 65568 | tf_op jit(solution)/shard_map/ppermute | solution.py:274
  22.0 3.7 %score.1 = (bf16[64,1024]{1,0:T(8,128)(2,1)S(1)}, f32[32,1024]{1,0:T(8,128)S(1)}, f32[32,1024]{1,0:T(8,128)S(1)}, bf16[64,4096]{1,0:T(8,128)(2,1)S(1)}, f32[4096,1024]{1,0:T(8,128)}) custom-call(bf16[32,1024]{1,0:T(8,128)(2,1)S(1)} %join.5.qa_ref, bf16[32,1024]{1,0:T(8,128)(2,1)S(1)} %collective-permute-done.3.qb_ref, ...), custom_call_target="tpu_custom_call" | custom-call | flops 1073741824 | bytes 8388608 | tf_op jit(solution)/shard_map/score/pallas_call | solution.py:222
  25.7 0.4 %collective-permute-start.4 = (f32[32,1024]{1,0:T(8,128)S(1)}, f32[32,1024]{1,0:T(8,128)S(1)}, u32[]{:S(2)}, u32[]{:S(2)}) collective-permute-start(f32[32,1024]{1,0:T(8,128)S(1)} %get-tuple-element.30), channel_id=1, source_target_pairs={{0,1},{1,0},{2,3},{3,2},{4,5},{5,4},{6,7},{7,6},{8,9},{9,8},{10,11... | collective-permute-start | bytes 393224 | tf_op jit(solution)/shard_map/ppermute | solution.py:274
  26.1 1.0 %collective-permute-done.4 = f32[32,1024]{1,0:T(8,128)S(1)} collective-permute-done((f32[32,1024]{1,0:T(8,128)S(1)}, f32[32,1024]{1,0:T(8,128)S(1)}, u32[]{:S(2)}, u32[]{:S(2)}) %collective-permute-start.4) | collective-permute-done | bytes 131104 | tf_op jit(solution)/shard_map/ppermute | solution.py:274
  27.2 1.7 %collective-permute-start.5 = (f32[16,1024]{1,0:T(8,128)S(1)}, f32[16,1024]{1,0:T(8,128)S(1)}, u32[]{:S(2)}, u32[]{:S(2)}) collective-permute-start(f32[16,1024]{1,0:T(8,128)S(1)} %slice.25), channel_id=1, source_target_pairs={{0,3},{1,2},{2,1},{3,0},{4,7},{5,6},{6,5},{7,4},{8,11},{9,10},{10,... | collective-permute-start | bytes 196616 | tf_op jit(solution)/shard_map/ppermute | solution.py:274
  28.9 2.8 %outer.3._ = f32[4096,1024]{1,0:T(8,128)} custom-call(bf16[64,4096]{1,0:T(8,128)(2,1)S(1)} %get-tuple-element.31.dlogit_ref, bf16[64,1024]{1,0:T(8,128)(2,1)S(1)} %get-tuple-element.32.q_ref, f32[4096,1024]{1,0:T(8,128)} %get-tuple-element.33._), custom_call_target="tpu_custom_call", output_to_operand_aliasing={{}: (2, {})} | custom-call | flops 184549376 | bytes 5767168 | tf_op jit(solution)/shard_map/outer/pallas_call | solution.py:250
  31.8 1.6 %collective-permute-start.6 = (f32[8,1024]{1,0:T(8,128)S(1)}, f32[8,1024]{1,0:T(8,128)S(1)}, u32[]{:S(2)}, u32[]{:S(2)}) collective-permute-start(f32[8,1024]{1,0:T(8,128)S(1)} %slice.27), channel_id=1, source_target_pairs={{0,5},{1,4},{2,7},{3,6},{4,1},{5,0},{6,3},{7,2},{8,13},{9,12},{10,... | collective-permute-start | bytes 98312 | tf_op jit(solution)/shard_map/ppermute | solution.py:274
  33.4 2.3 %outer.4._ = f32[4096,1024]{1,0:T(8,128)} custom-call(bf16[64,4096]{1,0:T(8,128)(2,1)S(1)} %get-tuple-element.31.dlogit_ref, bf16[64,1024]{1,0:T(8,128)(2,1)S(1)} %get-tuple-element.32.q_ref, f32[4096,1024]{1,0:T(8,128)} %outer.3._), custom_call_target="tpu_custom_call", output_to_operand_aliasing={{}: (2, {})} | custom-call | flops 134217728 | bytes 4194304 | tf_op jit(solution)/shard_map/outer/pallas_call | solution.py:250
  35.7 2.6 %collective-permute-start.7 = (f32[4,1024]{1,0:T(4,128)S(1)}, f32[4,1024]{1,0:T(4,128)S(1)}, u32[]{:S(2)}, u32[]{:S(2)}) collective-permute-start(f32[4,1024]{1,0:T(4,128)S(1)} %slice.29), channel_id=1, source_target_pairs={{0,9},{1,8},{2,11},{3,10},{4,13},{5,12},{6,15},{7,14},{8,1},{9,0},... | collective-permute-start | bytes 49160 | tf_op jit(solution)/shard_map/ppermute | solution.py:274
  38.3 1.8 %outer.5 = f32[4096,1024]{1,0:T(8,128)} custom-call(bf16[64,4096]{1,0:T(8,128)(2,1)S(1)} %get-tuple-element.31.dlogit_ref, bf16[64,1024]{1,0:T(8,128)(2,1)S(1)} %get-tuple-element.32.q_ref, f32[4096,1024]{1,0:T(8,128)} %outer.4._), custom_call_target="tpu_custom_call", output_to_operand_aliasing={{}: (2, {})} | custom-call | flops 83886080 | bytes 2621440 | tf_op jit(solution)/shard_map/outer/pallas_call | solution.py:250
  40.1 0.6 %slice_add_fusion.2 = f32[4,1024]{1,0:T(4,128)} fusion(f32[4,1024]{1,0:T(4,128)S(1)} %collective-permute-done.7, f32[8,1024]{1,0:T(8,128)S(1)} %slice_add_fusion.1), kind=kLoop, calls=%fused_computation.2 | loop fusion | flops 4096 | bytes 49152 | tf_op jit(solution)/shard_map/add | solution.py:299
  (15 shorter events, 0.1 us)
Async XLA Ops:
  0.6 11.9 %slice-start = ((s8[8388608]{0:T(1024)(128)(4,1)}), s8[4194304]{0:T(1024)(128)(4,1)S(1)}, s32[]{:S(2)}) async-start(s8[8388608]{0:T(1024)(128)(4,1)} %bitcast.2), calls=%async_computation | async-start | bytes 8388608
  0.6 11.9 %slice-start.1 = ((s8[8388608]{0:T(1024)(128)(4,1)}), s8[4194304]{0:T(1024)(128)(4,1)S(1)}, s32[]{:S(2)}) async-start(s8[8388608]{0:T(1024)(128)(4,1)} %bitcast.2), calls=%async_computation.1 | async-start | bytes 8388608
  9.0 4.9 %collective-permute-start = (bf16[4,1024]{1,0:T(4,128)(2,1)S(1)}, bf16[4,1024]{1,0:T(4,128)(2,1)S(1)}, u32[]{:S(2)}, u32[]{:S(2)}) collective-permute-start(bf16[4,1024]{1,0:T(4,128)(2,1)S(1)} %get-tuple-element.21._.a_ref), channel_id=1, source_target_pairs={{0,9},{1,8},{2,11},{3,10},{4,13},{5,12},{6,15},{7,14},{8,1},{9,0},... | collective-permute-start | bytes 24584 | tf_op jit(solution)/shard_map/ppermute | solution.py:274
  13.9 3.3 %collective-permute-start.1 = (bf16[8,1024]{1,0:T(8,128)(2,1)S(1)}, bf16[8,1024]{1,0:T(8,128)(2,1)S(1)}, u32[]{:S(2)}, u32[]{:S(2)}) collective-permute-start(bf16[8,1024]{1,0:T(8,128)(2,1)S(1)} %join.3._.a_ref), channel_id=1, source_target_pairs={{0,5},{1,4},{2,7},{3,6},{4,1},{5,0},{6,3},{7,2},{8,13},{9,12},{10,... | collective-permute-start | bytes 49160 | tf_op jit(solution)/shard_map/ppermute | solution.py:274
  17.3 3.3 %collective-permute-start.2 = (bf16[16,1024]{1,0:T(8,128)(2,1)S(1)}, bf16[16,1024]{1,0:T(8,128)(2,1)S(1)}, u32[]{:S(2)}, u32[]{:S(2)}) collective-permute-start(bf16[16,1024]{1,0:T(8,128)(2,1)S(1)} %join.4._.a_ref), channel_id=1, source_target_pairs={{0,3},{1,2},{2,1},{3,0},{4,7},{5,6},{6,5},{7,4},{8,11},{9,10},{10,... | collective-permute-start | bytes 98312 | tf_op jit(solution)/shard_map/ppermute | solution.py:274
  20.6 1.4 %collective-permute-start.3 = (bf16[32,1024]{1,0:T(8,128)(2,1)S(1)}, bf16[32,1024]{1,0:T(8,128)(2,1)S(1)}, u32[]{:S(2)}, u32[]{:S(2)}) collective-permute-start(bf16[32,1024]{1,0:T(8,128)(2,1)S(1)} %join.5.qa_ref), channel_id=1, source_target_pairs={{0,1},{1,0},{2,3},{3,2},{4,5},{5,4},{6,7},{7,6},{8,9},{9,8},{10,11... | collective-permute-start | bytes 196616 | tf_op jit(solution)/shard_map/ppermute | solution.py:274
  25.7 1.4 %collective-permute-start.4 = (f32[32,1024]{1,0:T(8,128)S(1)}, f32[32,1024]{1,0:T(8,128)S(1)}, u32[]{:S(2)}, u32[]{:S(2)}) collective-permute-start(f32[32,1024]{1,0:T(8,128)S(1)} %get-tuple-element.30), channel_id=1, source_target_pairs={{0,1},{1,0},{2,3},{3,2},{4,5},{5,4},{6,7},{7,6},{8,9},{9,8},{10,11... | collective-permute-start | bytes 393224 | tf_op jit(solution)/shard_map/ppermute | solution.py:274
  27.2 4.6 %collective-permute-start.5 = (f32[16,1024]{1,0:T(8,128)S(1)}, f32[16,1024]{1,0:T(8,128)S(1)}, u32[]{:S(2)}, u32[]{:S(2)}) collective-permute-start(f32[16,1024]{1,0:T(8,128)S(1)} %slice.25), channel_id=1, source_target_pairs={{0,3},{1,2},{2,1},{3,0},{4,7},{5,6},{6,5},{7,4},{8,11},{9,10},{10,... | collective-permute-start | bytes 196616 | tf_op jit(solution)/shard_map/ppermute | solution.py:274
  31.8 3.9 %collective-permute-start.6 = (f32[8,1024]{1,0:T(8,128)S(1)}, f32[8,1024]{1,0:T(8,128)S(1)}, u32[]{:S(2)}, u32[]{:S(2)}) collective-permute-start(f32[8,1024]{1,0:T(8,128)S(1)} %slice.27), channel_id=1, source_target_pairs={{0,5},{1,4},{2,7},{3,6},{4,1},{5,0},{6,3},{7,2},{8,13},{9,12},{10,... | collective-permute-start | bytes 98312 | tf_op jit(solution)/shard_map/ppermute | solution.py:274
  35.7 4.4 %collective-permute-start.7 = (f32[4,1024]{1,0:T(4,128)S(1)}, f32[4,1024]{1,0:T(4,128)S(1)}, u32[]{:S(2)}, u32[]{:S(2)}) collective-permute-start(f32[4,1024]{1,0:T(4,128)S(1)} %slice.29), channel_id=1, source_target_pairs={{0,9},{1,8},{2,11},{3,10},{4,13},{5,12},{6,15},{7,14},{8,1},{9,0},... | collective-permute-start | bytes 49160 | tf_op jit(solution)/shard_map/ppermute | solution.py:274

commit v7 on v5

--- a/solution.py
+++ b/solution.py
@@ -98,8 +98,11 @@
     place = lax.broadcasted_iota(jnp.int32, (length, 1), 0).astype(F32)
     down_copy.wait()
     rows = []
+    ahead = dot(act_ref[:length, :], down_ref[...], NN)
     for k in range(count):
-        ffn = dot(act_ref[k * length : (k + 1) * length, :], down_ref[...], NN)
+        ffn = ahead
+        if k + 1 < count:
+            ahead = dot(act_ref[(k + 1) * length : (k + 2) * length, :], down_ref[...], NN)
         centered, scale = normed(x_ref[k].astype(F32) + ffn)
         own = kept[k : k + 1, :]
         scale = jnp.where(place < own, scale, 0.0)

time: 40.9 us -> 40.9 us (level)
  no operation moved by 1% of the time
where the time goes in v7:
time: 40.9 us; the launch traced here: 40.8 us
  Pallas kernels  21.4 us (52%)
  starting transfers between devices  13.9 us (34%)
  waiting for transfers between devices  4.04 us (10%)
  between operations  0.77 us (2%)
  other arithmetic  0.65 us (2%)
    ppermute x8, starting transfers between devices, swap(): return lax.ppermute(values, 'cluster', [(i, i ^ pair) for i in range(n)])  13.9 us
    pallas_call x1, Pallas kernels, encode(): pl.pallas_call(functools.partial(encode_kernel, order, c_dev, up_step), o...  8.37 us
    pallas_call x3, Pallas kernels, outer(): pl.pallas_call(functools.partial(outer_kernel, first, rows), out_shape=ja...  6.95 us
    ppermute x8, waiting for transfers between devices, swap(): return lax.ppermute(values, 'cluster', [(i, i ^ pair) for i in range(n)])  4.04 us
    pallas_call x1, Pallas kernels, score(): pl.pallas_call(functools.partial(score_kernel, len(flipped)), out_shape=(...  3.73 us
    pallas_call x3, Pallas kernels, flip(): pl.pallas_call(functools.partial(flip_kernel, first), out_shape=(pltpu.VM...  2.31 us
  transfers between devices with their start and end apart: 8, of which 5 were waited for; matrix products, arithmetic and copies ran while one was open for 0% of the time, Pallas kernels for 23%

profile of v7, /device:TPU:0, one launch (start us, length us, event | category | flops | bytes accessed | tf_op | source)
XLA Modules:
  0.0 40.8 jit_solution(2176832188389209137)
XLA Ops:
  0.6 0.0 slice-start.1
  0.7 8.4 %encode.1 = (bf16[4,1024]{1,0:T(4,128)(2,1)S(1)}, f32[64,4096]{1,0:T(8,128)S(1)}) custom-call(bf16[4,128,1024]{2,1,0:T(8,128)(2,1)} %x_hbm.1, s32[4,128]{1,0:T(4,128)} %ids_hbm.1, bf16[1024,2048]{1,0:T(8,128)(2,1)} %up_hbm.1, bf16[2048,1024]{1,0:T(8,128)(2,1)} %down_hbm.1, s32[16,64]{1,0:T(8,128)} %bitcast.4, s32[1,64]{1,0:T(1,128)} %bitcast.5), custom_call_target="tpu_custom_call" | custom-call | flops 4294967296 | bytes 9437184 | tf_op jit(solution)/shard_map/encode/pallas_call | solution.py:120
  9.0 3.5 %collective-permute-start = (bf16[4,1024]{1,0:T(4,128)(2,1)S(1)}, bf16[4,1024]{1,0:T(4,128)(2,1)S(1)}, u32[]{:S(2)}, u32[]{:S(2)}) collective-permute-start(bf16[4,1024]{1,0:T(4,128)(2,1)S(1)} %get-tuple-element.21._.a_ref), channel_id=1, source_target_pairs={{0,9},{1,8},{2,11},{3,10},{4,13},{5,12},{6,15},{7,14},{8,1},{9,0},... | collective-permute-start | bytes 24584 | tf_op jit(solution)/shard_map/ppermute | solution.py:277
  12.6 0.7 %flip.3 = (bf16[1024,1280]{1,0:T(8,128)(2,1)S(1)}, f32[8,128]{1,0:T(8,128)S(1)}) custom-call(bf16[4096,1024]{1,0:T(8,128)(2,1)S(1)} %bitcast.3, bf16[4,1024]{1,0:T(4,128)(2,1)S(1)} %get-tuple-element.21._.a_ref), custom_call_target="tpu_custom_call" | custom-call | bytes 2621440 | tf_op jit(solution)/shard_map/flip/pallas_call | solution.py:156
  13.3 0.6 %collective-permute-done.b_ref = bf16[4,1024]{1,0:T(4,128)(2,1)S(1)} collective-permute-done((bf16[4,1024]{1,0:T(4,128)(2,1)S(1)}, bf16[4,1024]{1,0:T(4,128)(2,1)S(1)}, u32[]{:S(2)}, u32[]{:S(2)}) %collective-permute-start) | collective-permute-done | bytes 8224 | tf_op jit(solution)/shard_map/ppermute | solution.py:277
  13.9 1.9 %collective-permute-start.1 = (bf16[8,1024]{1,0:T(8,128)(2,1)S(1)}, bf16[8,1024]{1,0:T(8,128)(2,1)S(1)}, u32[]{:S(2)}, u32[]{:S(2)}) collective-permute-start(bf16[8,1024]{1,0:T(8,128)(2,1)S(1)} %join.3._.a_ref), channel_id=1, source_target_pairs={{0,5},{1,4},{2,7},{3,6},{4,1},{5,0},{6,3},{7,2},{8,13},{9,12},{10,... | collective-permute-start | bytes 49160 | tf_op jit(solution)/shard_map/ppermute | solution.py:277
  15.8 0.9 %flip.4 = (bf16[1024,1536]{1,0:T(8,128)(2,1)S(1)}, f32[8,128]{1,0:T(8,128)S(1)}) custom-call(bf16[4096,1024]{1,0:T(8,128)(2,1)S(1)} %bitcast.3, bf16[8,1024]{1,0:T(8,128)(2,1)S(1)} %join.3._.a_ref), custom_call_target="tpu_custom_call" | custom-call | bytes 3145728 | tf_op jit(solution)/shard_map/flip/pallas_call | solution.py:156
  16.7 0.6 %collective-permute-done.1.b_ref = bf16[8,1024]{1,0:T(8,128)(2,1)S(1)} collective-permute-done((bf16[8,1024]{1,0:T(8,128)(2,1)S(1)}, bf16[8,1024]{1,0:T(8,128)(2,1)S(1)}, u32[]{:S(2)}, u32[]{:S(2)}) %collective-permute-start.1) | collective-permute-done | bytes 16416 | tf_op jit(solution)/shard_map/ppermute | solution.py:277
  17.3 1.7 %collective-permute-start.2 = (bf16[16,1024]{1,0:T(8,128)(2,1)S(1)}, bf16[16,1024]{1,0:T(8,128)(2,1)S(1)}, u32[]{:S(2)}, u32[]{:S(2)}) collective-permute-start(bf16[16,1024]{1,0:T(8,128)(2,1)S(1)} %join.4._.a_ref), channel_id=1, source_target_pairs={{0,3},{1,2},{2,1},{3,0},{4,7},{5,6},{6,5},{7,4},{8,11},{9,10},{10,... | collective-permute-start | bytes 98312 | tf_op jit(solution)/shard_map/ppermute | solution.py:277
  18.9 0.7 %flip.5 = (bf16[1024,1280]{1,0:T(8,128)(2,1)S(1)}, f32[8,128]{1,0:T(8,128)S(1)}) custom-call(bf16[4096,1024]{1,0:T(8,128)(2,1)S(1)} %bitcast.3, bf16[16,1024]{1,0:T(8,128)(2,1)S(1)} %join.4._.a_ref), custom_call_target="tpu_custom_call" | custom-call | bytes 2621440 | tf_op jit(solution)/shard_map/flip/pallas_call | solution.py:156
  19.7 0.9 %collective-permute-done.2.b_ref = bf16[16,1024]{1,0:T(8,128)(2,1)S(1)} collective-permute-done((bf16[16,1024]{1,0:T(8,128)(2,1)S(1)}, bf16[16,1024]{1,0:T(8,128)(2,1)S(1)}, u32[]{:S(2)}, u32[]{:S(2)}) %collective-permute-start.2) | collective-permute-done | bytes 32800 | tf_op jit(solution)/shard_map/ppermute | solution.py:277
  20.6 0.5 %collective-permute-start.3 = (bf16[32,1024]{1,0:T(8,128)(2,1)S(1)}, bf16[32,1024]{1,0:T(8,128)(2,1)S(1)}, u32[]{:S(2)}, u32[]{:S(2)}) collective-permute-start(bf16[32,1024]{1,0:T(8,128)(2,1)S(1)} %join.5.qa_ref), channel_id=1, source_target_pairs={{0,1},{1,0},{2,3},{3,2},{4,5},{5,4},{6,7},{7,6},{8,9},{9,8},{10,11... | collective-permute-start | bytes 196616 | tf_op jit(solution)/shard_map/ppermute | solution.py:277
  21.1 0.9 %collective-permute-done.3.qb_ref = bf16[32,1024]{1,0:T(8,128)(2,1)S(1)} collective-permute-done((bf16[32,1024]{1,0:T(8,128)(2,1)S(1)}, bf16[32,1024]{1,0:T(8,128)(2,1)S(1)}, u32[]{:S(2)}, u32[]{:S(2)}) %collective-permute-start.3) | collective-permute-done | bytes 65568 | tf_op jit(solution)/shard_map/ppermute | solution.py:277
  22.0 3.7 %score.1 = (bf16[64,1024]{1,0:T(8,128)(2,1)S(1)}, f32[32,1024]{1,0:T(8,128)S(1)}, f32[32,1024]{1,0:T(8,128)S(1)}, bf16[64,4096]{1,0:T(8,128)(2,1)S(1)}, f32[4096,1024]{1,0:T(8,128)}) custom-call(bf16[32,1024]{1,0:T(8,128)(2,1)S(1)} %join.5.qa_ref, bf16[32,1024]{1,0:T(8,128)(2,1)S(1)} %collective-permute-done.3.qb_ref, ...), custom_call_target="tpu_custom_call" | custom-call | flops 1073741824 | bytes 8388608 | tf_op jit(solution)/shard_map/score/pallas_call | solution.py:225
  25.7 0.4 %collective-permute-start.4 = (f32[32,1024]{1,0:T(8,128)S(1)}, f32[32,1024]{1,0:T(8,128)S(1)}, u32[]{:S(2)}, u32[]{:S(2)}) collective-permute-start(f32[32,1024]{1,0:T(8,128)S(1)} %get-tuple-element.30), channel_id=1, source_target_pairs={{0,1},{1,0},{2,3},{3,2},{4,5},{5,4},{6,7},{7,6},{8,9},{9,8},{10,11... | collective-permute-start | bytes 393224 | tf_op jit(solution)/shard_map/ppermute | solution.py:277
  26.1 1.0 %collective-permute-done.4 = f32[32,1024]{1,0:T(8,128)S(1)} collective-permute-done((f32[32,1024]{1,0:T(8,128)S(1)}, f32[32,1024]{1,0:T(8,128)S(1)}, u32[]{:S(2)}, u32[]{:S(2)}) %collective-permute-start.4) | collective-permute-done | bytes 131104 | tf_op jit(solution)/shard_map/ppermute | solution.py:277
  27.2 1.7 %collective-permute-start.5 = (f32[16,1024]{1,0:T(8,128)S(1)}, f32[16,1024]{1,0:T(8,128)S(1)}, u32[]{:S(2)}, u32[]{:S(2)}) collective-permute-start(f32[16,1024]{1,0:T(8,128)S(1)} %slice.25), channel_id=1, source_target_pairs={{0,3},{1,2},{2,1},{3,0},{4,7},{5,6},{6,5},{7,4},{8,11},{9,10},{10,... | collective-permute-start | bytes 196616 | tf_op jit(solution)/shard_map/ppermute | solution.py:277
  28.9 2.7 %outer.3._ = f32[4096,1024]{1,0:T(8,128)} custom-call(bf16[64,4096]{1,0:T(8,128)(2,1)S(1)} %get-tuple-element.31.dlogit_ref, bf16[64,1024]{1,0:T(8,128)(2,1)S(1)} %get-tuple-element.32.q_ref, f32[4096,1024]{1,0:T(8,128)} %get-tuple-element.33._), custom_call_target="tpu_custom_call", output_to_operand_aliasing={{}: (2, {})} | custom-call | flops 167772160 | bytes 5242880 | tf_op jit(solution)/shard_map/outer/pallas_call | solution.py:253
  31.6 1.6 %collective-permute-start.6 = (f32[8,1024]{1,0:T(8,128)S(1)}, f32[8,1024]{1,0:T(8,128)S(1)}, u32[]{:S(2)}, u32[]{:S(2)}) collective-permute-start(f32[8,1024]{1,0:T(8,128)S(1)} %slice.27), channel_id=1, source_target_pairs={{0,5},{1,4},{2,7},{3,6},{4,1},{5,0},{6,3},{7,2},{8,13},{9,12},{10,... | collective-permute-start | bytes 98312 | tf_op jit(solution)/shard_map/ppermute | solution.py:277
  33.2 2.1 %outer.4._ = f32[4096,1024]{1,0:T(8,128)} custom-call(bf16[64,4096]{1,0:T(8,128)(2,1)S(1)} %get-tuple-element.31.dlogit_ref, bf16[64,1024]{1,0:T(8,128)(2,1)S(1)} %get-tuple-element.32.q_ref, f32[4096,1024]{1,0:T(8,128)} %outer.3._), custom_call_target="tpu_custom_call", output_to_operand_aliasing={{}: (2, {})} | custom-call | flops 117440512 | bytes 3670016 | tf_op jit(solution)/shard_map/outer/pallas_call | solution.py:253
  35.4 2.6 %collective-permute-start.7 = (f32[4,1024]{1,0:T(4,128)S(1)}, f32[4,1024]{1,0:T(4,128)S(1)}, u32[]{:S(2)}, u32[]{:S(2)}) collective-permute-start(f32[4,1024]{1,0:T(4,128)S(1)} %slice.29), channel_id=1, source_target_pairs={{0,9},{1,8},{2,11},{3,10},{4,13},{5,12},{6,15},{7,14},{8,1},{9,0},... | collective-permute-start | bytes 49160 | tf_op jit(solution)/shard_map/ppermute | solution.py:277
  38.0 2.1 %outer.5 = f32[4096,1024]{1,0:T(8,128)} custom-call(bf16[64,4096]{1,0:T(8,128)(2,1)S(1)} %get-tuple-element.31.dlogit_ref, bf16[64,1024]{1,0:T(8,128)(2,1)S(1)} %get-tuple-element.32.q_ref, f32[4096,1024]{1,0:T(8,128)} %outer.4._), custom_call_target="tpu_custom_call", output_to_operand_aliasing={{}: (2, {})} | custom-call | flops 117440512 | bytes 3670016 | tf_op jit(solution)/shard_map/outer/pallas_call | solution.py:253
  40.2 0.0 collective-permute-done.7
  40.2 0.6 %slice_add_fusion.2 = f32[4,1024]{1,0:T(4,128)} fusion(f32[4,1024]{1,0:T(4,128)S(1)} %collective-permute-done.7, f32[8,1024]{1,0:T(8,128)S(1)} %slice_add_fusion.1), kind=kLoop, calls=%fused_computation.2 | loop fusion | flops 4096 | bytes 49152 | tf_op jit(solution)/shard_map/add | solution.py:302
  (15 shorter events, 0.1 us)
Async XLA Ops:
  0.6 11.9 %slice-start = ((s8[8388608]{0:T(1024)(128)(4,1)}), s8[4194304]{0:T(1024)(128)(4,1)S(1)}, s32[]{:S(2)}) async-start(s8[8388608]{0:T(1024)(128)(4,1)} %bitcast.2), calls=%async_computation | async-start | bytes 8388608
  0.6 11.9 %slice-start.1 = ((s8[8388608]{0:T(1024)(128)(4,1)}), s8[4194304]{0:T(1024)(128)(4,1)S(1)}, s32[]{:S(2)}) async-start(s8[8388608]{0:T(1024)(128)(4,1)} %bitcast.2), calls=%async_computation.1 | async-start | bytes 8388608
  9.0 4.9 %collective-permute-start = (bf16[4,1024]{1,0:T(4,128)(2,1)S(1)}, bf16[4,1024]{1,0:T(4,128)(2,1)S(1)}, u32[]{:S(2)}, u32[]{:S(2)}) collective-permute-start(bf16[4,1024]{1,0:T(4,128)(2,1)S(1)} %get-tuple-element.21._.a_ref), channel_id=1, source_target_pairs={{0,9},{1,8},{2,11},{3,10},{4,13},{5,12},{6,15},{7,14},{8,1},{9,0},... | collective-permute-start | bytes 24584 | tf_op jit(solution)/shard_map/ppermute | solution.py:277
  13.9 3.3 %collective-permute-start.1 = (bf16[8,1024]{1,0:T(8,128)(2,1)S(1)}, bf16[8,1024]{1,0:T(8,128)(2,1)S(1)}, u32[]{:S(2)}, u32[]{:S(2)}) collective-permute-start(bf16[8,1024]{1,0:T(8,128)(2,1)S(1)} %join.3._.a_ref), channel_id=1, source_target_pairs={{0,5},{1,4},{2,7},{3,6},{4,1},{5,0},{6,3},{7,2},{8,13},{9,12},{10,... | collective-permute-start | bytes 49160 | tf_op jit(solution)/shard_map/ppermute | solution.py:277
  17.3 3.3 %collective-permute-start.2 = (bf16[16,1024]{1,0:T(8,128)(2,1)S(1)}, bf16[16,1024]{1,0:T(8,128)(2,1)S(1)}, u32[]{:S(2)}, u32[]{:S(2)}) collective-permute-start(bf16[16,1024]{1,0:T(8,128)(2,1)S(1)} %join.4._.a_ref), channel_id=1, source_target_pairs={{0,3},{1,2},{2,1},{3,0},{4,7},{5,6},{6,5},{7,4},{8,11},{9,10},{10,... | collective-permute-start | bytes 98312 | tf_op jit(solution)/shard_map/ppermute | solution.py:277
  20.6 1.4 %collective-permute-start.3 = (bf16[32,1024]{1,0:T(8,128)(2,1)S(1)}, bf16[32,1024]{1,0:T(8,128)(2,1)S(1)}, u32[]{:S(2)}, u32[]{:S(2)}) collective-permute-start(bf16[32,1024]{1,0:T(8,128)(2,1)S(1)} %join.5.qa_ref), channel_id=1, source_target_pairs={{0,1},{1,0},{2,3},{3,2},{4,5},{5,4},{6,7},{7,6},{8,9},{9,8},{10,11... | collective-permute-start | bytes 196616 | tf_op jit(solution)/shard_map/ppermute | solution.py:277
  25.7 1.4 %collective-permute-start.4 = (f32[32,1024]{1,0:T(8,128)S(1)}, f32[32,1024]{1,0:T(8,128)S(1)}, u32[]{:S(2)}, u32[]{:S(2)}) collective-permute-start(f32[32,1024]{1,0:T(8,128)S(1)} %get-tuple-element.30), channel_id=1, source_target_pairs={{0,1},{1,0},{2,3},{3,2},{4,5},{5,4},{6,7},{7,6},{8,9},{9,8},{10,11... | collective-permute-start | bytes 393224 | tf_op jit(solution)/shard_map/ppermute | solution.py:277
  27.2 4.4 %collective-permute-start.5 = (f32[16,1024]{1,0:T(8,128)S(1)}, f32[16,1024]{1,0:T(8,128)S(1)}, u32[]{:S(2)}, u32[]{:S(2)}) collective-permute-start(f32[16,1024]{1,0:T(8,128)S(1)} %slice.25), channel_id=1, source_target_pairs={{0,3},{1,2},{2,1},{3,0},{4,7},{5,6},{6,5},{7,4},{8,11},{9,10},{10,... | collective-permute-start | bytes 196616 | tf_op jit(solution)/shard_map/ppermute | solution.py:277
  31.6 3.8 %collective-permute-start.6 = (f32[8,1024]{1,0:T(8,128)S(1)}, f32[8,1024]{1,0:T(8,128)S(1)}, u32[]{:S(2)}, u32[]{:S(2)}) collective-permute-start(f32[8,1024]{1,0:T(8,128)S(1)} %slice.27), channel_id=1, source_target_pairs={{0,5},{1,4},{2,7},{3,6},{4,1},{5,0},{6,3},{7,2},{8,13},{9,12},{10,... | collective-permute-start | bytes 98312 | tf_op jit(solution)/shard_map/ppermute | solution.py:277
  35.4 4.8 %collective-permute-start.7 = (f32[4,1024]{1,0:T(4,128)S(1)}, f32[4,1024]{1,0:T(4,128)S(1)}, u32[]{:S(2)}, u32[]{:S(2)}) collective-permute-start(f32[4,1024]{1,0:T(4,128)S(1)} %slice.29), channel_id=1, source_target_pairs={{0,9},{1,8},{2,11},{3,10},{4,13},{5,12},{6,15},{7,14},{8,1},{9,0},... | collective-permute-start | bytes 49160 | tf_op jit(solution)/shard_map/ppermute | solution.py:277
